TPU v7x, 32 devices: a whole 2x2x4 slice. The times are simulated.
32 devices in a mesh: users: 16 (over z, x, core), period: 2 (over y).
Axes of the slice: x: 2, y: 2, z: 4, core: 2. Of those that a mesh axis runs over, the one named last changes fastest.
Arguments:
- ratings: float32 [2, 6, 6144, 768], P('period', None, 'users'), may hold values from -6 to 6
- observed: bfloat16 [2, 6, 6144, 768], P('period', None, 'users'), may hold values from 0 to 2, as said below
- user_factors: float32 [6144, 256], P('users'), may hold values from -0.625 to 0.625
- item_factors: float32 [2, 12288, 256], P('period', 'users'), may hold values from -0.625 to 0.625
Outputs:
- user_out: float32 [6144, 256], P('users')
- item_out: float32 [2, 12288, 256], P('period', 'users')
Inputs may be any that keep to these rules, and one draw needn't show every extreme that they name: `observed`: an entry is either 0 (unobserved) or a weight of 0.5 or more.
All inputs are finite; a program needn't handle non-finite values.
Results may differ from a plain program's by a relative error of at most 0.0003.
Values sent between devices are 32-bit elements; how exact they have to be, the bound alone decides.
No kernel may reach another device: no remote copies, remote signals or barrier semaphores. Data moves between devices by JAX's collectives and lax.ppermute only.
A program may use at most 64 MiB of HBM per device.

v0:
```python
import jax
import jax.numpy as jnp
from jax import lax
from jax.sharding import PartitionSpec as P

OUTER = 2
STRATA = 3


step_rate = 0.002


def from_behind(array, axis, by):
    peers = lax.axis_size(axis)
    return lax.ppermute(array, axis, [(i, (i + by) % peers) for i in range(peers)])


def update(current, factors_v, tile_rows, weights):
    highest = lax.Precision.HIGHEST
    predicted = lax.dot_general(
        current,
        factors_v,
        (((1,), (1,)), ((), ())),
        precision=highest,
        preferred_element_type=jnp.float32,
    )
    residual = weights * (tile_rows - predicted)
    new_u = current + step_rate * jnp.dot(
        residual, factors_v, precision=highest, preferred_element_type=jnp.float32
    )
    new_v = factors_v + step_rate * lax.dot_general(
        residual,
        current,
        (((0,), (0,)), ((), ())),
        precision=highest,
        preferred_element_type=jnp.float32,
    )
    return (new_u, new_v)


def rotate(factors_v):
    return from_behind(factors_v, "users", -1)


def combine(anchor, current):
    change = current - anchor
    periods_count = lax.axis_size("period")
    share_rows = anchor.shape[0] // periods_count
    summed = lax.psum_scatter(change, "period", scatter_dimension=0, tiled=True)
    anchor_share = lax.dynamic_slice_in_dim(
        anchor, lax.axis_index("period") * share_rows, share_rows, 0
    )
    return lax.all_gather(anchor_share + summed / periods_count, "period", axis=0, tiled=True)


def on_device(ratings, observed, user_factors, item_factors):
    factors_u = user_factors
    factors_v = item_factors[0]
    for outer_step in range(OUTER):
        anchor = factors_u
        current = factors_u
        for within in range(STRATA):
            stratum = outer_step * STRATA + within
            if within > 0:
                factors_v = rotate(factors_v)
            weights = observed[0, stratum].astype(jnp.float32)
            current, factors_v = update(current, factors_v, ratings[0, stratum], weights)
        if outer_step + 1 == OUTER:
            factors_u = combine(anchor, current)
        else:
            factors_u = combine(anchor, current)
            factors_v = rotate(factors_v)
    factors_v = from_behind(factors_v, "users", OUTER * STRATA - 1)
    return (factors_u, factors_v[None])


def solution(mesh):
    in_specs = (
        P("period", None, "users", None),
        P("period", None, "users", None),
        P("users", None),
        P("period", "users", None),
    )
    out_specs = (P("users", None), P("period", "users", None))
    return jax.shard_map(
        on_device, mesh=mesh, in_specs=in_specs, out_specs=out_specs, check_vma=False
    )
```

profile of v0, /device:TPU:0, one launch (start us, length us, event | category | flops | bytes accessed | tf_op | source)
XLA Modules:
  0.0 152.7 jit_solution(2961139230301178274)
XLA Ops:
  7.2 3.0 %fusion.5 = f32[384,768]{1,0:T(8,128)S(1)} fusion(f32[384,256]{1,0:T(8,128)} %param.6, f32[1,6,384,768]{3,2,1,0:T(8,128)} %param.4, f32[1,768,256]{2,1,0:T(8,128)} %param.7, bf16[1,6,384,768]{3,2,1,0:T(8,128)(2,1)} %param.5), kind=kOutput, calls=%fused_computation.11 | convolution fusion | flops 906854400 | bytes 4128768 | tf_op jit(solution)/shard_map/dot_general | solution.py:20
  10.3 2.0 %fusion.11 = f32[768,256]{1,0:T(8,128)S(1)} fusion(f32[384,768]{1,0:T(8,128)S(1)} %fusion.5, f32[384,256]{1,0:T(8,128)S(1)} %copy-done, f32[1,768,256]{2,1,0:T(8,128)S(1)} %copy-done.1), kind=kOutput, calls=%fused_computation.23 | convolution fusion | flops 906362880 | bytes 3145728 | tf_op jit(solution)/shard_map/dot_general | solution.py:31
  12.3 5.5 %collective-permute-start = (f32[768,256]{1,0:T(8,128)S(1)}, f32[768,256]{1,0:T(8,128)S(1)}, u32[]{:S(2)}, u32[]{:S(2)}) collective-permute-start(f32[768,256]{1,0:T(8,128)S(1)} %fusion.11), channel_id=1, source_target_pairs={{0,30},{2,0},{4,2},{6,4},{8,6},{10,8},{12,10},{14,12},{16,14},{18,... | collective-permute-start | bytes 2359304 | tf_op jit(solution)/shard_map/ppermute | solution.py:15
  17.8 1.1 fusion.17
  18.9 8.4 %collective-permute-done = f32[768,256]{1,0:T(8,128)S(1)} collective-permute-done((f32[768,256]{1,0:T(8,128)S(1)}, f32[768,256]{1,0:T(8,128)S(1)}, u32[]{:S(2)}, u32[]{:S(2)}) %collective-permute-start) | collective-permute-done | bytes 786464 | tf_op jit(solution)/shard_map/ppermute | solution.py:15
  27.3 2.6 %fusion.4 = f32[384,768]{1,0:T(8,128)S(1)} fusion(f32[384,256]{1,0:T(8,128)S(1)} %fusion.17, f32[768,256]{1,0:T(8,128)S(1)} %collective-permute-done, f32[1,6,384,768]{3,2,1,0:T(8,128)} %param.4, bf16[1,6,384,768]{3,2,1,0:T(8,128)(2,1)} %param.5), kind=kOutput, calls=%fused_computation.9 | convolution fusion | flops 906854400 | bytes 4128768 | tf_op jit(solution)/shard_map/dot_general | solution.py:20
  29.9 2.0 %fusion.10 = f32[768,256]{1,0:T(8,128)S(1)} fusion(f32[768,256]{1,0:T(8,128)S(1)} %collective-permute-done, f32[384,768]{1,0:T(8,128)S(1)} %fusion.4, f32[384,256]{1,0:T(8,128)S(1)} %fusion.17), kind=kOutput, calls=%fused_computation.21 | convolution fusion | flops 906362880 | bytes 3145728 | tf_op jit(solution)/shard_map/dot_general | solution.py:31
  31.9 4.7 %collective-permute-start.1 = (f32[768,256]{1,0:T(8,128)S(1)}, f32[768,256]{1,0:T(8,128)S(1)}, u32[]{:S(2)}, u32[]{:S(2)}) collective-permute-start(f32[768,256]{1,0:T(8,128)S(1)} %fusion.10), channel_id=1, source_target_pairs={{0,30},{2,0},{4,2},{6,4},{8,6},{10,8},{12,10},{14,12},{16,14},{18,... | collective-permute-start | bytes 2359304 | tf_op jit(solution)/shard_map/ppermute | solution.py:15
  36.6 1.1 fusion.16
  37.7 8.4 %collective-permute-done.1 = f32[768,256]{1,0:T(8,128)S(1)} collective-permute-done((f32[768,256]{1,0:T(8,128)S(1)}, f32[768,256]{1,0:T(8,128)S(1)}, u32[]{:S(2)}, u32[]{:S(2)}) %collective-permute-start.1) | collective-permute-done | bytes 786464 | tf_op jit(solution)/shard_map/ppermute | solution.py:15
  46.1 2.6 %fusion.3 = f32[384,768]{1,0:T(8,128)S(1)} fusion(f32[384,256]{1,0:T(8,128)S(1)} %fusion.16, f32[768,256]{1,0:T(8,128)S(1)} %collective-permute-done.1, f32[1,6,384,768]{3,2,1,0:T(8,128)} %param.4, bf16[1,6,384,768]{3,2,1,0:T(8,128)(2,1)} %param.5), kind=kOutput, calls=%fused_computation.7 | convolution fusion | flops 906854400 | bytes 4128768 | tf_op jit(solution)/shard_map/dot_general | solution.py:20
  48.7 1.9 %fusion.18 = f32[384,256]{1,0:T(8,128)} fusion(f32[384,256]{1,0:T(8,128)S(1)} %copy-done, f32[384,256]{1,0:T(8,128)S(1)} %fusion.16, f32[384,768]{1,0:T(8,128)S(1)} %fusion.3, f32[768,256]{1,0:T(8,128)S(1)} %collective-permute-done.1), kind=kOutput, calls=%fused_computation.36 | convolution fusion | flops 906264576 | bytes 3145728 | tf_op jit(solution)/shard_map/dot_general | solution.py:28
  50.8 2.0 %fusion.9 = f32[768,256]{1,0:T(8,128)S(1)} fusion(f32[768,256]{1,0:T(8,128)S(1)} %collective-permute-done.1, f32[384,768]{1,0:T(8,128)S(1)} %fusion.3, f32[384,256]{1,0:T(8,128)S(1)} %fusion.16), kind=kOutput, calls=%fused_computation.19 | convolution fusion | flops 906362880 | bytes 3145728 | tf_op jit(solution)/shard_map/dot_general | solution.py:31
  52.8 4.7 %collective-permute-start.2 = (f32[768,256]{1,0:T(8,128)S(1)}, f32[768,256]{1,0:T(8,128)S(1)}, u32[]{:S(2)}, u32[]{:S(2)}) collective-permute-start(f32[768,256]{1,0:T(8,128)S(1)} %fusion.9), channel_id=1, source_target_pairs={{0,30},{2,0},{4,2},{6,4},{8,6},{10,8},{12,10},{14,12},{16,14},{18,... | collective-permute-start | bytes 2359304 | tf_op jit(solution)/shard_map/ppermute | solution.py:15
  57.5 7.8 %reduce-scatter.3.cloned.1.call-done = f32[192,256]{1,0:T(8,128)} async-done(((f32[384,256]{1,0:T(8,128)}), f32[192,256]{1,0:T(8,128)}) %reduce-scatter.3.cloned.1.call-update) | async-done | bytes 196624 | tf_op jit(solution)/shard_map/reduce_scatter | solution.py:49
  66.2 7.1 %all_gather.6 = f32[384,256]{1,0:T(8,128)S(1)} all-gather(f32[192,256]{1,0:T(8,128)S(1)} %multiply_add_fusion.1), channel_id=1, replica_groups=mesh['users'=16,'period'=2] {'period'}, dimensions={0}, use_global_device_ids=true | all-gather | bytes 589824 | tf_op jit(solution)/shard_map/all_gather | solution.py:53
  73.4 2.6 %fusion.2 = f32[384,768]{1,0:T(8,128)S(1)} fusion(f32[384,256]{1,0:T(8,128)S(1)} %all_gather.6, f32[768,256]{1,0:T(8,128)S(1)} %collective-permute-done.2, f32[1,6,384,768]{3,2,1,0:T(8,128)} %param.4, bf16[1,6,384,768]{3,2,1,0:T(8,128)(2,1)} %param.5), kind=kOutput, calls=%fused_computation.5 | convolution fusion | flops 906854400 | bytes 4128768 | tf_op jit(solution)/shard_map/dot_general | solution.py:20
  76.0 2.0 %fusion.8 = f32[768,256]{1,0:T(8,128)S(1)} fusion(f32[768,256]{1,0:T(8,128)S(1)} %collective-permute-done.2, f32[384,768]{1,0:T(8,128)S(1)} %fusion.2, f32[384,256]{1,0:T(8,128)S(1)} %all_gather.6), kind=kOutput, calls=%fused_computation.17 | convolution fusion | flops 906362880 | bytes 3145728 | tf_op jit(solution)/shard_map/dot_general | solution.py:31
  78.0 2.7 %collective-permute-start.3 = (f32[768,256]{1,0:T(8,128)S(1)}, f32[768,256]{1,0:T(8,128)S(1)}, u32[]{:S(2)}, u32[]{:S(2)}) collective-permute-start(f32[768,256]{1,0:T(8,128)S(1)} %fusion.8), channel_id=1, source_target_pairs={{0,30},{2,0},{4,2},{6,4},{8,6},{10,8},{12,10},{14,12},{16,14},{18,... | collective-permute-start | bytes 2359304 | tf_op jit(solution)/shard_map/ppermute | solution.py:15
  80.7 1.1 fusion.14
  81.8 8.4 %collective-permute-done.3 = f32[768,256]{1,0:T(8,128)S(1)} collective-permute-done((f32[768,256]{1,0:T(8,128)S(1)}, f32[768,256]{1,0:T(8,128)S(1)}, u32[]{:S(2)}, u32[]{:S(2)}) %collective-permute-start.3) | collective-permute-done | bytes 786464 | tf_op jit(solution)/shard_map/ppermute | solution.py:15
  90.2 2.6 %fusion.1 = f32[384,768]{1,0:T(8,128)S(1)} fusion(f32[384,256]{1,0:T(8,128)S(1)} %fusion.14, f32[768,256]{1,0:T(8,128)S(1)} %collective-permute-done.3, f32[1,6,384,768]{3,2,1,0:T(8,128)} %param.4, bf16[1,6,384,768]{3,2,1,0:T(8,128)(2,1)} %param.5), kind=kOutput, calls=%fused_computation.3 | convolution fusion | flops 906854400 | bytes 4128768 | tf_op jit(solution)/shard_map/dot_general | solution.py:20
  92.8 2.0 %fusion.7 = f32[768,256]{1,0:T(8,128)S(1)} fusion(f32[768,256]{1,0:T(8,128)S(1)} %collective-permute-done.3, f32[384,768]{1,0:T(8,128)S(1)} %fusion.1, f32[384,256]{1,0:T(8,128)S(1)} %fusion.14), kind=kOutput, calls=%fused_computation.15 | convolution fusion | flops 906362880 | bytes 3145728 | tf_op jit(solution)/shard_map/dot_general | solution.py:31
  94.8 4.9 %collective-permute-start.4 = (f32[768,256]{1,0:T(8,128)S(1)}, f32[768,256]{1,0:T(8,128)S(1)}, u32[]{:S(2)}, u32[]{:S(2)}) collective-permute-start(f32[768,256]{1,0:T(8,128)S(1)} %fusion.7), channel_id=1, source_target_pairs={{0,30},{2,0},{4,2},{6,4},{8,6},{10,8},{12,10},{14,12},{16,14},{18,... | collective-permute-start | bytes 2359304 | tf_op jit(solution)/shard_map/ppermute | solution.py:15
  99.7 1.1 fusion.13
  100.8 8.4 %collective-permute-done.4 = f32[768,256]{1,0:T(8,128)S(1)} collective-permute-done((f32[768,256]{1,0:T(8,128)S(1)}, f32[768,256]{1,0:T(8,128)S(1)}, u32[]{:S(2)}, u32[]{:S(2)}) %collective-permute-start.4) | collective-permute-done | bytes 786464 | tf_op jit(solution)/shard_map/ppermute | solution.py:15
  109.2 2.6 %fusion = f32[384,768]{1,0:T(8,128)S(1)} fusion(f32[384,256]{1,0:T(8,128)S(1)} %fusion.13, f32[768,256]{1,0:T(8,128)S(1)} %collective-permute-done.4, f32[1,6,384,768]{3,2,1,0:T(8,128)} %param.4, bf16[1,6,384,768]{3,2,1,0:T(8,128)(2,1)} %param.5), kind=kOutput, calls=%fused_computation.1 | convolution fusion | flops 906854400 | bytes 4128768 | tf_op jit(solution)/shard_map/dot_general | solution.py:20
  111.8 1.9 %fusion.19 = f32[384,256]{1,0:T(8,128)} fusion(f32[384,256]{1,0:T(8,128)S(1)} %all_gather.6, f32[384,256]{1,0:T(8,128)S(1)} %fusion.13, f32[384,768]{1,0:T(8,128)S(1)} %fusion, f32[768,256]{1,0:T(8,128)S(1)} %collective-permute-done.4), kind=kOutput, calls=%fused_computation.37 | convolution fusion | flops 906264576 | bytes 3145728 | tf_op jit(solution)/shard_map/dot_general | solution.py:28
  113.7 2.0 %fusion.6 = f32[768,256]{1,0:T(8,128)S(1)} fusion(f32[768,256]{1,0:T(8,128)S(1)} %collective-permute-done.4, f32[384,768]{1,0:T(8,128)S(1)} %fusion, f32[384,256]{1,0:T(8,128)S(1)} %fusion.13), kind=kOutput, calls=%fused_computation.13 | convolution fusion | flops 906362880 | bytes 3145728 | tf_op jit(solution)/shard_map/dot_general | solution.py:31
  115.8 11.7 %reduce-scatter.5.cloned.1.call-done = f32[192,256]{1,0:T(8,128)} async-done(((f32[384,256]{1,0:T(8,128)}), f32[192,256]{1,0:T(8,128)}) %reduce-scatter.5.cloned.1.call-update) | async-done | bytes 196624 | tf_op jit(solution)/shard_map/reduce_scatter | solution.py:49
  128.4 7.1 %all_gather.7 = f32[384,256]{1,0:T(8,128)S(1)} all-gather(f32[192,256]{1,0:T(8,128)S(1)} %multiply_add_fusion), channel_id=1, replica_groups=mesh['users'=16,'period'=2] {'period'}, dimensions={0}, use_global_device_ids=true | all-gather | bytes 589824 | tf_op jit(solution)/shard_map/all_gather | solution.py:53
  135.5 8.7 %collective-permute-done.5 = f32[768,256]{1,0:T(8,128)S(1)} collective-permute-done((f32[768,256]{1,0:T(8,128)S(1)}, f32[768,256]{1,0:T(8,128)S(1)}, u32[]{:S(2)}, u32[]{:S(2)}) %collective-permute-start.5) | collective-permute-done | bytes 786464 | tf_op jit(solution)/shard_map/ppermute | solution.py:15
  (14 shorter events, 3.9 us)
Async XLA Ops:
  7.2 3.1 %copy-start = (f32[384,256]{1,0:T(8,128)S(1)}, f32[384,256]{1,0:T(8,128)}, u32[]{:S(2)}) copy-start(f32[384,256]{1,0:T(8,128)} %param.6) | copy-start | bytes 1179652
  7.2 3.1 %copy-start.1 = (f32[1,768,256]{2,1,0:T(8,128)S(1)}, f32[1,768,256]{2,1,0:T(8,128)}, u32[]{:S(2)}) copy-start(f32[1,768,256]{2,1,0:T(8,128)} %param.7) | copy-start | bytes 2359300
  7.2 58.1 %reduce-scatter.3.cloned.1.call-start = ((), (), s32[]{:S(2)}) async-start(), calls=%async_computation.2 | async-start | bytes 589824 | tf_op jit(solution)/shard_map/reduce_scatter | solution.py:49
  12.3 15.0 %collective-permute-start = (f32[768,256]{1,0:T(8,128)S(1)}, f32[768,256]{1,0:T(8,128)S(1)}, u32[]{:S(2)}, u32[]{:S(2)}) collective-permute-start(f32[768,256]{1,0:T(8,128)S(1)} %fusion.11), channel_id=1, source_target_pairs={{0,30},{2,0},{4,2},{6,4},{8,6},{10,8},{12,10},{14,12},{16,14},{18,... | collective-permute-start | bytes 2359304 | tf_op jit(solution)/shard_map/ppermute | solution.py:15
  31.9 14.2 %collective-permute-start.1 = (f32[768,256]{1,0:T(8,128)S(1)}, f32[768,256]{1,0:T(8,128)S(1)}, u32[]{:S(2)}, u32[]{:S(2)}) collective-permute-start(f32[768,256]{1,0:T(8,128)S(1)} %fusion.10), channel_id=1, source_target_pairs={{0,30},{2,0},{4,2},{6,4},{8,6},{10,8},{12,10},{14,12},{16,14},{18,... | collective-permute-start | bytes 2359304 | tf_op jit(solution)/shard_map/ppermute | solution.py:15
  50.6 76.9 %reduce-scatter.5.cloned.1.call-start = ((), (), s32[]{:S(2)}) async-start(), calls=%async_computation.3 | async-start | bytes 589824 | tf_op jit(solution)/shard_map/reduce_scatter | solution.py:49
  52.8 20.5 %collective-permute-start.2 = (f32[768,256]{1,0:T(8,128)S(1)}, f32[768,256]{1,0:T(8,128)S(1)}, u32[]{:S(2)}, u32[]{:S(2)}) collective-permute-start(f32[768,256]{1,0:T(8,128)S(1)} %fusion.9), channel_id=1, source_target_pairs={{0,30},{2,0},{4,2},{6,4},{8,6},{10,8},{12,10},{14,12},{16,14},{18,... | collective-permute-start | bytes 2359304 | tf_op jit(solution)/shard_map/ppermute | solution.py:15
  78.0 12.2 %collective-permute-start.3 = (f32[768,256]{1,0:T(8,128)S(1)}, f32[768,256]{1,0:T(8,128)S(1)}, u32[]{:S(2)}, u32[]{:S(2)}) collective-permute-start(f32[768,256]{1,0:T(8,128)S(1)} %fusion.8), channel_id=1, source_target_pairs={{0,30},{2,0},{4,2},{6,4},{8,6},{10,8},{12,10},{14,12},{16,14},{18,... | collective-permute-start | bytes 2359304 | tf_op jit(solution)/shard_map/ppermute | solution.py:15
  94.8 14.4 %collective-permute-start.4 = (f32[768,256]{1,0:T(8,128)S(1)}, f32[768,256]{1,0:T(8,128)S(1)}, u32[]{:S(2)}, u32[]{:S(2)}) collective-permute-start(f32[768,256]{1,0:T(8,128)S(1)} %fusion.7), channel_id=1, source_target_pairs={{0,30},{2,0},{4,2},{6,4},{8,6},{10,8},{12,10},{14,12},{16,14},{18,... | collective-permute-start | bytes 2359304 | tf_op jit(solution)/shard_map/ppermute | solution.py:15
  115.7 28.5 %collective-permute-start.5 = (f32[768,256]{1,0:T(8,128)S(1)}, f32[768,256]{1,0:T(8,128)S(1)}, u32[]{:S(2)}, u32[]{:S(2)}) collective-permute-start(f32[768,256]{1,0:T(8,128)S(1)} %fusion.6), channel_id=1, source_target_pairs={{0,10},{2,12},{4,14},{6,16},{8,18},{10,20},{12,22},{14,24},{16,26}... | collective-permute-start | bytes 2359304 | tf_op jit(solution)/shard_map/ppermute | solution.py:15
Sparse Core Ops, SparseCore 0:
  50.7 14.5 reduce-scatter.2
  113.8 13.6 reduce-scatter.4
where the time goes:
time: 153 us
  waiting for transfers between devices  61.8 us (40%)
  matrix products  36.2 us (24%)
  starting transfers between devices  22.7 us (15%)
  blocking collectives  14.3 us (9%)
  between operations  14.2 us (9%)
  other arithmetic  1.9 us (1%)
  local copies, waits for them, and re-layouts  1.63 us (1%)
    ppermute x6, waiting for transfers between devices, from_behind(): lax.ppermute(array, axis, [(i, (i + by) % peers) for i in range(peers)])  42.3 us
    ppermute x6, starting transfers between devices, from_behind(): lax.ppermute(array, axis, [(i, (i + by) % peers) for i in range(peers)])  22.4 us
    reduce_scatter x2, waiting for transfers between devices, combine(): summed = lax.psum_scatter(change, 'period', scatter_dimension=0, tiled=True)  19.4 us
    dot_general x6, matrix products, update(): lax.dot_general(current, factors_v, (((1,), (1,)), ((), ())), precision=h...  15.9 us
    all_gather x2, blocking collectives, combine(): lax.all_gather(anchor_share + summed / periods_count, 'period', axis=0, t...  14.3 us
    dot_general x6, matrix products, update(): lax.dot_general(residual, current, (((0,), (0,)), ((), ())), precision=hi...  12.3 us
    dot_general x6, matrix products, update(): jnp.dot(residual, factors_v, precision=highest, preferred_element_type=jn...  8.08 us
  transfers between devices with their start and end apart: 8, of which 7 were waited for; matrix products, arithmetic and copies ran while one was open for 7% of the time, Pallas kernels for 0%

commit v1 on v0

v1 whole, which is shorter than its diff:
```python
import jax
import jax.numpy as jnp
from jax import lax
from jax.sharding import PartitionSpec as P

OUTER = 2
STRATA = 3
PIECES = 3


step_rate = 0.002


def from_behind(array, axis, by):
    peers = lax.axis_size(axis)
    return lax.ppermute(array, axis, [(i, (i + by) % peers) for i in range(peers)])


def dot(lhs, rhs, dims):
    return lax.dot_general(
        lhs, rhs, (dims, ((), ())), precision=lax.Precision.HIGH, preferred_element_type=jnp.float32
    )


def combine(anchor, current):
    change = current - anchor
    periods_count = lax.axis_size("period")
    if periods_count & (periods_count - 1):
        summed = lax.psum(change, "period")
    else:
        summed, reach = change, 1
        while reach < periods_count:
            partners = [(i, i ^ reach) for i in range(periods_count)]
            summed = summed + lax.ppermute(summed, "period", partners)
            reach *= 2
    return anchor + summed / periods_count


def on_device(ratings, observed, user_factors, item_factors):
    factors_u = user_factors
    items = item_factors.shape[1]
    rows = items // PIECES
    pieces = [item_factors[0, i * rows : (i + 1) * rows] for i in range(PIECES)]
    last = OUTER * STRATA - 1
    for outer_step in range(OUTER):
        anchor = factors_u
        current = factors_u
        for within in range(STRATA):
            stratum = outer_step * STRATA + within
            gained = current
            for i in range(PIECES):
                cols = slice(i * rows, (i + 1) * rows)
                held = pieces[i]
                predicted = dot(current, held, ((1,), (1,)))
                weights = observed[0, stratum, :, cols].astype(jnp.float32)
                residual = weights * (ratings[0, stratum, :, cols] - predicted)
                moved = held + step_rate * dot(residual, current, ((0,), (0,)))
                gained = gained + step_rate * dot(residual, held, ((1,), (0,)))
                pieces[i] = from_behind(moved, "users", last if stratum == last else -1)
            current = gained
        factors_u = combine(anchor, current)
    return (factors_u, jnp.concatenate(pieces, axis=0)[None])


def solution(mesh):
    in_specs = (
        P("period", None, "users", None),
        P("period", None, "users", None),
        P("users", None),
        P("period", "users", None),
    )
    out_specs = (P("users", None), P("period", "users", None))
    return jax.shard_map(
        on_device, mesh=mesh, in_specs=in_specs, out_specs=out_specs, check_vma=False
    )
```

time: 153 us -> 108 us (0.71)
  waiting for transfers between devices: 61.8 us -> 42.9 us
  blocking collectives: 14.3 us -> 0 us
  between operations: 14.2 us -> 1.18 us
  starting transfers between devices: 22.7 us -> 32.2 us
  matrix products: 36.2 us -> 29.7 us
  local copies, waits for them, and re-layouts: 1.63 us -> 0.03 us
    reduce_scatter x2 -> x0, waiting for transfers between devices: 19.4 us -> none  [combine(): summed = lax.psum_scatter(change, 'period', scatter_dimension=0, tiled=True)]
    all_gather x2 -> x0, blocking collectives: 14.3 us -> none  [combine(): lax.all_gather(anchor_share + summed / periods_count, 'period', axis=0, t...]
    ppermute x6 -> x18, starting transfers between devices: 22.4 us -> 30.1 us  [from_behind(): lax.ppermute(array, axis, [(i, (i + by) % peers) for i in range(peers)])]
    dot_general x18 -> x54, matrix products: 36.2 us -> 29.7 us  [dot(): lax.dot_general(lhs, rhs, (dims, ((), ())), precision=lax.Precision.HIGH,...]
    ppermute x0 -> x2, waiting for transfers between devices: none -> 5.08 us  [combine(): summed = summed + lax.ppermute(summed, 'period', partners)]
    ppermute x6 -> x18, waiting for transfers between devices: 42.3 us -> 37.8 us  [from_behind(): lax.ppermute(array, axis, [(i, (i + by) % peers) for i in range(peers)])]
    ppermute x0 -> x2, starting transfers between devices: none -> 2.16 us  [combine(): summed = summed + lax.ppermute(summed, 'period', partners)]
    unnamed x6 -> x8, local copies, waits for them, and re-layouts: 1.63 us -> 0.03 us
  transfers between devices with their start and end apart: 8 -> 20, of which waited for: 7 -> 8; matrix products, arithmetic and copies ran while one was open for 7% -> 25% of each run, Pallas kernels for 0% -> 0%
where the time goes in v1:
time: 108 us
  waiting for transfers between devices  42.9 us (40%)
  starting transfers between devices  32.2 us (30%)
  matrix products  29.7 us (28%)
  other arithmetic  1.83 us (2%)
  between operations  1.18 us (1%)
    ppermute x18, waiting for transfers between devices, from_behind(): lax.ppermute(array, axis, [(i, (i + by) % peers) for i in range(peers)])  37.8 us
    ppermute x18, starting transfers between devices, from_behind(): lax.ppermute(array, axis, [(i, (i + by) % peers) for i in range(peers)])  30.1 us
    dot_general x54, matrix products, dot(): lax.dot_general(lhs, rhs, (dims, ((), ())), precision=lax.Precision.HIGH,...  29.7 us
    ppermute x2, waiting for transfers between devices, combine(): summed = summed + lax.ppermute(summed, 'period', partners)  5.08 us
    ppermute x2, starting transfers between devices, combine(): summed = summed + lax.ppermute(summed, 'period', partners)  2.16 us
  transfers between devices with their start and end apart: 20, of which 8 were waited for; matrix products, arithmetic and copies ran while one was open for 25% of the time, Pallas kernels for 0%

profile of v1, /device:TPU:0, one launch (start us, length us, event | category | flops | bytes accessed | tf_op | source)
XLA Modules:
  0.0 107.8 jit_solution(17949566752236931191)
XLA Ops:
  0.7 1.8 %fusion.5 = f32[384,256]{1,0:T(8,128)S(1)} fusion(f32[384,256]{1,0:T(8,128)} %param.6, f32[1,6,384,768]{3,2,1,0:T(8,128)} %param.4, f32[1,768,256]{2,1,0:T(8,128)} %param.7, bf16[1,6,384,768]{3,2,1,0:T(8,128)(2,1)} %param.5), kind=kOutput, calls=%fused_computation.41 | convolution fusion | flops 151289856 | bytes 1638400 | tf_op jit(solution)/shard_map/dot_general | solution.py:20
  2.5 2.3 %fusion.40 = f32[256,256]{1,0:T(8,128)S(1)} fusion(f32[384,256]{1,0:T(8,128)S(1)} %fusion.5, f32[384,256]{1,0:T(8,128)} %param.6, f32[1,768,256]{2,1,0:T(8,128)} %param.7), kind=kOutput, calls=%fused_computation.94 | convolution fusion | flops 151126016 | bytes 1310720 | tf_op jit(solution)/shard_map/dot_general | solution.py:20
  4.8 5.5 %collective-permute-start.2 = (f32[256,256]{1,0:T(8,128)S(1)}, f32[256,256]{1,0:T(8,128)S(1)}, u32[]{:S(2)}, u32[]{:S(2)}) collective-permute-start(f32[256,256]{1,0:T(8,128)S(1)} %fusion.40), channel_id=1, source_target_pairs={{0,30},{2,0},{4,2},{6,4},{8,6},{10,8},{12,10},{14,12},{16,14},{18,... | collective-permute-start | bytes 786440 | tf_op jit(solution)/shard_map/ppermute | solution.py:16
  10.3 1.6 %fusion.4 = f32[384,256]{1,0:T(8,128)S(1)} fusion(f32[384,256]{1,0:T(8,128)} %param.6, f32[1,6,384,768]{3,2,1,0:T(8,128)} %param.4, f32[1,768,256]{2,1,0:T(8,128)} %param.7, bf16[1,6,384,768]{3,2,1,0:T(8,128)(2,1)} %param.5), kind=kOutput, calls=%fused_computation.40 | convolution fusion | flops 151289856 | bytes 1638400 | tf_op jit(solution)/shard_map/dot_general | solution.py:20
  11.9 1.6 %fusion.39 = f32[256,256]{1,0:T(8,128)S(1)} fusion(f32[384,256]{1,0:T(8,128)S(1)} %fusion.4, f32[384,256]{1,0:T(8,128)} %param.6, f32[1,768,256]{2,1,0:T(8,128)} %param.7), kind=kOutput, calls=%fused_computation.93 | convolution fusion | flops 151126016 | bytes 1310720 | tf_op jit(solution)/shard_map/dot_general | solution.py:20
  13.5 0.7 collective-permute-start.1
  14.2 1.6 %fusion = f32[384,256]{1,0:T(8,128)S(1)} fusion(f32[384,256]{1,0:T(8,128)} %param.6, f32[1,6,384,768]{3,2,1,0:T(8,128)} %param.4, f32[1,768,256]{2,1,0:T(8,128)} %param.7, bf16[1,6,384,768]{3,2,1,0:T(8,128)(2,1)} %param.5), kind=kOutput, calls=%fused_computation.36 | convolution fusion | flops 151289856 | bytes 1638400 | tf_op jit(solution)/shard_map/dot_general | solution.py:20
  15.9 1.5 %fusion.38 = f32[256,256]{1,0:T(8,128)S(1)} fusion(f32[384,256]{1,0:T(8,128)S(1)} %fusion, f32[384,256]{1,0:T(8,128)S(1)} %copy-done, f32[1,768,256]{2,1,0:T(8,128)} %param.7), kind=kOutput, calls=%fused_computation.92 | convolution fusion | flops 151126016 | bytes 1310720 | tf_op jit(solution)/shard_map/dot_general | solution.py:20
  18.5 2.8 %collective-permute-done = f32[256,256]{1,0:T(8,128)S(1)} collective-permute-done((f32[256,256]{1,0:T(8,128)S(1)}, f32[256,256]{1,0:T(8,128)S(1)}, u32[]{:S(2)}, u32[]{:S(2)}) %collective-permute-start) | collective-permute-done | bytes 262176 | tf_op jit(solution)/shard_map/ppermute | solution.py:16
  22.2 4.7 %collective-permute-start.3 = (f32[256,256]{1,0:T(8,128)S(1)}, f32[256,256]{1,0:T(8,128)S(1)}, u32[]{:S(2)}, u32[]{:S(2)}) collective-permute-start(f32[256,256]{1,0:T(8,128)S(1)} %fusion.41), channel_id=1, source_target_pairs={{0,30},{2,0},{4,2},{6,4},{8,6},{10,8},{12,10},{14,12},{16,14},{18,... | collective-permute-start | bytes 786440 | tf_op jit(solution)/shard_map/ppermute | solution.py:16
  29.8 6.5 %collective-permute-done.4 = f32[256,256]{1,0:T(8,128)S(1)} collective-permute-done((f32[256,256]{1,0:T(8,128)S(1)}, f32[256,256]{1,0:T(8,128)S(1)}, u32[]{:S(2)}, u32[]{:S(2)}) %collective-permute-start.4) | collective-permute-done | bytes 262176 | tf_op jit(solution)/shard_map/ppermute | solution.py:16
  37.3 4.7 %collective-permute-start.8 = (f32[256,256]{1,0:T(8,128)S(1)}, f32[256,256]{1,0:T(8,128)S(1)}, u32[]{:S(2)}, u32[]{:S(2)}) collective-permute-start(f32[256,256]{1,0:T(8,128)S(1)} %fusion.45), channel_id=1, source_target_pairs={{0,30},{2,0},{4,2},{6,4},{8,6},{10,8},{12,10},{14,12},{16,14},{18,... | collective-permute-start | bytes 786440 | tf_op jit(solution)/shard_map/ppermute | solution.py:16
  43.7 1.6 %collective-permute-start.6 = (f32[384,256]{1,0:T(8,128)S(1)}, f32[384,256]{1,0:T(8,128)S(1)}, u32[]{:S(2)}, u32[]{:S(2)}) collective-permute-start(f32[384,256]{1,0:T(8,128)S(1)} %fusion.16), channel_id=1, source_target_pairs={{0,1},{1,0},{2,3},{3,2},{4,5},{5,4},{6,7},{7,6},{8,9},{9,8},{10,11... | collective-permute-start | bytes 1179656 | tf_op jit(solution)/shard_map/ppermute | solution.py:34
  45.3 0.5 fusion.46
  46.5 5.1 %collective-permute-done.6 = f32[384,256]{1,0:T(8,128)S(1)} collective-permute-done((f32[384,256]{1,0:T(8,128)S(1)}, f32[384,256]{1,0:T(8,128)S(1)}, u32[]{:S(2)}, u32[]{:S(2)}) %collective-permute-start.6) | collective-permute-done | bytes 393248 | tf_op jit(solution)/shard_map/ppermute | solution.py:34
  52.0 0.5 fusion.49
  52.6 3.0 %collective-permute-start.12 = (f32[256,256]{1,0:T(8,128)S(1)}, f32[256,256]{1,0:T(8,128)S(1)}, u32[]{:S(2)}, u32[]{:S(2)}) collective-permute-start(f32[256,256]{1,0:T(8,128)S(1)} %fusion.49), channel_id=1, source_target_pairs={{0,30},{2,0},{4,2},{6,4},{8,6},{10,8},{12,10},{14,12},{16,14},{18,... | collective-permute-start | bytes 786440 | tf_op jit(solution)/shard_map/ppermute | solution.py:16
  55.9 0.5 fusion.48
  56.9 0.5 fusion.47
  57.4 0.7 collective-permute-start.10
  59.2 5.8 %collective-permute-done.10 = f32[256,256]{1,0:T(8,128)S(1)} collective-permute-done((f32[256,256]{1,0:T(8,128)S(1)}, f32[256,256]{1,0:T(8,128)S(1)}, u32[]{:S(2)}, u32[]{:S(2)}) %collective-permute-start.10) | collective-permute-done | bytes 262176 | tf_op jit(solution)/shard_map/ppermute | solution.py:16
  65.9 4.7 %collective-permute-start.13 = (f32[256,256]{1,0:T(8,128)S(1)}, f32[256,256]{1,0:T(8,128)S(1)}, u32[]{:S(2)}, u32[]{:S(2)}) collective-permute-start(f32[256,256]{1,0:T(8,128)S(1)} %fusion.50), channel_id=1, source_target_pairs={{0,30},{2,0},{4,2},{6,4},{8,6},{10,8},{12,10},{14,12},{16,14},{18,... | collective-permute-start | bytes 786440 | tf_op jit(solution)/shard_map/ppermute | solution.py:16
  73.6 6.6 %collective-permute-done.14 = f32[256,256]{1,0:T(8,128)S(1)} collective-permute-done((f32[256,256]{1,0:T(8,128)S(1)}, f32[256,256]{1,0:T(8,128)S(1)}, u32[]{:S(2)}, u32[]{:S(2)}) %collective-permute-start.14) | collective-permute-done | bytes 262176 | tf_op jit(solution)/shard_map/ppermute | solution.py:16
  80.5 0.5 fusion.54
  81.5 0.5 fusion.55
  83.0 5.5 %collective-permute-start.17 = (f32[256,256]{1,0:T(8,128)S(1)}, f32[256,256]{1,0:T(8,128)S(1)}, u32[]{:S(2)}, u32[]{:S(2)}) collective-permute-start(f32[256,256]{1,0:T(8,128)S(1)} %fusion.53), channel_id=1, source_target_pairs={{0,10},{2,12},{4,14},{6,16},{8,18},{10,20},{12,22},{14,24},{16,26}... | collective-permute-start | bytes 786440 | tf_op jit(solution)/shard_map/ppermute | solution.py:16
  89.5 0.6 collective-permute-start.16
  90.1 10.4 %collective-permute-done.18 = f32[256,256]{1,0:T(8,128)S(1)} collective-permute-done((f32[256,256]{1,0:T(8,128)S(1)}, f32[256,256]{1,0:T(8,128)S(1)}, u32[]{:S(2)}, u32[]{:S(2)}) %collective-permute-start.18) | collective-permute-done | bytes 262176 | tf_op jit(solution)/shard_map/ppermute | solution.py:16
  100.5 2.8 %collective-permute-done.19 = f32[256,256]{1,0:T(8,128)S(1)} collective-permute-done((f32[256,256]{1,0:T(8,128)S(1)}, f32[256,256]{1,0:T(8,128)S(1)}, u32[]{:S(2)}, u32[]{:S(2)}) %collective-permute-start.19) | collective-permute-done | bytes 262176 | tf_op jit(solution)/shard_map/ppermute | solution.py:16
  103.3 2.8 %collective-permute-done.17 = f32[256,256]{1,0:T(8,128)S(1)} collective-permute-done((f32[256,256]{1,0:T(8,128)S(1)}, f32[256,256]{1,0:T(8,128)S(1)}, u32[]{:S(2)}, u32[]{:S(2)}) %collective-permute-start.17) | collective-permute-done | bytes 262176 | tf_op jit(solution)/shard_map/ppermute | solution.py:16
  106.1 0.9 maximum_bitcast_fusion
  107.0 0.8 multiply_add_fusion
  (73 shorter events, 17.0 us)
Async XLA Ops:
  0.6 20.7 %copy-start.1 = (f32[1,6,384,768]{3,2,1,0:T(8,128)S(1)}, f32[1,6,384,768]{3,2,1,0:T(8,128)}, u32[]{:S(2)}) copy-start(f32[1,6,384,768]{3,2,1,0:T(8,128)} %param.4) | copy-start | bytes 21233668
  0.6 15.2 %copy-start = (f32[384,256]{1,0:T(8,128)S(1)}, f32[384,256]{1,0:T(8,128)}, u32[]{:S(2)}) copy-start(f32[384,256]{1,0:T(8,128)} %param.6) | copy-start | bytes 1179652
  0.7 16.8 %copy-start.2 = (f32[1,768,256]{2,1,0:T(8,128)S(1)}, f32[1,768,256]{2,1,0:T(8,128)}, u32[]{:S(2)}) copy-start(f32[1,768,256]{2,1,0:T(8,128)} %param.7) | copy-start | bytes 2359300
  0.7 20.6 %copy-start.3 = (bf16[1,6,384,768]{3,2,1,0:T(8,128)(2,1)S(1)}, bf16[1,6,384,768]{3,2,1,0:T(8,128)(2,1)}, u32[]{:S(2)}) copy-start(bf16[1,6,384,768]{3,2,1,0:T(8,128)(2,1)} %param.5) | copy-start | bytes 10616836
  4.8 22.1 %collective-permute-start.2 = (f32[256,256]{1,0:T(8,128)S(1)}, f32[256,256]{1,0:T(8,128)S(1)}, u32[]{:S(2)}, u32[]{:S(2)}) collective-permute-start(f32[256,256]{1,0:T(8,128)S(1)} %fusion.40), channel_id=1, source_target_pairs={{0,30},{2,0},{4,2},{6,4},{8,6},{10,8},{12,10},{14,12},{16,14},{18,... | collective-permute-start | bytes 786440 | tf_op jit(solution)/shard_map/ppermute | solution.py:16
  13.5 14.3 %collective-permute-start.1 = (f32[256,256]{1,0:T(8,128)S(1)}, f32[256,256]{1,0:T(8,128)S(1)}, u32[]{:S(2)}, u32[]{:S(2)}) collective-permute-start(f32[256,256]{1,0:T(8,128)S(1)} %fusion.39), channel_id=1, source_target_pairs={{0,30},{2,0},{4,2},{6,4},{8,6},{10,8},{12,10},{14,12},{16,14},{18,... | collective-permute-start | bytes 786440 | tf_op jit(solution)/shard_map/ppermute | solution.py:16
  17.3 4.0 %collective-permute-start = (f32[256,256]{1,0:T(8,128)S(1)}, f32[256,256]{1,0:T(8,128)S(1)}, u32[]{:S(2)}, u32[]{:S(2)}) collective-permute-start(f32[256,256]{1,0:T(8,128)S(1)} %fusion.38), channel_id=1, source_target_pairs={{0,30},{2,0},{4,2},{6,4},{8,6},{10,8},{12,10},{14,12},{16,14},{18,... | collective-permute-start | bytes 786440 | tf_op jit(solution)/shard_map/ppermute | solution.py:16
  22.2 20.8 %collective-permute-start.3 = (f32[256,256]{1,0:T(8,128)S(1)}, f32[256,256]{1,0:T(8,128)S(1)}, u32[]{:S(2)}, u32[]{:S(2)}) collective-permute-start(f32[256,256]{1,0:T(8,128)S(1)} %fusion.41), channel_id=1, source_target_pairs={{0,30},{2,0},{4,2},{6,4},{8,6},{10,8},{12,10},{14,12},{16,14},{18,... | collective-permute-start | bytes 786440 | tf_op jit(solution)/shard_map/ppermute | solution.py:16
  27.8 14.2 %collective-permute-start.5 = (f32[256,256]{1,0:T(8,128)S(1)}, f32[256,256]{1,0:T(8,128)S(1)}, u32[]{:S(2)}, u32[]{:S(2)}) collective-permute-start(f32[256,256]{1,0:T(8,128)S(1)} %fusion.43), channel_id=1, source_target_pairs={{0,30},{2,0},{4,2},{6,4},{8,6},{10,8},{12,10},{14,12},{16,14},{18,... | collective-permute-start | bytes 786440 | tf_op jit(solution)/shard_map/ppermute | solution.py:16
  28.7 7.6 %collective-permute-start.4 = (f32[256,256]{1,0:T(8,128)S(1)}, f32[256,256]{1,0:T(8,128)S(1)}, u32[]{:S(2)}, u32[]{:S(2)}) collective-permute-start(f32[256,256]{1,0:T(8,128)S(1)} %fusion.42), channel_id=1, source_target_pairs={{0,30},{2,0},{4,2},{6,4},{8,6},{10,8},{12,10},{14,12},{16,14},{18,... | collective-permute-start | bytes 786440 | tf_op jit(solution)/shard_map/ppermute | solution.py:16
  37.3 18.3 %collective-permute-start.8 = (f32[256,256]{1,0:T(8,128)S(1)}, f32[256,256]{1,0:T(8,128)S(1)}, u32[]{:S(2)}, u32[]{:S(2)}) collective-permute-start(f32[256,256]{1,0:T(8,128)S(1)} %fusion.45), channel_id=1, source_target_pairs={{0,30},{2,0},{4,2},{6,4},{8,6},{10,8},{12,10},{14,12},{16,14},{18,... | collective-permute-start | bytes 786440 | tf_op jit(solution)/shard_map/ppermute | solution.py:16
  43.7 7.8 %collective-permute-start.6 = (f32[384,256]{1,0:T(8,128)S(1)}, f32[384,256]{1,0:T(8,128)S(1)}, u32[]{:S(2)}, u32[]{:S(2)}) collective-permute-start(f32[384,256]{1,0:T(8,128)S(1)} %fusion.16), channel_id=1, source_target_pairs={{0,1},{1,0},{2,3},{3,2},{4,5},{5,4},{6,7},{7,6},{8,9},{9,8},{10,11... | collective-permute-start | bytes 1179656 | tf_op jit(solution)/shard_map/ppermute | solution.py:34
  45.8 5.8 %collective-permute-start.9 = (f32[256,256]{1,0:T(8,128)S(1)}, f32[256,256]{1,0:T(8,128)S(1)}, u32[]{:S(2)}, u32[]{:S(2)}) collective-permute-start(f32[256,256]{1,0:T(8,128)S(1)} %fusion.46), channel_id=1, source_target_pairs={{0,30},{2,0},{4,2},{6,4},{8,6},{10,8},{12,10},{14,12},{16,14},{18,... | collective-permute-start | bytes 786440 | tf_op jit(solution)/shard_map/ppermute | solution.py:16
  46.4 10.1 %collective-permute-start.7 = (f32[256,256]{1,0:T(8,128)S(1)}, f32[256,256]{1,0:T(8,128)S(1)}, u32[]{:S(2)}, u32[]{:S(2)}) collective-permute-start(f32[256,256]{1,0:T(8,128)S(1)} %fusion.44), channel_id=1, source_target_pairs={{0,30},{2,0},{4,2},{6,4},{8,6},{10,8},{12,10},{14,12},{16,14},{18,... | collective-permute-start | bytes 786440 | tf_op jit(solution)/shard_map/ppermute | solution.py:16
  52.6 18.0 %collective-permute-start.12 = (f32[256,256]{1,0:T(8,128)S(1)}, f32[256,256]{1,0:T(8,128)S(1)}, u32[]{:S(2)}, u32[]{:S(2)}) collective-permute-start(f32[256,256]{1,0:T(8,128)S(1)} %fusion.49), channel_id=1, source_target_pairs={{0,30},{2,0},{4,2},{6,4},{8,6},{10,8},{12,10},{14,12},{16,14},{18,... | collective-permute-start | bytes 786440 | tf_op jit(solution)/shard_map/ppermute | solution.py:16
  56.4 15.1 %collective-permute-start.11 = (f32[256,256]{1,0:T(8,128)S(1)}, f32[256,256]{1,0:T(8,128)S(1)}, u32[]{:S(2)}, u32[]{:S(2)}) collective-permute-start(f32[256,256]{1,0:T(8,128)S(1)} %fusion.48), channel_id=1, source_target_pairs={{0,30},{2,0},{4,2},{6,4},{8,6},{10,8},{12,10},{14,12},{16,14},{18,... | collective-permute-start | bytes 786440 | tf_op jit(solution)/shard_map/ppermute | solution.py:16
  57.4 7.6 %collective-permute-start.10 = (f32[256,256]{1,0:T(8,128)S(1)}, f32[256,256]{1,0:T(8,128)S(1)}, u32[]{:S(2)}, u32[]{:S(2)}) collective-permute-start(f32[256,256]{1,0:T(8,128)S(1)} %fusion.47), channel_id=1, source_target_pairs={{0,30},{2,0},{4,2},{6,4},{8,6},{10,8},{12,10},{14,12},{16,14},{18,... | collective-permute-start | bytes 786440 | tf_op jit(solution)/shard_map/ppermute | solution.py:16
  65.9 16.2 %collective-permute-start.13 = (f32[256,256]{1,0:T(8,128)S(1)}, f32[256,256]{1,0:T(8,128)S(1)}, u32[]{:S(2)}, u32[]{:S(2)}) collective-permute-start(f32[256,256]{1,0:T(8,128)S(1)} %fusion.50), channel_id=1, source_target_pairs={{0,30},{2,0},{4,2},{6,4},{8,6},{10,8},{12,10},{14,12},{16,14},{18,... | collective-permute-start | bytes 786440 | tf_op jit(solution)/shard_map/ppermute | solution.py:16
  71.5 9.6 %collective-permute-start.15 = (f32[256,256]{1,0:T(8,128)S(1)}, f32[256,256]{1,0:T(8,128)S(1)}, u32[]{:S(2)}, u32[]{:S(2)}) collective-permute-start(f32[256,256]{1,0:T(8,128)S(1)} %fusion.52), channel_id=1, source_target_pairs={{0,30},{2,0},{4,2},{6,4},{8,6},{10,8},{12,10},{14,12},{16,14},{18,... | collective-permute-start | bytes 786440 | tf_op jit(solution)/shard_map/ppermute | solution.py:16
  72.5 7.7 %collective-permute-start.14 = (f32[256,256]{1,0:T(8,128)S(1)}, f32[256,256]{1,0:T(8,128)S(1)}, u32[]{:S(2)}, u32[]{:S(2)}) collective-permute-start(f32[256,256]{1,0:T(8,128)S(1)} %fusion.51), channel_id=1, source_target_pairs={{0,30},{2,0},{4,2},{6,4},{8,6},{10,8},{12,10},{14,12},{16,14},{18,... | collective-permute-start | bytes 786440 | tf_op jit(solution)/shard_map/ppermute | solution.py:16
  81.0 19.4 %collective-permute-start.18 = (f32[256,256]{1,0:T(8,128)S(1)}, f32[256,256]{1,0:T(8,128)S(1)}, u32[]{:S(2)}, u32[]{:S(2)}) collective-permute-start(f32[256,256]{1,0:T(8,128)S(1)} %fusion.54), channel_id=1, source_target_pairs={{0,10},{2,12},{4,14},{6,16},{8,18},{10,20},{12,22},{14,24},{16,26}... | collective-permute-start | bytes 786440 | tf_op jit(solution)/shard_map/ppermute | solution.py:16
  82.0 21.2 %collective-permute-start.19 = (f32[256,256]{1,0:T(8,128)S(1)}, f32[256,256]{1,0:T(8,128)S(1)}, u32[]{:S(2)}, u32[]{:S(2)}) collective-permute-start(f32[256,256]{1,0:T(8,128)S(1)} %fusion.55), channel_id=1, source_target_pairs={{0,10},{2,12},{4,14},{6,16},{8,18},{10,20},{12,22},{14,24},{16,26}... | collective-permute-start | bytes 786440 | tf_op jit(solution)/shard_map/ppermute | solution.py:16
  83.0 23.1 %collective-permute-start.17 = (f32[256,256]{1,0:T(8,128)S(1)}, f32[256,256]{1,0:T(8,128)S(1)}, u32[]{:S(2)}, u32[]{:S(2)}) collective-permute-start(f32[256,256]{1,0:T(8,128)S(1)} %fusion.53), channel_id=1, source_target_pairs={{0,10},{2,12},{4,14},{6,16},{8,18},{10,20},{12,22},{14,24},{16,26}... | collective-permute-start | bytes 786440 | tf_op jit(solution)/shard_map/ppermute | solution.py:16
  89.5 17.5 %collective-permute-start.16 = (f32[384,256]{1,0:T(8,128)S(1)}, f32[384,256]{1,0:T(8,128)S(1)}, u32[]{:S(2)}, u32[]{:S(2)}) collective-permute-start(f32[384,256]{1,0:T(8,128)S(1)} %fusion.35), channel_id=1, source_target_pairs={{0,1},{1,0},{2,3},{3,2},{4,5},{5,4},{6,7},{7,6},{8,9},{9,8},{10,11... | collective-permute-start | bytes 1179656 | tf_op jit(solution)/shard_map/ppermute | solution.py:34

commit v2 on v1

--- a/solution.py
+++ b/solution.py
@@ -3,9 +3,10 @@
 from jax import lax
 from jax.sharding import PartitionSpec as P
 
+
 OUTER = 2
 STRATA = 3
-PIECES = 3
+PIECES = 6
 
 
 step_rate = 0.002
@@ -22,18 +23,18 @@
     )
 
 
-def combine(anchor, current):
-    change = current - anchor
+def combine(current):
     periods_count = lax.axis_size("period")
     if periods_count & (periods_count - 1):
-        summed = lax.psum(change, "period")
+        summed = lax.psum(current, "period")
     else:
-        summed, reach = change, 1
+        summed, reach = current, 1
         while reach < periods_count:
             partners = [(i, i ^ reach) for i in range(periods_count)]
-            summed = summed + lax.ppermute(summed, "period", partners)
+            partner = lax.ppermute(summed, "period", partners)
+            summed = summed + partner
             reach *= 2
-    return anchor + summed / periods_count
+    return summed / periods_count
 
 
 def on_device(ratings, observed, user_factors, item_factors):
@@ -43,7 +44,6 @@
     pieces = [item_factors[0, i * rows : (i + 1) * rows] for i in range(PIECES)]
     last = OUTER * STRATA - 1
     for outer_step in range(OUTER):
-        anchor = factors_u
         current = factors_u
         for within in range(STRATA):
             stratum = outer_step * STRATA + within
@@ -58,7 +58,7 @@
                 gained = gained + step_rate * dot(residual, held, ((1,), (0,)))
                 pieces[i] = from_behind(moved, "users", last if stratum == last else -1)
             current = gained
-        factors_u = combine(anchor, current)
+        factors_u = combine(current)
     return (factors_u, jnp.concatenate(pieces, axis=0)[None])
 
 

time: 108 us -> 128 us (1.19)
  matrix products: 29.7 us -> 47.7 us
  starting transfers between devices: 32.2 us -> 41.3 us
  waiting for transfers between devices: 42.9 us -> 36.4 us
    dot_general x54 -> x108, matrix products: 29.7 us -> 47.7 us  [dot(): lax.dot_general(lhs, rhs, (dims, ((), ())), precision=lax.Precision.HIGH,...]
    ppermute x18 -> x36, waiting for transfers between devices: 37.8 us -> 25.6 us  [from_behind(): lax.ppermute(array, axis, [(i, (i + by) % peers) for i in range(peers)])]
    ppermute x18 -> x36, starting transfers between devices: 30.1 us -> 38.1 us  [from_behind(): lax.ppermute(array, axis, [(i, (i + by) % peers) for i in range(peers)])]
    ppermute x2, waiting for transfers between devices: 5.08 us -> 10.8 us  [combine(): partner = lax.ppermute(summed, 'period', partners)]
  transfers between devices with their start and end apart: 20 -> 38, of which waited for: 8 -> 7; matrix products, arithmetic and copies ran while one was open for 25% -> 34% of each run, Pallas kernels for 0% -> 0%
where the time goes in v2:
time: 128 us
  matrix products  47.7 us (37%)
  starting transfers between devices  41.3 us (32%)
  waiting for transfers between devices  36.4 us (28%)
  between operations  1.79 us (1%)
    dot_general x108, matrix products, dot(): lax.dot_general(lhs, rhs, (dims, ((), ())), precision=lax.Precision.HIGH,...  47.7 us
    ppermute x36, starting transfers between devices, from_behind(): lax.ppermute(array, axis, [(i, (i + by) % peers) for i in range(peers)])  38.1 us
    ppermute x36, waiting for transfers between devices, from_behind(): lax.ppermute(array, axis, [(i, (i + by) % peers) for i in range(peers)])  25.6 us
    ppermute x2, waiting for transfers between devices, combine(): partner = lax.ppermute(summed, 'period', partners)  10.8 us
    ppermute x2, starting transfers between devices, combine(): partner = lax.ppermute(summed, 'period', partners)  3.18 us
  transfers between devices with their start and end apart: 38, of which 7 were waited for; matrix products, arithmetic and copies ran while one was open for 34% of the time, Pallas kernels for 0%

profile of v2, /device:TPU:0, one launch (start us, length us, event | category | flops | bytes accessed | tf_op | source)
XLA Modules:
  0.0 128.2 jit_solution(11059634519195138066)
XLA Ops:
  0.7 1.6 %fusion.66 = f32[384,128]{1,0:T(8,128)S(1)} fusion(f32[384,256]{1,0:T(8,128)} %param.6, f32[1,6,384,768]{3,2,1,0:T(8,128)} %param.4, f32[1,768,256]{2,1,0:T(8,128)} %param.7, bf16[1,6,384,768]{3,2,1,0:T(8,128)(2,1)} %param.5), kind=kOutput, calls=%fused_computation.133 | convolution fusion | flops 75644928 | bytes 1015808 | tf_op jit(solution)/shard_map/dot_general | solution.py:21
  2.3 2.1 %fusion.102 = f32[128,256]{1,0:T(8,128)S(1)} fusion(f32[384,128]{1,0:T(8,128)S(1)} %fusion.66, f32[384,256]{1,0:T(8,128)} %param.6, f32[1,768,256]{2,1,0:T(8,128)} %param.7), kind=kOutput, calls=%fused_computation.205 | convolution fusion | flops 75563008 | bytes 851968 | tf_op jit(solution)/shard_map/dot_general | solution.py:21
  4.4 5.5 %collective-permute-start.5 = (f32[128,256]{1,0:T(8,128)S(1)}, f32[128,256]{1,0:T(8,128)S(1)}, u32[]{:S(2)}, u32[]{:S(2)}) collective-permute-start(f32[128,256]{1,0:T(8,128)S(1)} %fusion.102), channel_id=1, source_target_pairs={{0,30},{2,0},{4,2},{6,4},{8,6},{10,8},{12,10},{14,12},{16,14},{18,... | collective-permute-start | bytes 393224 | tf_op jit(solution)/shard_map/ppermute | solution.py:17
  9.9 1.5 %fusion.67 = f32[384,128]{1,0:T(8,128)S(1)} fusion(f32[384,256]{1,0:T(8,128)} %param.6, f32[1,6,384,768]{3,2,1,0:T(8,128)} %param.4, f32[1,768,256]{2,1,0:T(8,128)} %param.7, bf16[1,6,384,768]{3,2,1,0:T(8,128)(2,1)} %param.5), kind=kOutput, calls=%fused_computation.135 | convolution fusion | flops 75644928 | bytes 1015808 | tf_op jit(solution)/shard_map/dot_general | solution.py:21
  11.4 1.4 %fusion.103 = f32[128,256]{1,0:T(8,128)S(1)} fusion(f32[384,128]{1,0:T(8,128)S(1)} %fusion.67, f32[384,256]{1,0:T(8,128)} %param.6, f32[1,768,256]{2,1,0:T(8,128)} %param.7), kind=kOutput, calls=%fused_computation.207 | convolution fusion | flops 75563008 | bytes 851968 | tf_op jit(solution)/shard_map/dot_general | solution.py:21
  13.5 1.8 %fusion.68 = f32[384,128]{1,0:T(8,128)S(1)} fusion(f32[384,256]{1,0:T(8,128)} %param.6, f32[1,6,384,768]{3,2,1,0:T(8,128)} %param.4, f32[1,768,256]{2,1,0:T(8,128)} %param.7, bf16[1,6,384,768]{3,2,1,0:T(8,128)(2,1)} %param.5), kind=kOutput, calls=%fused_computation.137 | convolution fusion | flops 75644928 | bytes 1015808 | tf_op jit(solution)/shard_map/dot_general | solution.py:21
  15.3 1.4 %fusion.104 = f32[128,256]{1,0:T(8,128)S(1)} fusion(f32[384,128]{1,0:T(8,128)S(1)} %fusion.68, f32[384,256]{1,0:T(8,128)} %param.6, f32[1,768,256]{2,1,0:T(8,128)} %param.7), kind=kOutput, calls=%fused_computation.209 | convolution fusion | flops 75563008 | bytes 851968 | tf_op jit(solution)/shard_map/dot_general | solution.py:21
  16.8 1.5 %fusion.69 = f32[384,128]{1,0:T(8,128)S(1)} fusion(f32[384,256]{1,0:T(8,128)} %param.6, f32[1,6,384,768]{3,2,1,0:T(8,128)} %param.4, f32[1,768,256]{2,1,0:T(8,128)} %param.7, bf16[1,6,384,768]{3,2,1,0:T(8,128)(2,1)} %param.5), kind=kOutput, calls=%fused_computation.139 | convolution fusion | flops 75644928 | bytes 1015808 | tf_op jit(solution)/shard_map/dot_general | solution.py:21
  18.3 1.4 %fusion.105 = f32[128,256]{1,0:T(8,128)S(1)} fusion(f32[384,128]{1,0:T(8,128)S(1)} %fusion.69, f32[384,256]{1,0:T(8,128)} %param.6, f32[1,768,256]{2,1,0:T(8,128)} %param.7), kind=kOutput, calls=%fused_computation.211 | convolution fusion | flops 75563008 | bytes 851968 | tf_op jit(solution)/shard_map/dot_general | solution.py:21
  20.4 1.3 %fusion.70 = f32[384,128]{1,0:T(8,128)S(1)} fusion(f32[384,256]{1,0:T(8,128)S(1)} %copy-done, f32[1,6,384,768]{3,2,1,0:T(8,128)} %param.4, f32[1,768,256]{2,1,0:T(8,128)S(1)} %copy-done.1, bf16[1,6,384,768]{3,2,1,0:T(8,128)(2,1)} %param.5), kind=kOutput, calls=%fused_computation.141 | convolution fusion | flops 75644928 | bytes 1015808 | tf_op jit(solution)/shard_map/dot_general | solution.py:21
  22.8 1.2 fusion.71
  26.3 0.9 collective-permute-start
  32.4 1.8 %collective-permute-start.8 = (f32[128,256]{1,0:T(8,128)S(1)}, f32[128,256]{1,0:T(8,128)S(1)}, u32[]{:S(2)}, u32[]{:S(2)}) collective-permute-start(f32[128,256]{1,0:T(8,128)S(1)} %fusion.99), channel_id=1, source_target_pairs={{0,30},{2,0},{4,2},{6,4},{8,6},{10,8},{12,10},{14,12},{16,14},{18,... | collective-permute-start | bytes 393224 | tf_op jit(solution)/shard_map/ppermute | solution.py:17
  36.7 1.4 %collective-permute-done.6 = f32[128,256]{1,0:T(8,128)S(1)} collective-permute-done((f32[128,256]{1,0:T(8,128)S(1)}, f32[128,256]{1,0:T(8,128)S(1)}, u32[]{:S(2)}, u32[]{:S(2)}) %collective-permute-start.6) | collective-permute-done | bytes 131104 | tf_op jit(solution)/shard_map/ppermute | solution.py:17
  38.1 4.6 %collective-permute-start.7 = (f32[128,256]{1,0:T(8,128)S(1)}, f32[128,256]{1,0:T(8,128)S(1)}, u32[]{:S(2)}, u32[]{:S(2)}) collective-permute-start(f32[128,256]{1,0:T(8,128)S(1)} %fusion.100), channel_id=1, source_target_pairs={{0,30},{2,0},{4,2},{6,4},{8,6},{10,8},{12,10},{14,12},{16,14},{18,... | collective-permute-start | bytes 393224 | tf_op jit(solution)/shard_map/ppermute | solution.py:17
  48.4 1.6 %collective-permute-start.12 = (f32[384,256]{1,0:T(8,128)S(1)}, f32[384,256]{1,0:T(8,128)S(1)}, u32[]{:S(2)}, u32[]{:S(2)}) collective-permute-start(f32[384,256]{1,0:T(8,128)S(1)} %fusion.30), channel_id=1, source_target_pairs={{0,1},{1,0},{2,3},{3,2},{4,5},{5,4},{6,7},{7,6},{8,9},{9,8},{10,11... | collective-permute-start | bytes 1179656 | tf_op jit(solution)/shard_map/ppermute | solution.py:34
  50.7 9.3 %collective-permute-done.12 = f32[384,256]{1,0:T(8,128)S(1)} collective-permute-done((f32[384,256]{1,0:T(8,128)S(1)}, f32[384,256]{1,0:T(8,128)S(1)}, u32[]{:S(2)}, u32[]{:S(2)}) %collective-permute-start.12) | collective-permute-done | bytes 393248 | tf_op jit(solution)/shard_map/ppermute | solution.py:34
  60.0 1.5 %collective-permute-start.15 = (f32[128,256]{1,0:T(8,128)S(1)}, f32[128,256]{1,0:T(8,128)S(1)}, u32[]{:S(2)}, u32[]{:S(2)}) collective-permute-start(f32[128,256]{1,0:T(8,128)S(1)} %fusion.93), channel_id=1, source_target_pairs={{0,30},{2,0},{4,2},{6,4},{8,6},{10,8},{12,10},{14,12},{16,14},{18,... | collective-permute-start | bytes 393224 | tf_op jit(solution)/shard_map/ppermute | solution.py:17
  61.6 0.9 collective-permute-start.14
  65.4 3.2 %collective-permute-start.22 = (f32[128,256]{1,0:T(8,128)S(1)}, f32[128,256]{1,0:T(8,128)S(1)}, u32[]{:S(2)}, u32[]{:S(2)}) collective-permute-start(f32[128,256]{1,0:T(8,128)S(1)} %fusion.86), channel_id=1, source_target_pairs={{0,30},{2,0},{4,2},{6,4},{8,6},{10,8},{12,10},{14,12},{16,14},{18,... | collective-permute-start | bytes 393224 | tf_op jit(solution)/shard_map/ppermute | solution.py:17
  72.2 1.8 %collective-permute-done.19 = f32[128,256]{1,0:T(8,128)S(1)} collective-permute-done((f32[128,256]{1,0:T(8,128)S(1)}, f32[128,256]{1,0:T(8,128)S(1)}, u32[]{:S(2)}, u32[]{:S(2)}) %collective-permute-start.19) | collective-permute-done | bytes 131104 | tf_op jit(solution)/shard_map/ppermute | solution.py:17
  73.9 4.6 %collective-permute-start.20 = (f32[128,256]{1,0:T(8,128)S(1)}, f32[128,256]{1,0:T(8,128)S(1)}, u32[]{:S(2)}, u32[]{:S(2)}) collective-permute-start(f32[128,256]{1,0:T(8,128)S(1)} %fusion.88), channel_id=1, source_target_pairs={{0,30},{2,0},{4,2},{6,4},{8,6},{10,8},{12,10},{14,12},{16,14},{18,... | collective-permute-start | bytes 393224 | tf_op jit(solution)/shard_map/ppermute | solution.py:17
  82.5 3.1 %collective-permute-start.28 = (f32[128,256]{1,0:T(8,128)S(1)}, f32[128,256]{1,0:T(8,128)S(1)}, u32[]{:S(2)}, u32[]{:S(2)}) collective-permute-start(f32[128,256]{1,0:T(8,128)S(1)} %fusion.80), channel_id=1, source_target_pairs={{0,30},{2,0},{4,2},{6,4},{8,6},{10,8},{12,10},{14,12},{16,14},{18,... | collective-permute-start | bytes 393224 | tf_op jit(solution)/shard_map/ppermute | solution.py:17
  88.1 1.4 %collective-permute-done.26 = f32[128,256]{1,0:T(8,128)S(1)} collective-permute-done((f32[128,256]{1,0:T(8,128)S(1)}, f32[128,256]{1,0:T(8,128)S(1)}, u32[]{:S(2)}, u32[]{:S(2)}) %collective-permute-start.26) | collective-permute-done | bytes 131104 | tf_op jit(solution)/shard_map/ppermute | solution.py:17
  89.5 4.6 %collective-permute-start.27 = (f32[128,256]{1,0:T(8,128)S(1)}, f32[128,256]{1,0:T(8,128)S(1)}, u32[]{:S(2)}, u32[]{:S(2)}) collective-permute-start(f32[128,256]{1,0:T(8,128)S(1)} %fusion.81), channel_id=1, source_target_pairs={{0,30},{2,0},{4,2},{6,4},{8,6},{10,8},{12,10},{14,12},{16,14},{18,... | collective-permute-start | bytes 393224 | tf_op jit(solution)/shard_map/ppermute | solution.py:17
  97.0 0.9 collective-permute-start.36
  98.9 1.8 %collective-permute-start.35 = (f32[128,256]{1,0:T(8,128)S(1)}, f32[128,256]{1,0:T(8,128)S(1)}, u32[]{:S(2)}, u32[]{:S(2)}) collective-permute-start(f32[128,256]{1,0:T(8,128)S(1)} %fusion.74), channel_id=1, source_target_pairs={{0,10},{2,12},{4,14},{6,16},{8,18},{10,20},{12,22},{14,24},{16,26}... | collective-permute-start | bytes 393224 | tf_op jit(solution)/shard_map/ppermute | solution.py:17
  103.2 16.3 %collective-permute-done.32 = f32[128,256]{1,0:T(8,128)S(1)} collective-permute-done((f32[128,256]{1,0:T(8,128)S(1)}, f32[128,256]{1,0:T(8,128)S(1)}, u32[]{:S(2)}, u32[]{:S(2)}) %collective-permute-start.32) | collective-permute-done | bytes 131104 | tf_op jit(solution)/shard_map/ppermute | solution.py:17
  119.5 1.6 %collective-permute-start.31 = (f32[384,256]{1,0:T(8,128)S(1)}, f32[384,256]{1,0:T(8,128)S(1)}, u32[]{:S(2)}, u32[]{:S(2)}) collective-permute-start(f32[384,256]{1,0:T(8,128)S(1)} %fusion.15), channel_id=1, source_target_pairs={{0,1},{1,0},{2,3},{3,2},{4,5},{5,4},{6,7},{7,6},{8,9},{9,8},{10,11... | collective-permute-start | bytes 1179656 | tf_op jit(solution)/shard_map/ppermute | solution.py:34
  121.1 4.6 %collective-permute-done.34 = f32[128,256]{1,0:T(8,128)S(1)} collective-permute-done((f32[128,256]{1,0:T(8,128)S(1)}, f32[128,256]{1,0:T(8,128)S(1)}, u32[]{:S(2)}, u32[]{:S(2)}) %collective-permute-start.34) | collective-permute-done | bytes 131104 | tf_op jit(solution)/shard_map/ppermute | solution.py:17
  125.8 1.6 %collective-permute-done.31 = f32[384,256]{1,0:T(8,128)S(1)} collective-permute-done((f32[384,256]{1,0:T(8,128)S(1)}, f32[384,256]{1,0:T(8,128)S(1)}, u32[]{:S(2)}, u32[]{:S(2)}) %collective-permute-start.31) | collective-permute-done | bytes 393248 | tf_op jit(solution)/shard_map/ppermute | solution.py:34
  127.4 0.8 add_multiply_fusion
  (170 shorter events, 37.4 us)
Async XLA Ops:
  4.4 21.8 %collective-permute-start.5 = (f32[128,256]{1,0:T(8,128)S(1)}, f32[128,256]{1,0:T(8,128)S(1)}, u32[]{:S(2)}, u32[]{:S(2)}) collective-permute-start(f32[128,256]{1,0:T(8,128)S(1)} %fusion.102), channel_id=1, source_target_pairs={{0,30},{2,0},{4,2},{6,4},{8,6},{10,8},{12,10},{14,12},{16,14},{18,... | collective-permute-start | bytes 393224 | tf_op jit(solution)/shard_map/ppermute | solution.py:17
  12.8 15.0 %collective-permute-start.4 = (f32[128,256]{1,0:T(8,128)S(1)}, f32[128,256]{1,0:T(8,128)S(1)}, u32[]{:S(2)}, u32[]{:S(2)}) collective-permute-start(f32[128,256]{1,0:T(8,128)S(1)} %fusion.103), channel_id=1, source_target_pairs={{0,30},{2,0},{4,2},{6,4},{8,6},{10,8},{12,10},{14,12},{16,14},{18,... | collective-permute-start | bytes 393224 | tf_op jit(solution)/shard_map/ppermute | solution.py:17
  16.7 12.2 %collective-permute-start.3 = (f32[128,256]{1,0:T(8,128)S(1)}, f32[128,256]{1,0:T(8,128)S(1)}, u32[]{:S(2)}, u32[]{:S(2)}) collective-permute-start(f32[128,256]{1,0:T(8,128)S(1)} %fusion.104), channel_id=1, source_target_pairs={{0,30},{2,0},{4,2},{6,4},{8,6},{10,8},{12,10},{14,12},{16,14},{18,... | collective-permute-start | bytes 393224 | tf_op jit(solution)/shard_map/ppermute | solution.py:17
  19.7 11.0 %collective-permute-start.2 = (f32[128,256]{1,0:T(8,128)S(1)}, f32[128,256]{1,0:T(8,128)S(1)}, u32[]{:S(2)}, u32[]{:S(2)}) collective-permute-start(f32[128,256]{1,0:T(8,128)S(1)} %fusion.105), channel_id=1, source_target_pairs={{0,30},{2,0},{4,2},{6,4},{8,6},{10,8},{12,10},{14,12},{16,14},{18,... | collective-permute-start | bytes 393224 | tf_op jit(solution)/shard_map/ppermute | solution.py:17
  22.1 13.2 %collective-permute-start.1 = (f32[128,256]{1,0:T(8,128)S(1)}, f32[128,256]{1,0:T(8,128)S(1)}, u32[]{:S(2)}, u32[]{:S(2)}) collective-permute-start(f32[128,256]{1,0:T(8,128)S(1)} %fusion.106), channel_id=1, source_target_pairs={{0,30},{2,0},{4,2},{6,4},{8,6},{10,8},{12,10},{14,12},{16,14},{18,... | collective-permute-start | bytes 393224 | tf_op jit(solution)/shard_map/ppermute | solution.py:17
  27.9 15.6 %collective-permute-start.11 = (f32[128,256]{1,0:T(8,128)S(1)}, f32[128,256]{1,0:T(8,128)S(1)}, u32[]{:S(2)}, u32[]{:S(2)}) collective-permute-start(f32[128,256]{1,0:T(8,128)S(1)} %fusion.96), channel_id=1, source_target_pairs={{0,30},{2,0},{4,2},{6,4},{8,6},{10,8},{12,10},{14,12},{16,14},{18,... | collective-permute-start | bytes 393224 | tf_op jit(solution)/shard_map/ppermute | solution.py:17
  29.0 15.5 %collective-permute-start.10 = (f32[128,256]{1,0:T(8,128)S(1)}, f32[128,256]{1,0:T(8,128)S(1)}, u32[]{:S(2)}, u32[]{:S(2)}) collective-permute-start(f32[128,256]{1,0:T(8,128)S(1)} %fusion.97), channel_id=1, source_target_pairs={{0,30},{2,0},{4,2},{6,4},{8,6},{10,8},{12,10},{14,12},{16,14},{18,... | collective-permute-start | bytes 393224 | tf_op jit(solution)/shard_map/ppermute | solution.py:17
  30.7 14.9 %collective-permute-start.9 = (f32[128,256]{1,0:T(8,128)S(1)}, f32[128,256]{1,0:T(8,128)S(1)}, u32[]{:S(2)}, u32[]{:S(2)}) collective-permute-start(f32[128,256]{1,0:T(8,128)S(1)} %fusion.98), channel_id=1, source_target_pairs={{0,30},{2,0},{4,2},{6,4},{8,6},{10,8},{12,10},{14,12},{16,14},{18,... | collective-permute-start | bytes 393224 | tf_op jit(solution)/shard_map/ppermute | solution.py:17
  32.4 14.3 %collective-permute-start.8 = (f32[128,256]{1,0:T(8,128)S(1)}, f32[128,256]{1,0:T(8,128)S(1)}, u32[]{:S(2)}, u32[]{:S(2)}) collective-permute-start(f32[128,256]{1,0:T(8,128)S(1)} %fusion.99), channel_id=1, source_target_pairs={{0,30},{2,0},{4,2},{6,4},{8,6},{10,8},{12,10},{14,12},{16,14},{18,... | collective-permute-start | bytes 393224 | tf_op jit(solution)/shard_map/ppermute | solution.py:17
  38.1 9.3 %collective-permute-start.7 = (f32[128,256]{1,0:T(8,128)S(1)}, f32[128,256]{1,0:T(8,128)S(1)}, u32[]{:S(2)}, u32[]{:S(2)}) collective-permute-start(f32[128,256]{1,0:T(8,128)S(1)} %fusion.100), channel_id=1, source_target_pairs={{0,30},{2,0},{4,2},{6,4},{8,6},{10,8},{12,10},{14,12},{16,14},{18,... | collective-permute-start | bytes 393224 | tf_op jit(solution)/shard_map/ppermute | solution.py:17
  43.4 26.2 %collective-permute-start.13 = (f32[128,256]{1,0:T(8,128)S(1)}, f32[128,256]{1,0:T(8,128)S(1)}, u32[]{:S(2)}, u32[]{:S(2)}) collective-permute-start(f32[128,256]{1,0:T(8,128)S(1)} %fusion.95), channel_id=1, source_target_pairs={{0,30},{2,0},{4,2},{6,4},{8,6},{10,8},{12,10},{14,12},{16,14},{18,... | collective-permute-start | bytes 393224 | tf_op jit(solution)/shard_map/ppermute | solution.py:17
  44.5 17.1 %collective-permute-start.18 = (f32[128,256]{1,0:T(8,128)S(1)}, f32[128,256]{1,0:T(8,128)S(1)}, u32[]{:S(2)}, u32[]{:S(2)}) collective-permute-start(f32[128,256]{1,0:T(8,128)S(1)} %fusion.90), channel_id=1, source_target_pairs={{0,30},{2,0},{4,2},{6,4},{8,6},{10,8},{12,10},{14,12},{16,14},{18,... | collective-permute-start | bytes 393224 | tf_op jit(solution)/shard_map/ppermute | solution.py:17
  45.6 17.6 %collective-permute-start.17 = (f32[128,256]{1,0:T(8,128)S(1)}, f32[128,256]{1,0:T(8,128)S(1)}, u32[]{:S(2)}, u32[]{:S(2)}) collective-permute-start(f32[128,256]{1,0:T(8,128)S(1)} %fusion.91), channel_id=1, source_target_pairs={{0,30},{2,0},{4,2},{6,4},{8,6},{10,8},{12,10},{14,12},{16,14},{18,... | collective-permute-start | bytes 393224 | tf_op jit(solution)/shard_map/ppermute | solution.py:17
  46.7 17.6 %collective-permute-start.16 = (f32[128,256]{1,0:T(8,128)S(1)}, f32[128,256]{1,0:T(8,128)S(1)}, u32[]{:S(2)}, u32[]{:S(2)}) collective-permute-start(f32[128,256]{1,0:T(8,128)S(1)} %fusion.92), channel_id=1, source_target_pairs={{0,30},{2,0},{4,2},{6,4},{8,6},{10,8},{12,10},{14,12},{16,14},{18,... | collective-permute-start | bytes 393224 | tf_op jit(solution)/shard_map/ppermute | solution.py:17
  48.4 11.6 %collective-permute-start.12 = (f32[384,256]{1,0:T(8,128)S(1)}, f32[384,256]{1,0:T(8,128)S(1)}, u32[]{:S(2)}, u32[]{:S(2)}) collective-permute-start(f32[384,256]{1,0:T(8,128)S(1)} %fusion.30), channel_id=1, source_target_pairs={{0,1},{1,0},{2,3},{3,2},{4,5},{5,4},{6,7},{7,6},{8,9},{9,8},{10,11... | collective-permute-start | bytes 1179656 | tf_op jit(solution)/shard_map/ppermute | solution.py:34
  61.6 9.1 %collective-permute-start.14 = (f32[128,256]{1,0:T(8,128)S(1)}, f32[128,256]{1,0:T(8,128)S(1)}, u32[]{:S(2)}, u32[]{:S(2)}) collective-permute-start(f32[128,256]{1,0:T(8,128)S(1)} %fusion.94), channel_id=1, source_target_pairs={{0,30},{2,0},{4,2},{6,4},{8,6},{10,8},{12,10},{14,12},{16,14},{18,... | collective-permute-start | bytes 393224 | tf_op jit(solution)/shard_map/ppermute | solution.py:17
  63.2 16.0 %collective-permute-start.24 = (f32[128,256]{1,0:T(8,128)S(1)}, f32[128,256]{1,0:T(8,128)S(1)}, u32[]{:S(2)}, u32[]{:S(2)}) collective-permute-start(f32[128,256]{1,0:T(8,128)S(1)} %fusion.84), channel_id=1, source_target_pairs={{0,30},{2,0},{4,2},{6,4},{8,6},{10,8},{12,10},{14,12},{16,14},{18,... | collective-permute-start | bytes 393224 | tf_op jit(solution)/shard_map/ppermute | solution.py:17
  64.3 16.0 %collective-permute-start.23 = (f32[128,256]{1,0:T(8,128)S(1)}, f32[128,256]{1,0:T(8,128)S(1)}, u32[]{:S(2)}, u32[]{:S(2)}) collective-permute-start(f32[128,256]{1,0:T(8,128)S(1)} %fusion.85), channel_id=1, source_target_pairs={{0,30},{2,0},{4,2},{6,4},{8,6},{10,8},{12,10},{14,12},{16,14},{18,... | collective-permute-start | bytes 393224 | tf_op jit(solution)/shard_map/ppermute | solution.py:17
  65.4 16.0 %collective-permute-start.22 = (f32[128,256]{1,0:T(8,128)S(1)}, f32[128,256]{1,0:T(8,128)S(1)}, u32[]{:S(2)}, u32[]{:S(2)}) collective-permute-start(f32[128,256]{1,0:T(8,128)S(1)} %fusion.86), channel_id=1, source_target_pairs={{0,30},{2,0},{4,2},{6,4},{8,6},{10,8},{12,10},{14,12},{16,14},{18,... | collective-permute-start | bytes 393224 | tf_op jit(solution)/shard_map/ppermute | solution.py:17
  69.7 17.0 %collective-permute-start.21 = (f32[128,256]{1,0:T(8,128)S(1)}, f32[128,256]{1,0:T(8,128)S(1)}, u32[]{:S(2)}, u32[]{:S(2)}) collective-permute-start(f32[128,256]{1,0:T(8,128)S(1)} %fusion.87), channel_id=1, source_target_pairs={{0,30},{2,0},{4,2},{6,4},{8,6},{10,8},{12,10},{14,12},{16,14},{18,... | collective-permute-start | bytes 393224 | tf_op jit(solution)/shard_map/ppermute | solution.py:17
  73.9 8.6 %collective-permute-start.20 = (f32[128,256]{1,0:T(8,128)S(1)}, f32[128,256]{1,0:T(8,128)S(1)}, u32[]{:S(2)}, u32[]{:S(2)}) collective-permute-start(f32[128,256]{1,0:T(8,128)S(1)} %fusion.88), channel_id=1, source_target_pairs={{0,30},{2,0},{4,2},{6,4},{8,6},{10,8},{12,10},{14,12},{16,14},{18,... | collective-permute-start | bytes 393224 | tf_op jit(solution)/shard_map/ppermute | solution.py:17
  79.2 19.7 %collective-permute-start.25 = (f32[128,256]{1,0:T(8,128)S(1)}, f32[128,256]{1,0:T(8,128)S(1)}, u32[]{:S(2)}, u32[]{:S(2)}) collective-permute-start(f32[128,256]{1,0:T(8,128)S(1)} %fusion.83), channel_id=1, source_target_pairs={{0,30},{2,0},{4,2},{6,4},{8,6},{10,8},{12,10},{14,12},{16,14},{18,... | collective-permute-start | bytes 393224 | tf_op jit(solution)/shard_map/ppermute | solution.py:17
  80.3 14.5 %collective-permute-start.30 = (f32[128,256]{1,0:T(8,128)S(1)}, f32[128,256]{1,0:T(8,128)S(1)}, u32[]{:S(2)}, u32[]{:S(2)}) collective-permute-start(f32[128,256]{1,0:T(8,128)S(1)} %fusion.78), channel_id=1, source_target_pairs={{0,30},{2,0},{4,2},{6,4},{8,6},{10,8},{12,10},{14,12},{16,14},{18,... | collective-permute-start | bytes 393224 | tf_op jit(solution)/shard_map/ppermute | solution.py:17
  81.4 14.5 %collective-permute-start.29 = (f32[128,256]{1,0:T(8,128)S(1)}, f32[128,256]{1,0:T(8,128)S(1)}, u32[]{:S(2)}, u32[]{:S(2)}) collective-permute-start(f32[128,256]{1,0:T(8,128)S(1)} %fusion.79), channel_id=1, source_target_pairs={{0,30},{2,0},{4,2},{6,4},{8,6},{10,8},{12,10},{14,12},{16,14},{18,... | collective-permute-start | bytes 393224 | tf_op jit(solution)/shard_map/ppermute | solution.py:17
  82.5 14.5 %collective-permute-start.28 = (f32[128,256]{1,0:T(8,128)S(1)}, f32[128,256]{1,0:T(8,128)S(1)}, u32[]{:S(2)}, u32[]{:S(2)}) collective-permute-start(f32[128,256]{1,0:T(8,128)S(1)} %fusion.80), channel_id=1, source_target_pairs={{0,30},{2,0},{4,2},{6,4},{8,6},{10,8},{12,10},{14,12},{16,14},{18,... | collective-permute-start | bytes 393224 | tf_op jit(solution)/shard_map/ppermute | solution.py:17
  89.5 12.3 %collective-permute-start.27 = (f32[128,256]{1,0:T(8,128)S(1)}, f32[128,256]{1,0:T(8,128)S(1)}, u32[]{:S(2)}, u32[]{:S(2)}) collective-permute-start(f32[128,256]{1,0:T(8,128)S(1)} %fusion.81), channel_id=1, source_target_pairs={{0,30},{2,0},{4,2},{6,4},{8,6},{10,8},{12,10},{14,12},{16,14},{18,... | collective-permute-start | bytes 393224 | tf_op jit(solution)/shard_map/ppermute | solution.py:17
  94.8 24.7 %collective-permute-start.33 = (f32[128,256]{1,0:T(8,128)S(1)}, f32[128,256]{1,0:T(8,128)S(1)}, u32[]{:S(2)}, u32[]{:S(2)}) collective-permute-start(f32[128,256]{1,0:T(8,128)S(1)} %fusion.76), channel_id=1, source_target_pairs={{0,10},{2,12},{4,14},{6,16},{8,18},{10,20},{12,22},{14,24},{16,26}... | collective-permute-start | bytes 393224 | tf_op jit(solution)/shard_map/ppermute | solution.py:17
  95.9 29.8 %collective-permute-start.37 = (f32[128,256]{1,0:T(8,128)S(1)}, f32[128,256]{1,0:T(8,128)S(1)}, u32[]{:S(2)}, u32[]{:S(2)}) collective-permute-start(f32[128,256]{1,0:T(8,128)S(1)} %fusion.72), channel_id=1, source_target_pairs={{0,10},{2,12},{4,14},{6,16},{8,18},{10,20},{12,22},{14,24},{16,26}... | collective-permute-start | bytes 393224 | tf_op jit(solution)/shard_map/ppermute | solution.py:17
  97.0 28.7 %collective-permute-start.36 = (f32[128,256]{1,0:T(8,128)S(1)}, f32[128,256]{1,0:T(8,128)S(1)}, u32[]{:S(2)}, u32[]{:S(2)}) collective-permute-start(f32[128,256]{1,0:T(8,128)S(1)} %fusion.73), channel_id=1, source_target_pairs={{0,10},{2,12},{4,14},{6,16},{8,18},{10,20},{12,22},{14,24},{16,26}... | collective-permute-start | bytes 393224 | tf_op jit(solution)/shard_map/ppermute | solution.py:17
  98.9 26.8 %collective-permute-start.35 = (f32[128,256]{1,0:T(8,128)S(1)}, f32[128,256]{1,0:T(8,128)S(1)}, u32[]{:S(2)}, u32[]{:S(2)}) collective-permute-start(f32[128,256]{1,0:T(8,128)S(1)} %fusion.74), channel_id=1, source_target_pairs={{0,10},{2,12},{4,14},{6,16},{8,18},{10,20},{12,22},{14,24},{16,26}... | collective-permute-start | bytes 393224 | tf_op jit(solution)/shard_map/ppermute | solution.py:17
  101.8 17.7 %collective-permute-start.32 = (f32[128,256]{1,0:T(8,128)S(1)}, f32[128,256]{1,0:T(8,128)S(1)}, u32[]{:S(2)}, u32[]{:S(2)}) collective-permute-start(f32[128,256]{1,0:T(8,128)S(1)} %fusion.77), channel_id=1, source_target_pairs={{0,10},{2,12},{4,14},{6,16},{8,18},{10,20},{12,22},{14,24},{16,26}... | collective-permute-start | bytes 393224 | tf_op jit(solution)/shard_map/ppermute | solution.py:17
  119.5 7.8 %collective-permute-start.31 = (f32[384,256]{1,0:T(8,128)S(1)}, f32[384,256]{1,0:T(8,128)S(1)}, u32[]{:S(2)}, u32[]{:S(2)}) collective-permute-start(f32[384,256]{1,0:T(8,128)S(1)} %fusion.15), channel_id=1, source_target_pairs={{0,1},{1,0},{2,3},{3,2},{4,5},{5,4},{6,7},{7,6},{8,9},{9,8},{10,11... | collective-permute-start | bytes 1179656 | tf_op jit(solution)/shard_map/ppermute | solution.py:34
  (11 other events, 105.0 us)

commit v3 on v2

--- a/solution.py
+++ b/solution.py
@@ -1,12 +1,16 @@
+import functools
+
 import jax
 import jax.numpy as jnp
 from jax import lax
+from jax.experimental import pallas as pl
+from jax.experimental.pallas import tpu as pltpu
 from jax.sharding import PartitionSpec as P
 
 
 OUTER = 2
 STRATA = 3
-PIECES = 6
+PIECES = 3
 
 
 step_rate = 0.002
@@ -21,6 +25,68 @@
     return lax.dot_general(
         lhs, rhs, (dims, ((), ())), precision=lax.Precision.HIGH, preferred_element_type=jnp.float32
     )
+
+
+def halves(x):
+    high = x.astype(jnp.bfloat16)
+    return high, (x - high.astype(jnp.float32)).astype(jnp.bfloat16)
+
+
+def dot_of_halves(lhs, rhs, dims):
+    part = functools.partial(
+        lax.dot_general, dimension_numbers=(dims, ((), ())), preferred_element_type=jnp.float32
+    )
+    return part(lhs[0], rhs[0]) + (part(lhs[0], rhs[1]) + part(lhs[1], rhs[0]))
+
+
+def first_kernel(at, c_hbm, v_hbm, r_hbm, w_hbm, moved_ref, gain_ref, c, v, r, w, sems):
+    rows = v.shape[0]
+    copies = [
+        pltpu.make_async_copy(c_hbm, c, sems.at[0]),
+        pltpu.make_async_copy(v_hbm.at[0, pl.ds(at * rows, rows)], v, sems.at[1]),
+        pltpu.make_async_copy(r_hbm.at[0, 0, :, pl.ds(at * rows, rows)], r, sems.at[2]),
+        pltpu.make_async_copy(w_hbm.at[0, 0, :, pl.ds(at * rows, rows)], w, sems.at[3]),
+    ]
+    for copy in copies:
+        copy.start()
+    copies[0].wait()
+    copies[1].wait()
+    c_halves, v_halves = halves(c[...]), halves(v[...])
+    predicted = dot_of_halves(c_halves, v_halves, ((1,), (1,)))
+    copies[2].wait()
+    copies[3].wait()
+    residual = halves(w[...].astype(jnp.float32) * (r[...] - predicted))
+    moved_ref[...] = v[...] + step_rate * dot_of_halves(residual, c_halves, ((0,), (0,)))
+    gain_ref[...] = step_rate * dot_of_halves(residual, v_halves, ((1,), (0,)))
+
+
+def first_piece(at, user_factors, item_factors, ratings, observed):
+    users, rank = user_factors.shape
+    rows = item_factors.shape[1] // PIECES
+    anywhere = pl.BlockSpec(memory_space=pltpu.HBM)
+    inside = pl.BlockSpec(memory_space=pltpu.VMEM)
+    return pl.pallas_call(
+        functools.partial(first_kernel, at),
+        out_shape=(
+            jax.ShapeDtypeStruct((rows, rank), jnp.float32),
+            jax.ShapeDtypeStruct((users, rank), jnp.float32),
+        ),
+        in_specs=[anywhere] * 4,
+        out_specs=(inside, inside),
+        scratch_shapes=[
+            pltpu.VMEM((users, rank), jnp.float32),
+            pltpu.VMEM((rows, rank), jnp.float32),
+            pltpu.VMEM((users, rows), jnp.float32),
+            pltpu.VMEM((users, rows), jnp.bfloat16),
+            pltpu.SemaphoreType.DMA((4,)),
+        ],
+        compiler_params=pltpu.CompilerParams(vmem_limit_bytes=58 << 20),
+        cost_estimate=pl.CostEstimate(
+            flops=18 * users * rows * rank,
+            bytes_accessed=4 * (users * rank + rows * rank) + 6 * users * rows,
+            transcendentals=0,
+        ),
+    )(user_factors, item_factors, ratings, observed)
 
 
 def combine(current):
@@ -41,7 +107,7 @@
     factors_u = user_factors
     items = item_factors.shape[1]
     rows = items // PIECES
-    pieces = [item_factors[0, i * rows : (i + 1) * rows] for i in range(PIECES)]
+    pieces = [None] * PIECES
     last = OUTER * STRATA - 1
     for outer_step in range(OUTER):
         current = factors_u
@@ -49,13 +115,17 @@
             stratum = outer_step * STRATA + within
             gained = current
             for i in range(PIECES):
-                cols = slice(i * rows, (i + 1) * rows)
-                held = pieces[i]
-                predicted = dot(current, held, ((1,), (1,)))
-                weights = observed[0, stratum, :, cols].astype(jnp.float32)
-                residual = weights * (ratings[0, stratum, :, cols] - predicted)
-                moved = held + step_rate * dot(residual, current, ((0,), (0,)))
-                gained = gained + step_rate * dot(residual, held, ((1,), (0,)))
+                if stratum == 0:
+                    moved, gain = first_piece(i, current, item_factors, ratings, observed)
+                    gained = gained + gain
+                else:
+                    cols = slice(i * rows, (i + 1) * rows)
+                    held = pieces[i]
+                    predicted = dot(current, held, ((1,), (1,)))
+                    weights = observed[0, stratum, :, cols].astype(jnp.float32)
+                    residual = weights * (ratings[0, stratum, :, cols] - predicted)
+                    moved = held + step_rate * dot(residual, current, ((0,), (0,)))
+                    gained = gained + step_rate * dot(residual, held, ((1,), (0,)))
                 pieces[i] = from_behind(moved, "users", last if stratum == last else -1)
             current = gained
         factors_u = combine(current)

time: 128 us -> 109 us (0.85)
  matrix products: 47.7 us -> 21.7 us
  Pallas kernels: 0 us -> 8.83 us
  starting transfers between devices: 41.3 us -> 33.1 us
  waiting for transfers between devices: 36.4 us -> 40.8 us
  other arithmetic: 0.85 us -> 3.03 us
    dot_general x108 -> x45, matrix products: 47.7 us -> 21.7 us  [dot(): lax.dot_general(lhs, rhs, (dims, ((), ())), precision=lax.Precision.HIGH,...]
    ppermute x36 -> x18, waiting for transfers between devices: 25.6 us -> 35.7 us  [from_behind(): lax.ppermute(array, axis, [(i, (i + by) % peers) for i in range(peers)])]
    pallas_call x0 -> x3, Pallas kernels: none -> 8.83 us  [first_piece(): pl.pallas_call(functools.partial(first_kernel, at), out_shape=(jax.ShapeD...]
    ppermute x36 -> x18, starting transfers between devices: 38.1 us -> 31 us  [from_behind(): lax.ppermute(array, axis, [(i, (i + by) % peers) for i in range(peers)])]
    ppermute x2, waiting for transfers between devices: 10.8 us -> 5.11 us  [combine(): partner = lax.ppermute(summed, 'period', partners)]
  transfers between devices with their start and end apart: 38 -> 20, of which waited for: 7 -> 8; matrix products, arithmetic and copies ran while one was open for 34% -> 22% of each run, Pallas kernels for 0% -> 6%
where the time goes in v3:
time: 109 us
  waiting for transfers between devices  40.8 us (37%)
  starting transfers between devices  33.1 us (30%)
  matrix products  21.7 us (20%)
  Pallas kernels  8.83 us (8%)
  other arithmetic  3.03 us (3%)
  between operations  1.17 us (1%)
    ppermute x18, waiting for transfers between devices, from_behind(): lax.ppermute(array, axis, [(i, (i + by) % peers) for i in range(peers)])  35.7 us
    ppermute x18, starting transfers between devices, from_behind(): lax.ppermute(array, axis, [(i, (i + by) % peers) for i in range(peers)])  31 us
    dot_general x45, matrix products, dot(): lax.dot_general(lhs, rhs, (dims, ((), ())), precision=lax.Precision.HIGH,...  21.7 us
    pallas_call x3, Pallas kernels, first_piece(): pl.pallas_call(functools.partial(first_kernel, at), out_shape=(jax.ShapeD...  8.83 us
    ppermute x2, waiting for transfers between devices, combine(): partner = lax.ppermute(summed, 'period', partners)  5.11 us
  transfers between devices with their start and end apart: 20, of which 8 were waited for; matrix products, arithmetic and copies ran while one was open for 22% of the time, Pallas kernels for 6%

profile of v3, /device:TPU:0, one launch (start us, length us, event | category | flops | bytes accessed | tf_op | source)
XLA Modules:
  0.0 108.7 jit_solution(6857368914368536777)
XLA Ops:
  0.6 2.8 %shard_map.59 = (f32[256,256]{1,0:T(8,128)}, f32[384,256]{1,0:T(8,128)}) custom-call(f32[384,256]{1,0:T(8,128)} %c_hbm.5, f32[1,768,256]{2,1,0:T(8,128)} %v_hbm.5, f32[1,6,384,768]{3,2,1,0:T(8,128)} %r_hbm.5, bf16[1,6,384,768]{3,2,1,0:T(8,128)(2,1)} %w_hbm.5), custom_call_target="tpu_custom_call" | custom-call | flops 452984832 | bytes 1245184 | tf_op jit(solution)/shard_map/pallas_call | solution.py:68
  3.5 5.5 %collective-permute-start = (f32[256,256]{1,0:T(8,128)}, f32[256,256]{1,0:T(8,128)S(1)}, u32[]{:S(2)}, u32[]{:S(2)}) collective-permute-start(f32[256,256]{1,0:T(8,128)} %get-tuple-element.11), channel_id=1, source_target_pairs={{0,30},{2,0},{4,2},{6,4},{8,6},{10,8},{12,10},{14,12},{16,14},{18,... | collective-permute-start | bytes 786440 | tf_op jit(solution)/shard_map/ppermute | solution.py:21
  9.0 2.8 %shard_map.61 = (f32[256,256]{1,0:T(8,128)}, f32[384,256]{1,0:T(8,128)}) custom-call(f32[384,256]{1,0:T(8,128)} %c_hbm.5, f32[1,768,256]{2,1,0:T(8,128)} %v_hbm.5, f32[1,6,384,768]{3,2,1,0:T(8,128)} %r_hbm.5, bf16[1,6,384,768]{3,2,1,0:T(8,128)(2,1)} %w_hbm.5), custom_call_target="tpu_custom_call" | custom-call | flops 452984832 | bytes 1245184 | tf_op jit(solution)/shard_map/pallas_call | solution.py:68
  11.8 0.7 collective-permute-start.2
  12.6 3.2 %shard_map.60 = (f32[256,256]{1,0:T(8,128)}, f32[384,256]{1,0:T(8,128)}) custom-call(f32[384,256]{1,0:T(8,128)} %c_hbm.5, f32[1,768,256]{2,1,0:T(8,128)} %v_hbm.5, f32[1,6,384,768]{3,2,1,0:T(8,128)} %r_hbm.5, bf16[1,6,384,768]{3,2,1,0:T(8,128)(2,1)} %w_hbm.5), custom_call_target="tpu_custom_call" | custom-call | flops 452984832 | bytes 1245184 | tf_op jit(solution)/shard_map/pallas_call | solution.py:68
  15.9 1.2 %add_add_fusion = f32[384,256]{1,0:T(8,128)S(1)} fusion(f32[384,256]{1,0:T(8,128)S(1)} %copy-done.3, f32[384,256]{1,0:T(8,128)} %get-tuple-element.9, f32[384,256]{1,0:T(8,128)S(1)} %copy-done.1, f32[384,256]{1,0:T(8,128)S(1)} %copy-done.2), kind=kLoop, calls=%fused_computation.93 | loop fusion | flops 294912 | bytes 1966080 | tf_op jit(solution)/shard_map/add | solution.py:120
  17.1 2.9 %collective-permute-done.1 = f32[256,256]{1,0:T(8,128)S(1)} collective-permute-done((f32[256,256]{1,0:T(8,128)}, f32[256,256]{1,0:T(8,128)S(1)}, u32[]{:S(2)}, u32[]{:S(2)}) %collective-permute-start.1) | collective-permute-done | bytes 262176 | tf_op jit(solution)/shard_map/ppermute | solution.py:21
  20.0 1.4 %fusion.4 = f32[384,256]{1,0:T(8,128)S(1)} fusion(f32[384,256]{1,0:T(8,128)S(1)} %add_add_fusion, f32[256,256]{1,0:T(8,128)S(1)} %collective-permute-done.1, f32[1,6,384,768]{3,2,1,0:T(8,128)} %r_hbm.5, bf16[1,6,384,768]{3,2,1,0:T(8,128)(2,1)S(1)} %copy-done), kind=kOutput, calls=%fused_computation.34 | convolution fusion | flops 151289856 | bytes 1638400 | tf_op jit(solution)/shard_map/dot_general | solution.py:25
  21.9 4.5 %collective-permute-start.4 = (f32[256,256]{1,0:T(8,128)S(1)}, f32[256,256]{1,0:T(8,128)S(1)}, u32[]{:S(2)}, u32[]{:S(2)}) collective-permute-start(f32[256,256]{1,0:T(8,128)S(1)} %fusion.31), channel_id=1, source_target_pairs={{0,30},{2,0},{4,2},{6,4},{8,6},{10,8},{12,10},{14,12},{16,14},{18,... | collective-permute-start | bytes 786440 | tf_op jit(solution)/shard_map/ppermute | solution.py:21
  26.5 1.4 %fusion.5 = f32[384,256]{1,0:T(8,128)S(1)} fusion(f32[384,256]{1,0:T(8,128)S(1)} %add_add_fusion, f32[256,256]{1,0:T(8,128)S(1)} %collective-permute-done.2, f32[1,6,384,768]{3,2,1,0:T(8,128)} %r_hbm.5, bf16[1,6,384,768]{3,2,1,0:T(8,128)(2,1)S(1)} %copy-done), kind=kOutput, calls=%fused_computation.35 | convolution fusion | flops 151289856 | bytes 1638400 | tf_op jit(solution)/shard_map/dot_general | solution.py:25
  27.9 0.5 fusion.32
  28.5 1.7 %fusion = f32[384,256]{1,0:T(8,128)S(1)} fusion(f32[384,256]{1,0:T(8,128)S(1)} %add_add_fusion, f32[256,256]{1,0:T(8,128)S(1)} %collective-permute-done, f32[1,6,384,768]{3,2,1,0:T(8,128)} %r_hbm.5, bf16[1,6,384,768]{3,2,1,0:T(8,128)(2,1)S(1)} %copy-done), kind=kOutput, calls=%fused_computation.30 | convolution fusion | flops 151289856 | bytes 1638400 | tf_op jit(solution)/shard_map/dot_general | solution.py:25
  30.2 0.5 fusion.30
  31.8 4.2 %collective-permute-done.3 = f32[256,256]{1,0:T(8,128)S(1)} collective-permute-done((f32[256,256]{1,0:T(8,128)S(1)}, f32[256,256]{1,0:T(8,128)S(1)}, u32[]{:S(2)}, u32[]{:S(2)}) %collective-permute-start.3) | collective-permute-done | bytes 262176 | tf_op jit(solution)/shard_map/ppermute | solution.py:21
  36.4 0.5 fusion.33
  36.9 4.7 %collective-permute-start.7 = (f32[256,256]{1,0:T(8,128)S(1)}, f32[256,256]{1,0:T(8,128)S(1)}, u32[]{:S(2)}, u32[]{:S(2)}) collective-permute-start(f32[256,256]{1,0:T(8,128)S(1)} %fusion.33), channel_id=1, source_target_pairs={{0,30},{2,0},{4,2},{6,4},{8,6},{10,8},{12,10},{14,12},{16,14},{18,... | collective-permute-start | bytes 786440 | tf_op jit(solution)/shard_map/ppermute | solution.py:21
  43.4 1.6 %collective-permute-start.6 = (f32[384,256]{1,0:T(8,128)S(1)}, f32[384,256]{1,0:T(8,128)S(1)}, u32[]{:S(2)}, u32[]{:S(2)}) collective-permute-start(f32[384,256]{1,0:T(8,128)S(1)} %fusion.9), channel_id=1, source_target_pairs={{0,1},{1,0},{2,3},{3,2},{4,5},{5,4},{6,7},{7,6},{8,9},{9,8},{10,11... | collective-permute-start | bytes 1179656 | tf_op jit(solution)/shard_map/ppermute | solution.py:100
  46.1 5.1 %collective-permute-done.6 = f32[384,256]{1,0:T(8,128)S(1)} collective-permute-done((f32[384,256]{1,0:T(8,128)S(1)}, f32[384,256]{1,0:T(8,128)S(1)}, u32[]{:S(2)}, u32[]{:S(2)}) %collective-permute-start.6) | collective-permute-done | bytes 393248 | tf_op jit(solution)/shard_map/ppermute | solution.py:100
  51.7 0.5 fusion.38
  52.2 3.0 %collective-permute-start.12 = (f32[256,256]{1,0:T(8,128)S(1)}, f32[256,256]{1,0:T(8,128)S(1)}, u32[]{:S(2)}, u32[]{:S(2)}) collective-permute-start(f32[256,256]{1,0:T(8,128)S(1)} %fusion.38), channel_id=1, source_target_pairs={{0,30},{2,0},{4,2},{6,4},{8,6},{10,8},{12,10},{14,12},{16,14},{18,... | collective-permute-start | bytes 786440 | tf_op jit(solution)/shard_map/ppermute | solution.py:21
  56.1 1.7 %collective-permute-start.11 = (f32[256,256]{1,0:T(8,128)S(1)}, f32[256,256]{1,0:T(8,128)S(1)}, u32[]{:S(2)}, u32[]{:S(2)}) collective-permute-start(f32[256,256]{1,0:T(8,128)S(1)} %fusion.37), channel_id=1, source_target_pairs={{0,30},{2,0},{4,2},{6,4},{8,6},{10,8},{12,10},{14,12},{16,14},{18,... | collective-permute-start | bytes 786440 | tf_op jit(solution)/shard_map/ppermute | solution.py:21
  59.8 4.9 %collective-permute-done.10 = f32[256,256]{1,0:T(8,128)S(1)} collective-permute-done((f32[256,256]{1,0:T(8,128)S(1)}, f32[256,256]{1,0:T(8,128)S(1)}, u32[]{:S(2)}, u32[]{:S(2)}) %collective-permute-start.10) | collective-permute-done | bytes 262176 | tf_op jit(solution)/shard_map/ppermute | solution.py:21
  65.1 0.5 fusion.39
  65.6 4.7 %collective-permute-start.13 = (f32[256,256]{1,0:T(8,128)S(1)}, f32[256,256]{1,0:T(8,128)S(1)}, u32[]{:S(2)}, u32[]{:S(2)}) collective-permute-start(f32[256,256]{1,0:T(8,128)S(1)} %fusion.39), channel_id=1, source_target_pairs={{0,30},{2,0},{4,2},{6,4},{8,6},{10,8},{12,10},{14,12},{16,14},{18,... | collective-permute-start | bytes 786440 | tf_op jit(solution)/shard_map/ppermute | solution.py:21
  73.2 6.6 %collective-permute-done.14 = f32[256,256]{1,0:T(8,128)S(1)} collective-permute-done((f32[256,256]{1,0:T(8,128)S(1)}, f32[256,256]{1,0:T(8,128)S(1)}, u32[]{:S(2)}, u32[]{:S(2)}) %collective-permute-start.14) | collective-permute-done | bytes 262176 | tf_op jit(solution)/shard_map/ppermute | solution.py:21
  82.6 5.5 %collective-permute-start.17 = (f32[256,256]{1,0:T(8,128)S(1)}, f32[256,256]{1,0:T(8,128)S(1)}, u32[]{:S(2)}, u32[]{:S(2)}) collective-permute-start(f32[256,256]{1,0:T(8,128)S(1)} %fusion.42), channel_id=1, source_target_pairs={{0,10},{2,12},{4,14},{6,16},{8,18},{10,20},{12,22},{14,24},{16,26}... | collective-permute-start | bytes 786440 | tf_op jit(solution)/shard_map/ppermute | solution.py:21
  89.2 0.6 collective-permute-start.16
  89.8 11.5 %collective-permute-done.18 = f32[256,256]{1,0:T(8,128)S(1)} collective-permute-done((f32[256,256]{1,0:T(8,128)S(1)}, f32[256,256]{1,0:T(8,128)S(1)}, u32[]{:S(2)}, u32[]{:S(2)}) %collective-permute-start.18) | collective-permute-done | bytes 262176 | tf_op jit(solution)/shard_map/ppermute | solution.py:21
  101.3 2.8 %collective-permute-done.19 = f32[256,256]{1,0:T(8,128)S(1)} collective-permute-done((f32[256,256]{1,0:T(8,128)S(1)}, f32[256,256]{1,0:T(8,128)S(1)}, u32[]{:S(2)}, u32[]{:S(2)}) %collective-permute-start.19) | collective-permute-done | bytes 262176 | tf_op jit(solution)/shard_map/ppermute | solution.py:21
  104.1 2.8 %collective-permute-done.17 = f32[256,256]{1,0:T(8,128)S(1)} collective-permute-done((f32[256,256]{1,0:T(8,128)S(1)}, f32[256,256]{1,0:T(8,128)S(1)}, u32[]{:S(2)}, u32[]{:S(2)}) %collective-permute-start.17) | collective-permute-done | bytes 262176 | tf_op jit(solution)/shard_map/ppermute | solution.py:21
  106.9 0.9 maximum_bitcast_fusion
  107.8 0.8 add_multiply_fusion
  (73 shorter events, 15.5 us)
Async XLA Ops:
  3.5 25.0 %collective-permute-start = (f32[256,256]{1,0:T(8,128)}, f32[256,256]{1,0:T(8,128)S(1)}, u32[]{:S(2)}, u32[]{:S(2)}) collective-permute-start(f32[256,256]{1,0:T(8,128)} %get-tuple-element.11), channel_id=1, source_target_pairs={{0,30},{2,0},{4,2},{6,4},{8,6},{10,8},{12,10},{14,12},{16,14},{18,... | collective-permute-start | bytes 786440 | tf_op jit(solution)/shard_map/ppermute | solution.py:21
  11.8 4.0 %copy-start.1 = (f32[384,256]{1,0:T(8,128)S(1)}, f32[384,256]{1,0:T(8,128)}, u32[]{:S(2)}) copy-start(f32[384,256]{1,0:T(8,128)} %c_hbm.5) | copy-start | bytes 1179652
  11.8 4.0 %copy-start.2 = (f32[384,256]{1,0:T(8,128)S(1)}, f32[384,256]{1,0:T(8,128)}, u32[]{:S(2)}) copy-start(f32[384,256]{1,0:T(8,128)} %get-tuple-element.8) | copy-start | bytes 1179652
  11.8 4.0 %copy-start.3 = (f32[384,256]{1,0:T(8,128)S(1)}, f32[384,256]{1,0:T(8,128)}, u32[]{:S(2)}) copy-start(f32[384,256]{1,0:T(8,128)} %get-tuple-element.10) | copy-start | bytes 1179652
  11.8 8.2 %copy-start = (bf16[1,6,384,768]{3,2,1,0:T(8,128)(2,1)S(1)}, bf16[1,6,384,768]{3,2,1,0:T(8,128)(2,1)}, u32[]{:S(2)}) copy-start(bf16[1,6,384,768]{3,2,1,0:T(8,128)(2,1)} %w_hbm.5) | copy-start | bytes 10616836
  11.8 14.6 %collective-permute-start.2 = (f32[256,256]{1,0:T(8,128)}, f32[256,256]{1,0:T(8,128)S(1)}, u32[]{:S(2)}, u32[]{:S(2)}) collective-permute-start(f32[256,256]{1,0:T(8,128)} %get-tuple-element.13), channel_id=1, source_target_pairs={{0,30},{2,0},{4,2},{6,4},{8,6},{10,8},{12,10},{14,12},{16,14},{18,... | collective-permute-start | bytes 786440 | tf_op jit(solution)/shard_map/ppermute | solution.py:21
  15.8 4.3 %collective-permute-start.1 = (f32[256,256]{1,0:T(8,128)}, f32[256,256]{1,0:T(8,128)S(1)}, u32[]{:S(2)}, u32[]{:S(2)}) collective-permute-start(f32[256,256]{1,0:T(8,128)} %get-tuple-element.12), channel_id=1, source_target_pairs={{0,30},{2,0},{4,2},{6,4},{8,6},{10,8},{12,10},{14,12},{16,14},{18,... | collective-permute-start | bytes 786440 | tf_op jit(solution)/shard_map/ppermute | solution.py:21
  15.9 20.1 %slice-start = ((s8[7077888]{0:T(1024)(128)(4,1)}), s8[2883584]{0:T(1024)(128)(4,1)S(1)}, s32[]{:S(2)}) async-start(s8[7077888]{0:T(1024)(128)(4,1)} %bitcast.167), calls=%async_computation | async-start | bytes 5767168
  21.9 20.4 %collective-permute-start.4 = (f32[256,256]{1,0:T(8,128)S(1)}, f32[256,256]{1,0:T(8,128)S(1)}, u32[]{:S(2)}, u32[]{:S(2)}) collective-permute-start(f32[256,256]{1,0:T(8,128)S(1)} %fusion.31), channel_id=1, source_target_pairs={{0,30},{2,0},{4,2},{6,4},{8,6},{10,8},{12,10},{14,12},{16,14},{18,... | collective-permute-start | bytes 786440 | tf_op jit(solution)/shard_map/ppermute | solution.py:21
  27.8 8.1 %slice-start.1 = ((s8[7077888]{0:T(1024)(128)(4,1)}), s8[4194304]{0:T(1024)(128)(4,1)S(1)}, s32[]{:S(2)}) async-start(s8[7077888]{0:T(1024)(128)(4,1)} %bitcast.167), calls=%async_computation.1 | async-start | bytes 8388608
  28.4 13.2 %collective-permute-start.5 = (f32[256,256]{1,0:T(8,128)S(1)}, f32[256,256]{1,0:T(8,128)S(1)}, u32[]{:S(2)}, u32[]{:S(2)}) collective-permute-start(f32[256,256]{1,0:T(8,128)S(1)} %fusion.32), channel_id=1, source_target_pairs={{0,30},{2,0},{4,2},{6,4},{8,6},{10,8},{12,10},{14,12},{16,14},{18,... | collective-permute-start | bytes 786440 | tf_op jit(solution)/shard_map/ppermute | solution.py:21
  30.7 5.3 %collective-permute-start.3 = (f32[256,256]{1,0:T(8,128)S(1)}, f32[256,256]{1,0:T(8,128)S(1)}, u32[]{:S(2)}, u32[]{:S(2)}) collective-permute-start(f32[256,256]{1,0:T(8,128)S(1)} %fusion.30), channel_id=1, source_target_pairs={{0,30},{2,0},{4,2},{6,4},{8,6},{10,8},{12,10},{14,12},{16,14},{18,... | collective-permute-start | bytes 786440 | tf_op jit(solution)/shard_map/ppermute | solution.py:21
  36.9 20.9 %collective-permute-start.7 = (f32[256,256]{1,0:T(8,128)S(1)}, f32[256,256]{1,0:T(8,128)S(1)}, u32[]{:S(2)}, u32[]{:S(2)}) collective-permute-start(f32[256,256]{1,0:T(8,128)S(1)} %fusion.33), channel_id=1, source_target_pairs={{0,30},{2,0},{4,2},{6,4},{8,6},{10,8},{12,10},{14,12},{16,14},{18,... | collective-permute-start | bytes 786440 | tf_op jit(solution)/shard_map/ppermute | solution.py:21
  43.4 7.8 %collective-permute-start.6 = (f32[384,256]{1,0:T(8,128)S(1)}, f32[384,256]{1,0:T(8,128)S(1)}, u32[]{:S(2)}, u32[]{:S(2)}) collective-permute-start(f32[384,256]{1,0:T(8,128)S(1)} %fusion.9), channel_id=1, source_target_pairs={{0,1},{1,0},{2,3},{3,2},{4,5},{5,4},{6,7},{7,6},{8,9},{9,8},{10,11... | collective-permute-start | bytes 1179656 | tf_op jit(solution)/shard_map/ppermute | solution.py:100
  45.5 5.8 %collective-permute-start.9 = (f32[256,256]{1,0:T(8,128)S(1)}, f32[256,256]{1,0:T(8,128)S(1)}, u32[]{:S(2)}, u32[]{:S(2)}) collective-permute-start(f32[256,256]{1,0:T(8,128)S(1)} %fusion.35), channel_id=1, source_target_pairs={{0,30},{2,0},{4,2},{6,4},{8,6},{10,8},{12,10},{14,12},{16,14},{18,... | collective-permute-start | bytes 786440 | tf_op jit(solution)/shard_map/ppermute | solution.py:21
  46.1 9.1 %collective-permute-start.8 = (f32[256,256]{1,0:T(8,128)S(1)}, f32[256,256]{1,0:T(8,128)S(1)}, u32[]{:S(2)}, u32[]{:S(2)}) collective-permute-start(f32[256,256]{1,0:T(8,128)S(1)} %fusion.34), channel_id=1, source_target_pairs={{0,30},{2,0},{4,2},{6,4},{8,6},{10,8},{12,10},{14,12},{16,14},{18,... | collective-permute-start | bytes 786440 | tf_op jit(solution)/shard_map/ppermute | solution.py:21
  52.2 18.0 %collective-permute-start.12 = (f32[256,256]{1,0:T(8,128)S(1)}, f32[256,256]{1,0:T(8,128)S(1)}, u32[]{:S(2)}, u32[]{:S(2)}) collective-permute-start(f32[256,256]{1,0:T(8,128)S(1)} %fusion.38), channel_id=1, source_target_pairs={{0,30},{2,0},{4,2},{6,4},{8,6},{10,8},{12,10},{14,12},{16,14},{18,... | collective-permute-start | bytes 786440 | tf_op jit(solution)/shard_map/ppermute | solution.py:21
  56.1 15.1 %collective-permute-start.11 = (f32[256,256]{1,0:T(8,128)S(1)}, f32[256,256]{1,0:T(8,128)S(1)}, u32[]{:S(2)}, u32[]{:S(2)}) collective-permute-start(f32[256,256]{1,0:T(8,128)S(1)} %fusion.37), channel_id=1, source_target_pairs={{0,30},{2,0},{4,2},{6,4},{8,6},{10,8},{12,10},{14,12},{16,14},{18,... | collective-permute-start | bytes 786440 | tf_op jit(solution)/shard_map/ppermute | solution.py:21
  58.7 6.0 %collective-permute-start.10 = (f32[256,256]{1,0:T(8,128)S(1)}, f32[256,256]{1,0:T(8,128)S(1)}, u32[]{:S(2)}, u32[]{:S(2)}) collective-permute-start(f32[256,256]{1,0:T(8,128)S(1)} %fusion.36), channel_id=1, source_target_pairs={{0,30},{2,0},{4,2},{6,4},{8,6},{10,8},{12,10},{14,12},{16,14},{18,... | collective-permute-start | bytes 786440 | tf_op jit(solution)/shard_map/ppermute | solution.py:21
  65.6 16.2 %collective-permute-start.13 = (f32[256,256]{1,0:T(8,128)S(1)}, f32[256,256]{1,0:T(8,128)S(1)}, u32[]{:S(2)}, u32[]{:S(2)}) collective-permute-start(f32[256,256]{1,0:T(8,128)S(1)} %fusion.39), channel_id=1, source_target_pairs={{0,30},{2,0},{4,2},{6,4},{8,6},{10,8},{12,10},{14,12},{16,14},{18,... | collective-permute-start | bytes 786440 | tf_op jit(solution)/shard_map/ppermute | solution.py:21
  71.1 9.6 %collective-permute-start.15 = (f32[256,256]{1,0:T(8,128)S(1)}, f32[256,256]{1,0:T(8,128)S(1)}, u32[]{:S(2)}, u32[]{:S(2)}) collective-permute-start(f32[256,256]{1,0:T(8,128)S(1)} %fusion.41), channel_id=1, source_target_pairs={{0,30},{2,0},{4,2},{6,4},{8,6},{10,8},{12,10},{14,12},{16,14},{18,... | collective-permute-start | bytes 786440 | tf_op jit(solution)/shard_map/ppermute | solution.py:21
  72.1 7.7 %collective-permute-start.14 = (f32[256,256]{1,0:T(8,128)S(1)}, f32[256,256]{1,0:T(8,128)S(1)}, u32[]{:S(2)}, u32[]{:S(2)}) collective-permute-start(f32[256,256]{1,0:T(8,128)S(1)} %fusion.40), channel_id=1, source_target_pairs={{0,30},{2,0},{4,2},{6,4},{8,6},{10,8},{12,10},{14,12},{16,14},{18,... | collective-permute-start | bytes 786440 | tf_op jit(solution)/shard_map/ppermute | solution.py:21
  80.7 20.6 %collective-permute-start.18 = (f32[256,256]{1,0:T(8,128)S(1)}, f32[256,256]{1,0:T(8,128)S(1)}, u32[]{:S(2)}, u32[]{:S(2)}) collective-permute-start(f32[256,256]{1,0:T(8,128)S(1)} %fusion.43), channel_id=1, source_target_pairs={{0,10},{2,12},{4,14},{6,16},{8,18},{10,20},{12,22},{14,24},{16,26}... | collective-permute-start | bytes 786440 | tf_op jit(solution)/shard_map/ppermute | solution.py:21
  81.7 22.4 %collective-permute-start.19 = (f32[256,256]{1,0:T(8,128)S(1)}, f32[256,256]{1,0:T(8,128)S(1)}, u32[]{:S(2)}, u32[]{:S(2)}) collective-permute-start(f32[256,256]{1,0:T(8,128)S(1)} %fusion.44), channel_id=1, source_target_pairs={{0,10},{2,12},{4,14},{6,16},{8,18},{10,20},{12,22},{14,24},{16,26}... | collective-permute-start | bytes 786440 | tf_op jit(solution)/shard_map/ppermute | solution.py:21
  82.6 24.3 %collective-permute-start.17 = (f32[256,256]{1,0:T(8,128)S(1)}, f32[256,256]{1,0:T(8,128)S(1)}, u32[]{:S(2)}, u32[]{:S(2)}) collective-permute-start(f32[256,256]{1,0:T(8,128)S(1)} %fusion.42), channel_id=1, source_target_pairs={{0,10},{2,12},{4,14},{6,16},{8,18},{10,20},{12,22},{14,24},{16,26}... | collective-permute-start | bytes 786440 | tf_op jit(solution)/shard_map/ppermute | solution.py:21
  89.2 18.7 %collective-permute-start.16 = (f32[384,256]{1,0:T(8,128)S(1)}, f32[384,256]{1,0:T(8,128)S(1)}, u32[]{:S(2)}, u32[]{:S(2)}) collective-permute-start(f32[384,256]{1,0:T(8,128)S(1)} %fusion.27), channel_id=1, source_target_pairs={{0,1},{1,0},{2,3},{3,2},{4,5},{5,4},{6,7},{7,6},{8,9},{9,8},{10,11... | collective-permute-start | bytes 1179656 | tf_op jit(solution)/shard_map/ppermute | solution.py:100

commit v4 on v2

--- a/solution.py
+++ b/solution.py
@@ -1,12 +1,14 @@
 import jax
 import jax.numpy as jnp
 from jax import lax
+from jax.experimental import pallas as pl
+from jax.experimental.pallas import tpu as pltpu
 from jax.sharding import PartitionSpec as P
 
 
 OUTER = 2
 STRATA = 3
-PIECES = 6
+PIECES = 3
 
 
 step_rate = 0.002
@@ -21,6 +23,32 @@
     return lax.dot_general(
         lhs, rhs, (dims, ((), ())), precision=lax.Precision.HIGH, preferred_element_type=jnp.float32
     )
+
+
+def load_kernel(c_in, v_in, r_in, w_in, c_out, v_out, r_out, w_out, sems):
+    copies = [
+        pltpu.make_async_copy(c_in, c_out, sems.at[0]),
+        pltpu.make_async_copy(v_in.at[0], v_out, sems.at[1]),
+        pltpu.make_async_copy(r_in.at[0, 0], r_out, sems.at[2]),
+        pltpu.make_async_copy(w_in.at[0, 0], w_out, sems.at[3]),
+    ]
+    for copy in copies:
+        copy.start()
+    for copy in copies:
+        copy.wait()
+
+
+def load_first(user_factors, item_factors, ratings, observed):
+    operands = (user_factors, item_factors, ratings, observed)
+    shapes = (user_factors.shape, item_factors.shape[1:], ratings.shape[2:], observed.shape[2:])
+    return pl.pallas_call(
+        load_kernel,
+        out_shape=tuple(jax.ShapeDtypeStruct(s, a.dtype) for s, a in zip(shapes, operands)),
+        in_specs=[pl.BlockSpec(memory_space=pltpu.HBM)] * 4,
+        out_specs=(pl.BlockSpec(memory_space=pltpu.VMEM),) * 4,
+        scratch_shapes=[pltpu.SemaphoreType.DMA((4,))],
+        compiler_params=pltpu.CompilerParams(vmem_limit_bytes=8 << 20),
+    )(*[pltpu.with_memory_space_constraint(a, pltpu.HBM) for a in operands])
 
 
 def combine(current):
@@ -38,10 +66,12 @@
 
 
 def on_device(ratings, observed, user_factors, item_factors):
-    factors_u = user_factors
+    factors_u, first_items, first_ratings, first_weights = load_first(
+        user_factors, item_factors, ratings, observed
+    )
     items = item_factors.shape[1]
     rows = items // PIECES
-    pieces = [item_factors[0, i * rows : (i + 1) * rows] for i in range(PIECES)]
+    pieces = [first_items[i * rows : (i + 1) * rows] for i in range(PIECES)]
     last = OUTER * STRATA - 1
     for outer_step in range(OUTER):
         current = factors_u
@@ -50,10 +80,13 @@
             gained = current
             for i in range(PIECES):
                 cols = slice(i * rows, (i + 1) * rows)
+                if stratum == 0:
+                    tile, weights = first_ratings[:, cols], first_weights[:, cols]
+                else:
+                    tile, weights = ratings[0, stratum, :, cols], observed[0, stratum, :, cols]
                 held = pieces[i]
                 predicted = dot(current, held, ((1,), (1,)))
-                weights = observed[0, stratum, :, cols].astype(jnp.float32)
-                residual = weights * (ratings[0, stratum, :, cols] - predicted)
+                residual = weights.astype(jnp.float32) * (tile - predicted)
                 moved = held + step_rate * dot(residual, current, ((0,), (0,)))
                 gained = gained + step_rate * dot(residual, held, ((1,), (0,)))
                 pieces[i] = from_behind(moved, "users", last if stratum == last else -1)

time: 128 us -> 104 us (0.81)
  matrix products: 47.7 us -> 21.9 us
  starting transfers between devices: 41.3 us -> 33.3 us
  waiting for transfers between devices: 36.4 us -> 44.1 us
  Pallas kernels: 0 us -> 1.96 us
    dot_general x108 -> x54, matrix products: 47.7 us -> 21.9 us  [dot(): lax.dot_general(lhs, rhs, (dims, ((), ())), precision=lax.Precision.HIGH,...]
    ppermute x36 -> x18, waiting for transfers between devices: 25.6 us -> 39 us  [from_behind(): lax.ppermute(array, axis, [(i, (i + by) % peers) for i in range(peers)])]
    ppermute x36 -> x18, starting transfers between devices: 38.1 us -> 30.1 us  [from_behind(): lax.ppermute(array, axis, [(i, (i + by) % peers) for i in range(peers)])]
    ppermute x2, waiting for transfers between devices: 10.8 us -> 5.1 us  [combine(): partner = lax.ppermute(summed, 'period', partners)]
    pallas_call x0 -> x1, Pallas kernels: none -> 1.96 us  [load_first(): pl.pallas_call(load_kernel, out_shape=tuple((jax.ShapeDtypeStruct(s, a.dt...]
  transfers between devices with their start and end apart: 38 -> 20, of which waited for: 7 -> 8; matrix products, arithmetic and copies ran while one was open for 34% -> 21% of each run, Pallas kernels for 0% -> 0%
where the time goes in v4:
time: 104 us
  waiting for transfers between devices  44.1 us (42%)
  starting transfers between devices  33.3 us (32%)
  matrix products  21.9 us (21%)
  Pallas kernels  1.96 us (2%)
  other arithmetic  1.78 us (2%)
  between operations  1.19 us (1%)
    ppermute x18, waiting for transfers between devices, from_behind(): lax.ppermute(array, axis, [(i, (i + by) % peers) for i in range(peers)])  39 us
    ppermute x18, starting transfers between devices, from_behind(): lax.ppermute(array, axis, [(i, (i + by) % peers) for i in range(peers)])  30.1 us
    dot_general x54, matrix products, dot(): lax.dot_general(lhs, rhs, (dims, ((), ())), precision=lax.Precision.HIGH,...  21.9 us
    ppermute x2, waiting for transfers between devices, combine(): partner = lax.ppermute(summed, 'period', partners)  5.1 us
    ppermute x2, starting transfers between devices, combine(): partner = lax.ppermute(summed, 'period', partners)  3.17 us
  transfers between devices with their start and end apart: 20, of which 8 were waited for; matrix products, arithmetic and copies ran while one was open for 21% of the time, Pallas kernels for 0%

profile of v4, /device:TPU:0, one launch (start us, length us, event | category | flops | bytes accessed | tf_op | source)
XLA Modules:
  0.0 104.2 jit_solution(2609300245144986607)
XLA Ops:
  0.6 2.0 %shard_map.59 = (f32[384,256]{1,0:T(8,128)S(1)}, f32[768,256]{1,0:T(8,128)S(1)}, f32[384,768]{1,0:T(8,128)S(1)}, bf16[384,768]{1,0:T(8,128)(2,1)S(1)}) custom-call(f32[384,256]{1,0:T(8,128)} %c_in.1, f32[1,768,256]{2,1,0:T(8,128)} %v_in.1, f32[1,6,384,768]{3,2,1,0:T(8,128)} %r_in.1, bf16[1,6,384,768]{3,2,1,0:T(8,128)(2,1)} %w_in.1), custom_call_target="tpu_custom_call" | custom-call | tf_op jit(solution)/shard_map/pallas_call | solution.py:44
  3.0 0.5 fusion.38
  3.5 5.5 %collective-permute-start.2 = (f32[256,256]{1,0:T(8,128)S(1)}, f32[256,256]{1,0:T(8,128)S(1)}, u32[]{:S(2)}, u32[]{:S(2)}) collective-permute-start(f32[256,256]{1,0:T(8,128)S(1)} %fusion.38), channel_id=1, source_target_pairs={{0,30},{2,0},{4,2},{6,4},{8,6},{10,8},{12,10},{14,12},{16,14},{18,... | collective-permute-start | bytes 786440 | tf_op jit(solution)/shard_map/ppermute | solution.py:19
  9.4 0.5 fusion.37
  9.9 0.7 collective-permute-start.1
  12.7 5.9 %collective-permute-done = f32[256,256]{1,0:T(8,128)S(1)} collective-permute-done((f32[256,256]{1,0:T(8,128)S(1)}, f32[256,256]{1,0:T(8,128)S(1)}, u32[]{:S(2)}, u32[]{:S(2)}) %collective-permute-start) | collective-permute-done | bytes 262176 | tf_op jit(solution)/shard_map/ppermute | solution.py:19
  18.9 0.5 fusion.39
  19.4 4.7 %collective-permute-start.3 = (f32[256,256]{1,0:T(8,128)S(1)}, f32[256,256]{1,0:T(8,128)S(1)}, u32[]{:S(2)}, u32[]{:S(2)}) collective-permute-start(f32[256,256]{1,0:T(8,128)S(1)} %fusion.39), channel_id=1, source_target_pairs={{0,30},{2,0},{4,2},{6,4},{8,6},{10,8},{12,10},{14,12},{16,14},{18,... | collective-permute-start | bytes 786440 | tf_op jit(solution)/shard_map/ppermute | solution.py:19
  24.5 0.5 fusion.40
  25.5 0.5 fusion.41
  27.1 6.5 %collective-permute-done.5 = f32[256,256]{1,0:T(8,128)S(1)} collective-permute-done((f32[256,256]{1,0:T(8,128)S(1)}, f32[256,256]{1,0:T(8,128)S(1)}, u32[]{:S(2)}, u32[]{:S(2)}) %collective-permute-start.5) | collective-permute-done | bytes 262176 | tf_op jit(solution)/shard_map/ppermute | solution.py:19
  34.5 4.7 %collective-permute-start.9 = (f32[256,256]{1,0:T(8,128)S(1)}, f32[256,256]{1,0:T(8,128)S(1)}, u32[]{:S(2)}, u32[]{:S(2)}) collective-permute-start(f32[256,256]{1,0:T(8,128)S(1)} %fusion.44), channel_id=1, source_target_pairs={{0,30},{2,0},{4,2},{6,4},{8,6},{10,8},{12,10},{14,12},{16,14},{18,... | collective-permute-start | bytes 786440 | tf_op jit(solution)/shard_map/ppermute | solution.py:19
  41.0 1.6 %collective-permute-start.6 = (f32[384,256]{1,0:T(8,128)S(1)}, f32[384,256]{1,0:T(8,128)S(1)}, u32[]{:S(2)}, u32[]{:S(2)}) collective-permute-start(f32[384,256]{1,0:T(8,128)S(1)} %fusion.15), channel_id=1, source_target_pairs={{0,1},{1,0},{2,3},{3,2},{4,5},{5,4},{6,7},{7,6},{8,9},{9,8},{10,11... | collective-permute-start | bytes 1179656 | tf_op jit(solution)/shard_map/ppermute | solution.py:62
  43.1 0.5 fusion.42
  43.7 5.1 %collective-permute-done.6 = f32[384,256]{1,0:T(8,128)S(1)} collective-permute-done((f32[384,256]{1,0:T(8,128)S(1)}, f32[384,256]{1,0:T(8,128)S(1)}, u32[]{:S(2)}, u32[]{:S(2)}) %collective-permute-start.6) | collective-permute-done | bytes 393248 | tf_op jit(solution)/shard_map/ppermute | solution.py:62
  49.3 0.5 fusion.47
  50.9 1.6 %collective-permute-start.11 = (f32[256,256]{1,0:T(8,128)S(1)}, f32[256,256]{1,0:T(8,128)S(1)}, u32[]{:S(2)}, u32[]{:S(2)}) collective-permute-start(f32[256,256]{1,0:T(8,128)S(1)} %fusion.46), channel_id=1, source_target_pairs={{0,30},{2,0},{4,2},{6,4},{8,6},{10,8},{12,10},{14,12},{16,14},{18,... | collective-permute-start | bytes 786440 | tf_op jit(solution)/shard_map/ppermute | solution.py:19
  53.5 1.9 %collective-permute-start.10 = (f32[256,256]{1,0:T(8,128)S(1)}, f32[256,256]{1,0:T(8,128)S(1)}, u32[]{:S(2)}, u32[]{:S(2)}) collective-permute-start(f32[256,256]{1,0:T(8,128)S(1)} %fusion.45), channel_id=1, source_target_pairs={{0,30},{2,0},{4,2},{6,4},{8,6},{10,8},{12,10},{14,12},{16,14},{18,... | collective-permute-start | bytes 786440 | tf_op jit(solution)/shard_map/ppermute | solution.py:19
  56.4 3.1 %collective-permute-done.10 = f32[256,256]{1,0:T(8,128)S(1)} collective-permute-done((f32[256,256]{1,0:T(8,128)S(1)}, f32[256,256]{1,0:T(8,128)S(1)}, u32[]{:S(2)}, u32[]{:S(2)}) %collective-permute-start.10) | collective-permute-done | bytes 262176 | tf_op jit(solution)/shard_map/ppermute | solution.py:19
  59.9 0.5 fusion.48
  60.4 4.7 %collective-permute-start.13 = (f32[256,256]{1,0:T(8,128)S(1)}, f32[256,256]{1,0:T(8,128)S(1)}, u32[]{:S(2)}, u32[]{:S(2)}) collective-permute-start(f32[256,256]{1,0:T(8,128)S(1)} %fusion.48), channel_id=1, source_target_pairs={{0,30},{2,0},{4,2},{6,4},{8,6},{10,8},{12,10},{14,12},{16,14},{18,... | collective-permute-start | bytes 786440 | tf_op jit(solution)/shard_map/ppermute | solution.py:19
  68.1 6.6 %collective-permute-done.14 = f32[256,256]{1,0:T(8,128)S(1)} collective-permute-done((f32[256,256]{1,0:T(8,128)S(1)}, f32[256,256]{1,0:T(8,128)S(1)}, u32[]{:S(2)}, u32[]{:S(2)}) %collective-permute-start.14) | collective-permute-done | bytes 262176 | tf_op jit(solution)/shard_map/ppermute | solution.py:19
  75.0 0.5 fusion.52
  76.0 0.5 fusion.53
  77.0 0.5 fusion.51
  77.5 5.5 %collective-permute-start.17 = (f32[256,256]{1,0:T(8,128)S(1)}, f32[256,256]{1,0:T(8,128)S(1)}, u32[]{:S(2)}, u32[]{:S(2)}) collective-permute-start(f32[256,256]{1,0:T(8,128)S(1)} %fusion.51), channel_id=1, source_target_pairs={{0,10},{2,12},{4,14},{6,16},{8,18},{10,20},{12,22},{14,24},{16,26}... | collective-permute-start | bytes 786440 | tf_op jit(solution)/shard_map/ppermute | solution.py:19
  84.0 1.6 %collective-permute-start.16 = (f32[384,256]{1,0:T(8,128)S(1)}, f32[384,256]{1,0:T(8,128)S(1)}, u32[]{:S(2)}, u32[]{:S(2)}) collective-permute-start(f32[384,256]{1,0:T(8,128)S(1)} %fusion.33), channel_id=1, source_target_pairs={{0,1},{1,0},{2,3},{3,2},{4,5},{5,4},{6,7},{7,6},{8,9},{9,8},{10,11... | collective-permute-start | bytes 1179656 | tf_op jit(solution)/shard_map/ppermute | solution.py:62
  85.6 11.2 %collective-permute-done.18 = f32[256,256]{1,0:T(8,128)S(1)} collective-permute-done((f32[256,256]{1,0:T(8,128)S(1)}, f32[256,256]{1,0:T(8,128)S(1)}, u32[]{:S(2)}, u32[]{:S(2)}) %collective-permute-start.18) | collective-permute-done | bytes 262176 | tf_op jit(solution)/shard_map/ppermute | solution.py:19
  96.8 2.8 %collective-permute-done.19 = f32[256,256]{1,0:T(8,128)S(1)} collective-permute-done((f32[256,256]{1,0:T(8,128)S(1)}, f32[256,256]{1,0:T(8,128)S(1)}, u32[]{:S(2)}, u32[]{:S(2)}) %collective-permute-start.19) | collective-permute-done | bytes 262176 | tf_op jit(solution)/shard_map/ppermute | solution.py:19
  99.7 2.8 %collective-permute-done.17 = f32[256,256]{1,0:T(8,128)S(1)} collective-permute-done((f32[256,256]{1,0:T(8,128)S(1)}, f32[256,256]{1,0:T(8,128)S(1)}, u32[]{:S(2)}, u32[]{:S(2)}) %collective-permute-start.17) | collective-permute-done | bytes 262176 | tf_op jit(solution)/shard_map/ppermute | solution.py:19
  102.5 0.9 maximum_bitcast_fusion
  103.4 0.8 add_multiply_fusion
  (73 shorter events, 17.3 us)
Async XLA Ops:
  0.6 17.9 %slice-start = ((s8[7077888]{0:T(1024)(128)(4,1)}), s8[4194304]{0:T(1024)(128)(4,1)S(1)}, s32[]{:S(2)}) async-start(s8[7077888]{0:T(1024)(128)(4,1)} %bitcast.179), calls=%async_computation | async-start | bytes 8388608
  2.6 15.9 %slice-start.1 = ((s8[7077888]{0:T(1024)(128)(4,1)}), s8[2883584]{0:T(1024)(128)(4,1)S(1)}, s32[]{:S(2)}) async-start(s8[7077888]{0:T(1024)(128)(4,1)} %bitcast.179), calls=%async_computation.1 | async-start | bytes 5767168
  3.5 21.6 %collective-permute-start.2 = (f32[256,256]{1,0:T(8,128)S(1)}, f32[256,256]{1,0:T(8,128)S(1)}, u32[]{:S(2)}, u32[]{:S(2)}) collective-permute-start(f32[256,256]{1,0:T(8,128)S(1)} %fusion.38), channel_id=1, source_target_pairs={{0,30},{2,0},{4,2},{6,4},{8,6},{10,8},{12,10},{14,12},{16,14},{18,... | collective-permute-start | bytes 786440 | tf_op jit(solution)/shard_map/ppermute | solution.py:19
  9.9 8.6 %copy-start = (bf16[1,6,384,768]{3,2,1,0:T(8,128)(2,1)S(1)}, bf16[1,6,384,768]{3,2,1,0:T(8,128)(2,1)}, u32[]{:S(2)}) copy-start(bf16[1,6,384,768]{3,2,1,0:T(8,128)(2,1)} %w_in.1) | copy-start | bytes 10616836
  9.9 14.2 %collective-permute-start.1 = (f32[256,256]{1,0:T(8,128)S(1)}, f32[256,256]{1,0:T(8,128)S(1)}, u32[]{:S(2)}, u32[]{:S(2)}) collective-permute-start(f32[256,256]{1,0:T(8,128)S(1)} %fusion.37), channel_id=1, source_target_pairs={{0,30},{2,0},{4,2},{6,4},{8,6},{10,8},{12,10},{14,12},{16,14},{18,... | collective-permute-start | bytes 786440 | tf_op jit(solution)/shard_map/ppermute | solution.py:19
  11.6 7.0 %collective-permute-start = (f32[256,256]{1,0:T(8,128)S(1)}, f32[256,256]{1,0:T(8,128)S(1)}, u32[]{:S(2)}, u32[]{:S(2)}) collective-permute-start(f32[256,256]{1,0:T(8,128)S(1)} %fusion.36), channel_id=1, source_target_pairs={{0,30},{2,0},{4,2},{6,4},{8,6},{10,8},{12,10},{14,12},{16,14},{18,... | collective-permute-start | bytes 786440 | tf_op jit(solution)/shard_map/ppermute | solution.py:19
  19.4 20.8 %collective-permute-start.3 = (f32[256,256]{1,0:T(8,128)S(1)}, f32[256,256]{1,0:T(8,128)S(1)}, u32[]{:S(2)}, u32[]{:S(2)}) collective-permute-start(f32[256,256]{1,0:T(8,128)S(1)} %fusion.39), channel_id=1, source_target_pairs={{0,30},{2,0},{4,2},{6,4},{8,6},{10,8},{12,10},{14,12},{16,14},{18,... | collective-permute-start | bytes 786440 | tf_op jit(solution)/shard_map/ppermute | solution.py:19
  25.0 14.2 %collective-permute-start.4 = (f32[256,256]{1,0:T(8,128)S(1)}, f32[256,256]{1,0:T(8,128)S(1)}, u32[]{:S(2)}, u32[]{:S(2)}) collective-permute-start(f32[256,256]{1,0:T(8,128)S(1)} %fusion.40), channel_id=1, source_target_pairs={{0,30},{2,0},{4,2},{6,4},{8,6},{10,8},{12,10},{14,12},{16,14},{18,... | collective-permute-start | bytes 786440 | tf_op jit(solution)/shard_map/ppermute | solution.py:19
  26.0 7.6 %collective-permute-start.5 = (f32[256,256]{1,0:T(8,128)S(1)}, f32[256,256]{1,0:T(8,128)S(1)}, u32[]{:S(2)}, u32[]{:S(2)}) collective-permute-start(f32[256,256]{1,0:T(8,128)S(1)} %fusion.41), channel_id=1, source_target_pairs={{0,30},{2,0},{4,2},{6,4},{8,6},{10,8},{12,10},{14,12},{16,14},{18,... | collective-permute-start | bytes 786440 | tf_op jit(solution)/shard_map/ppermute | solution.py:19
  34.5 14.4 %collective-permute-start.9 = (f32[256,256]{1,0:T(8,128)S(1)}, f32[256,256]{1,0:T(8,128)S(1)}, u32[]{:S(2)}, u32[]{:S(2)}) collective-permute-start(f32[256,256]{1,0:T(8,128)S(1)} %fusion.44), channel_id=1, source_target_pairs={{0,30},{2,0},{4,2},{6,4},{8,6},{10,8},{12,10},{14,12},{16,14},{18,... | collective-permute-start | bytes 786440 | tf_op jit(solution)/shard_map/ppermute | solution.py:19
  41.0 7.8 %collective-permute-start.6 = (f32[384,256]{1,0:T(8,128)S(1)}, f32[384,256]{1,0:T(8,128)S(1)}, u32[]{:S(2)}, u32[]{:S(2)}) collective-permute-start(f32[384,256]{1,0:T(8,128)S(1)} %fusion.15), channel_id=1, source_target_pairs={{0,1},{1,0},{2,3},{3,2},{4,5},{5,4},{6,7},{7,6},{8,9},{9,8},{10,11... | collective-permute-start | bytes 1179656 | tf_op jit(solution)/shard_map/ppermute | solution.py:62
  43.1 7.0 %collective-permute-start.8 = (f32[256,256]{1,0:T(8,128)S(1)}, f32[256,256]{1,0:T(8,128)S(1)}, u32[]{:S(2)}, u32[]{:S(2)}) collective-permute-start(f32[256,256]{1,0:T(8,128)S(1)} %fusion.43), channel_id=1, source_target_pairs={{0,30},{2,0},{4,2},{6,4},{8,6},{10,8},{12,10},{14,12},{16,14},{18,... | collective-permute-start | bytes 786440 | tf_op jit(solution)/shard_map/ppermute | solution.py:19
  43.7 8.9 %collective-permute-start.7 = (f32[256,256]{1,0:T(8,128)S(1)}, f32[256,256]{1,0:T(8,128)S(1)}, u32[]{:S(2)}, u32[]{:S(2)}) collective-permute-start(f32[256,256]{1,0:T(8,128)S(1)} %fusion.42), channel_id=1, source_target_pairs={{0,30},{2,0},{4,2},{6,4},{8,6},{10,8},{12,10},{14,12},{16,14},{18,... | collective-permute-start | bytes 786440 | tf_op jit(solution)/shard_map/ppermute | solution.py:19
  49.8 15.3 %collective-permute-start.12 = (f32[256,256]{1,0:T(8,128)S(1)}, f32[256,256]{1,0:T(8,128)S(1)}, u32[]{:S(2)}, u32[]{:S(2)}) collective-permute-start(f32[256,256]{1,0:T(8,128)S(1)} %fusion.47), channel_id=1, source_target_pairs={{0,30},{2,0},{4,2},{6,4},{8,6},{10,8},{12,10},{14,12},{16,14},{18,... | collective-permute-start | bytes 786440 | tf_op jit(solution)/shard_map/ppermute | solution.py:19
  50.9 15.1 %collective-permute-start.11 = (f32[256,256]{1,0:T(8,128)S(1)}, f32[256,256]{1,0:T(8,128)S(1)}, u32[]{:S(2)}, u32[]{:S(2)}) collective-permute-start(f32[256,256]{1,0:T(8,128)S(1)} %fusion.46), channel_id=1, source_target_pairs={{0,30},{2,0},{4,2},{6,4},{8,6},{10,8},{12,10},{14,12},{16,14},{18,... | collective-permute-start | bytes 786440 | tf_op jit(solution)/shard_map/ppermute | solution.py:19
  53.5 6.1 %collective-permute-start.10 = (f32[256,256]{1,0:T(8,128)S(1)}, f32[256,256]{1,0:T(8,128)S(1)}, u32[]{:S(2)}, u32[]{:S(2)}) collective-permute-start(f32[256,256]{1,0:T(8,128)S(1)} %fusion.45), channel_id=1, source_target_pairs={{0,30},{2,0},{4,2},{6,4},{8,6},{10,8},{12,10},{14,12},{16,14},{18,... | collective-permute-start | bytes 786440 | tf_op jit(solution)/shard_map/ppermute | solution.py:19
  60.4 16.2 %collective-permute-start.13 = (f32[256,256]{1,0:T(8,128)S(1)}, f32[256,256]{1,0:T(8,128)S(1)}, u32[]{:S(2)}, u32[]{:S(2)}) collective-permute-start(f32[256,256]{1,0:T(8,128)S(1)} %fusion.48), channel_id=1, source_target_pairs={{0,30},{2,0},{4,2},{6,4},{8,6},{10,8},{12,10},{14,12},{16,14},{18,... | collective-permute-start | bytes 786440 | tf_op jit(solution)/shard_map/ppermute | solution.py:19
  66.0 9.6 %collective-permute-start.15 = (f32[256,256]{1,0:T(8,128)S(1)}, f32[256,256]{1,0:T(8,128)S(1)}, u32[]{:S(2)}, u32[]{:S(2)}) collective-permute-start(f32[256,256]{1,0:T(8,128)S(1)} %fusion.50), channel_id=1, source_target_pairs={{0,30},{2,0},{4,2},{6,4},{8,6},{10,8},{12,10},{14,12},{16,14},{18,... | collective-permute-start | bytes 786440 | tf_op jit(solution)/shard_map/ppermute | solution.py:19
  67.0 7.7 %collective-permute-start.14 = (f32[256,256]{1,0:T(8,128)S(1)}, f32[256,256]{1,0:T(8,128)S(1)}, u32[]{:S(2)}, u32[]{:S(2)}) collective-permute-start(f32[256,256]{1,0:T(8,128)S(1)} %fusion.49), channel_id=1, source_target_pairs={{0,30},{2,0},{4,2},{6,4},{8,6},{10,8},{12,10},{14,12},{16,14},{18,... | collective-permute-start | bytes 786440 | tf_op jit(solution)/shard_map/ppermute | solution.py:19
  75.5 21.3 %collective-permute-start.18 = (f32[256,256]{1,0:T(8,128)S(1)}, f32[256,256]{1,0:T(8,128)S(1)}, u32[]{:S(2)}, u32[]{:S(2)}) collective-permute-start(f32[256,256]{1,0:T(8,128)S(1)} %fusion.52), channel_id=1, source_target_pairs={{0,10},{2,12},{4,14},{6,16},{8,18},{10,20},{12,22},{14,24},{16,26}... | collective-permute-start | bytes 786440 | tf_op jit(solution)/shard_map/ppermute | solution.py:19
  76.5 23.1 %collective-permute-start.19 = (f32[256,256]{1,0:T(8,128)S(1)}, f32[256,256]{1,0:T(8,128)S(1)}, u32[]{:S(2)}, u32[]{:S(2)}) collective-permute-start(f32[256,256]{1,0:T(8,128)S(1)} %fusion.53), channel_id=1, source_target_pairs={{0,10},{2,12},{4,14},{6,16},{8,18},{10,20},{12,22},{14,24},{16,26}... | collective-permute-start | bytes 786440 | tf_op jit(solution)/shard_map/ppermute | solution.py:19
  77.5 25.0 %collective-permute-start.17 = (f32[256,256]{1,0:T(8,128)S(1)}, f32[256,256]{1,0:T(8,128)S(1)}, u32[]{:S(2)}, u32[]{:S(2)}) collective-permute-start(f32[256,256]{1,0:T(8,128)S(1)} %fusion.51), channel_id=1, source_target_pairs={{0,10},{2,12},{4,14},{6,16},{8,18},{10,20},{12,22},{14,24},{16,26}... | collective-permute-start | bytes 786440 | tf_op jit(solution)/shard_map/ppermute | solution.py:19
  84.0 19.4 %collective-permute-start.16 = (f32[384,256]{1,0:T(8,128)S(1)}, f32[384,256]{1,0:T(8,128)S(1)}, u32[]{:S(2)}, u32[]{:S(2)}) collective-permute-start(f32[384,256]{1,0:T(8,128)S(1)} %fusion.33), channel_id=1, source_target_pairs={{0,1},{1,0},{2,3},{3,2},{4,5},{5,4},{6,7},{7,6},{8,9},{9,8},{10,11... | collective-permute-start | bytes 1179656 | tf_op jit(solution)/shard_map/ppermute | solution.py:62

commit v5 on v4

--- a/solution.py
+++ b/solution.py
@@ -9,6 +9,8 @@
 OUTER = 2
 STRATA = 3
 PIECES = 3
+LAYER = 4
+SPLIT_ROUTE = (0,)
 
 
 step_rate = 0.002
@@ -17,6 +19,16 @@
 def from_behind(array, axis, by):
     peers = lax.axis_size(axis)
     return lax.ppermute(array, axis, [(i, (i + by) % peers) for i in range(peers)])
+
+
+def home(array, by, split):
+    peers = lax.axis_size("users")
+    if not split or peers % LAYER:
+        return from_behind(array, "users", by)
+    across = [(i, (i + (i % LAYER + by) // LAYER * LAYER) % peers) for i in range(peers)]
+    within = [(i, i // LAYER * LAYER + (i + by) % LAYER) for i in range(peers)]
+    array = lax.ppermute(array, "users", across)
+    return lax.ppermute(array, "users", within)
 
 
 def dot(lhs, rhs, dims):
@@ -88,8 +100,12 @@
                 predicted = dot(current, held, ((1,), (1,)))
                 residual = weights.astype(jnp.float32) * (tile - predicted)
                 moved = held + step_rate * dot(residual, current, ((0,), (0,)))
-                gained = gained + step_rate * dot(residual, held, ((1,), (0,)))
-                pieces[i] = from_behind(moved, "users", last if stratum == last else -1)
+                gained = step_rate * dot(residual, held, ((1,), (0,))) + gained
+                gained = lax.optimization_barrier(gained)
+                if stratum == last:
+                    pieces[i] = home(moved, last, i in SPLIT_ROUTE)
+                else:
+                    pieces[i] = from_behind(moved, "users", -1)
             current = gained
         factors_u = combine(current)
     return (factors_u, jnp.concatenate(pieces, axis=0)[None])

time: 104 us -> 103 us (level)
  starting transfers between devices: 33.3 us -> 28.3 us
  waiting for transfers between devices: 44.1 us -> 48.1 us
    ppermute x0 -> x2, waiting for transfers between devices: none -> 8.3 us  [the longest x1 8.3 us: home(): array = lax.ppermute(array, 'users', across)]
    ppermute x18 -> x17, waiting for transfers between devices: 39 us -> 34.3 us  [from_behind(): lax.ppermute(array, axis, [(i, (i + by) % peers) for i in range(peers)])]
    ppermute x18 -> x17, starting transfers between devices: 30.1 us -> 25.9 us  [from_behind(): lax.ppermute(array, axis, [(i, (i + by) % peers) for i in range(peers)])]
  transfers between devices with their start and end apart: 20 -> 21, of which waited for: 8 -> 10; matrix products, arithmetic and copies ran while one was open for 21% -> 21% of each run, Pallas kernels for 0% -> 0%
where the time goes in v5:
time: 103 us
  waiting for transfers between devices  48.1 us (47%)
  starting transfers between devices  28.3 us (27%)
  matrix products  21.9 us (21%)
  Pallas kernels  1.96 us (2%)
  other arithmetic  1.78 us (2%)
  between operations  1.19 us (1%)
    ppermute x17, waiting for transfers between devices, from_behind(): lax.ppermute(array, axis, [(i, (i + by) % peers) for i in range(peers)])  34.3 us
    ppermute x17, starting transfers between devices, from_behind(): lax.ppermute(array, axis, [(i, (i + by) % peers) for i in range(peers)])  25.9 us
    dot_general x54, matrix products, dot(): lax.dot_general(lhs, rhs, (dims, ((), ())), precision=lax.Precision.HIGH,...  21.9 us
    ppermute x1, waiting for transfers between devices, home(): array = lax.ppermute(array, 'users', across)  8.3 us
    ppermute x2, waiting for transfers between devices, combine(): partner = lax.ppermute(summed, 'period', partners)  5.47 us
    ppermute x2, starting transfers between devices, combine(): partner = lax.ppermute(summed, 'period', partners)  2.35 us
  transfers between devices with their start and end apart: 21, of which 10 were waited for; matrix products, arithmetic and copies ran while one was open for 21% of the time, Pallas kernels for 0%

profile of v5, /device:TPU:0, one launch (start us, length us, event | category | flops | bytes accessed | tf_op | source)
XLA Modules:
  0.0 103.3 jit_solution(15807821521368795667)
XLA Ops:
  0.6 2.0 %shard_map.59 = (f32[384,256]{1,0:T(8,128)S(1)}, f32[768,256]{1,0:T(8,128)S(1)}, f32[384,768]{1,0:T(8,128)S(1)}, bf16[384,768]{1,0:T(8,128)(2,1)S(1)}) custom-call(f32[384,256]{1,0:T(8,128)} %c_in.1, f32[1,768,256]{2,1,0:T(8,128)} %v_in.1, f32[1,6,384,768]{3,2,1,0:T(8,128)} %r_in.1, bf16[1,6,384,768]{3,2,1,0:T(8,128)(2,1)} %w_in.1), custom_call_target="tpu_custom_call" | custom-call | tf_op jit(solution)/shard_map/pallas_call | solution.py:56
  3.0 0.5 fusion.38
  3.5 5.5 %collective-permute-start.2 = (f32[256,256]{1,0:T(8,128)S(1)}, f32[256,256]{1,0:T(8,128)S(1)}, u32[]{:S(2)}, u32[]{:S(2)}) collective-permute-start(f32[256,256]{1,0:T(8,128)S(1)} %fusion.38), channel_id=1, source_target_pairs={{0,30},{2,0},{4,2},{6,4},{8,6},{10,8},{12,10},{14,12},{16,14},{18,... | collective-permute-start | bytes 786440 | tf_op jit(solution)/shard_map/ppermute | solution.py:21
  9.4 0.5 fusion.36
  9.9 0.7 collective-permute-start
  12.7 5.9 %collective-permute-done.1 = f32[256,256]{1,0:T(8,128)S(1)} collective-permute-done((f32[256,256]{1,0:T(8,128)S(1)}, f32[256,256]{1,0:T(8,128)S(1)}, u32[]{:S(2)}, u32[]{:S(2)}) %collective-permute-start.1) | collective-permute-done | bytes 262176 | tf_op jit(solution)/shard_map/ppermute | solution.py:21
  18.9 0.5 fusion.40
  19.4 4.7 %collective-permute-start.4 = (f32[256,256]{1,0:T(8,128)S(1)}, f32[256,256]{1,0:T(8,128)S(1)}, u32[]{:S(2)}, u32[]{:S(2)}) collective-permute-start(f32[256,256]{1,0:T(8,128)S(1)} %fusion.40), channel_id=1, source_target_pairs={{0,30},{2,0},{4,2},{6,4},{8,6},{10,8},{12,10},{14,12},{16,14},{18,... | collective-permute-start | bytes 786440 | tf_op jit(solution)/shard_map/ppermute | solution.py:21
  24.5 0.5 fusion.39
  25.8 0.5 fusion.41
  27.1 6.5 %collective-permute-done.5 = f32[256,256]{1,0:T(8,128)S(1)} collective-permute-done((f32[256,256]{1,0:T(8,128)S(1)}, f32[256,256]{1,0:T(8,128)S(1)}, u32[]{:S(2)}, u32[]{:S(2)}) %collective-permute-start.5) | collective-permute-done | bytes 262176 | tf_op jit(solution)/shard_map/ppermute | solution.py:21
  34.3 0.5 fusion.44
  34.9 4.7 %collective-permute-start.9 = (f32[256,256]{1,0:T(8,128)S(1)}, f32[256,256]{1,0:T(8,128)S(1)}, u32[]{:S(2)}, u32[]{:S(2)}) collective-permute-start(f32[256,256]{1,0:T(8,128)S(1)} %fusion.44), channel_id=1, source_target_pairs={{0,30},{2,0},{4,2},{6,4},{8,6},{10,8},{12,10},{14,12},{16,14},{18,... | collective-permute-start | bytes 786440 | tf_op jit(solution)/shard_map/ppermute | solution.py:21
  41.0 1.6 %collective-permute-start.6 = (f32[384,256]{1,0:T(8,128)S(1)}, f32[384,256]{1,0:T(8,128)S(1)}, u32[]{:S(2)}, u32[]{:S(2)}) collective-permute-start(f32[384,256]{1,0:T(8,128)S(1)} %fusion.13), channel_id=1, source_target_pairs={{0,1},{1,0},{2,3},{3,2},{4,5},{5,4},{6,7},{7,6},{8,9},{9,8},{10,11... | collective-permute-start | bytes 1179656 | tf_op jit(solution)/shard_map/ppermute | solution.py:74
  43.1 0.5 fusion.42
  43.9 4.9 %collective-permute-done.6 = f32[384,256]{1,0:T(8,128)S(1)} collective-permute-done((f32[384,256]{1,0:T(8,128)S(1)}, f32[384,256]{1,0:T(8,128)S(1)}, u32[]{:S(2)}, u32[]{:S(2)}) %collective-permute-start.6) | collective-permute-done | bytes 393248 | tf_op jit(solution)/shard_map/ppermute | solution.py:74
  49.6 0.5 fusion.47
  51.1 4.3 %collective-permute-start.10 = (f32[256,256]{1,0:T(8,128)S(1)}, f32[256,256]{1,0:T(8,128)S(1)}, u32[]{:S(2)}, u32[]{:S(2)}) collective-permute-start(f32[256,256]{1,0:T(8,128)S(1)} %fusion.45), channel_id=1, source_target_pairs={{0,30},{2,0},{4,2},{6,4},{8,6},{10,8},{12,10},{14,12},{16,14},{18,... | collective-permute-start | bytes 786440 | tf_op jit(solution)/shard_map/ppermute | solution.py:21
  57.1 2.2 %collective-permute-done.10 = f32[256,256]{1,0:T(8,128)S(1)} collective-permute-done((f32[256,256]{1,0:T(8,128)S(1)}, f32[256,256]{1,0:T(8,128)S(1)}, u32[]{:S(2)}, u32[]{:S(2)}) %collective-permute-start.10) | collective-permute-done | bytes 262176 | tf_op jit(solution)/shard_map/ppermute | solution.py:21
  59.7 0.5 fusion.48
  60.2 4.7 %collective-permute-start.13 = (f32[256,256]{1,0:T(8,128)S(1)}, f32[256,256]{1,0:T(8,128)S(1)}, u32[]{:S(2)}, u32[]{:S(2)}) collective-permute-start(f32[256,256]{1,0:T(8,128)S(1)} %fusion.48), channel_id=1, source_target_pairs={{0,30},{2,0},{4,2},{6,4},{8,6},{10,8},{12,10},{14,12},{16,14},{18,... | collective-permute-start | bytes 786440 | tf_op jit(solution)/shard_map/ppermute | solution.py:21
  67.7 0.6 collective-permute-start.14
  68.3 3.2 %collective-permute-done.15 = f32[256,256]{1,0:T(8,128)S(1)} collective-permute-done((f32[256,256]{1,0:T(8,128)S(1)}, f32[256,256]{1,0:T(8,128)S(1)}, u32[]{:S(2)}, u32[]{:S(2)}) %collective-permute-start.15) | collective-permute-done | bytes 262176 | tf_op jit(solution)/shard_map/ppermute | solution.py:21
  72.3 2.1 %collective-permute-done.14 = f32[256,256]{1,0:T(8,128)S(1)} collective-permute-done((f32[256,256]{1,0:T(8,128)S(1)}, f32[256,256]{1,0:T(8,128)S(1)}, u32[]{:S(2)}, u32[]{:S(2)}) %collective-permute-start.14) | collective-permute-done | bytes 262176 | tf_op jit(solution)/shard_map/ppermute | solution.py:21
  76.4 0.8 collective-permute-start.16
  77.8 0.5 fusion.53
  78.4 8.3 %collective-permute-done.17 = f32[256,256]{1,0:T(8,128)S(1)} collective-permute-done((f32[256,256]{1,0:T(8,128)S(1)}, f32[256,256]{1,0:T(8,128)S(1)}, u32[]{:S(2)}, u32[]{:S(2)}) %collective-permute-start.17) | collective-permute-done | bytes 262176 | tf_op jit(solution)/shard_map/ppermute | solution.py:30
  86.7 0.5 collective-permute-done.16
  87.2 0.8 add_multiply_fusion
  88.0 11.5 %collective-permute-done.19 = f32[256,256]{1,0:T(8,128)S(1)} collective-permute-done((f32[256,256]{1,0:T(8,128)S(1)}, f32[256,256]{1,0:T(8,128)S(1)}, u32[]{:S(2)}, u32[]{:S(2)}) %collective-permute-start.19) | collective-permute-done | bytes 262176 | tf_op jit(solution)/shard_map/ppermute | solution.py:21
  99.6 2.8 %collective-permute-done.20 = f32[256,256]{1,0:T(8,128)S(1)} collective-permute-done((f32[256,256]{1,0:T(8,128)S(1)}, f32[256,256]{1,0:T(8,128)S(1)}, u32[]{:S(2)}, u32[]{:S(2)}) %collective-permute-start.20) | collective-permute-done | bytes 262176 | tf_op jit(solution)/shard_map/ppermute | solution.py:21
  102.4 0.9 maximum_bitcast_fusion
  (75 shorter events, 17.9 us)
Async XLA Ops:
  0.6 17.9 %slice-start = ((s8[7077888]{0:T(1024)(128)(4,1)}), s8[4194304]{0:T(1024)(128)(4,1)S(1)}, s32[]{:S(2)}) async-start(s8[7077888]{0:T(1024)(128)(4,1)} %bitcast.179), calls=%async_computation | async-start | bytes 8388608
  2.6 15.9 %slice-start.1 = ((s8[7077888]{0:T(1024)(128)(4,1)}), s8[2883584]{0:T(1024)(128)(4,1)S(1)}, s32[]{:S(2)}) async-start(s8[7077888]{0:T(1024)(128)(4,1)} %bitcast.179), calls=%async_computation.1 | async-start | bytes 5767168
  3.5 21.6 %collective-permute-start.2 = (f32[256,256]{1,0:T(8,128)S(1)}, f32[256,256]{1,0:T(8,128)S(1)}, u32[]{:S(2)}, u32[]{:S(2)}) collective-permute-start(f32[256,256]{1,0:T(8,128)S(1)} %fusion.38), channel_id=1, source_target_pairs={{0,30},{2,0},{4,2},{6,4},{8,6},{10,8},{12,10},{14,12},{16,14},{18,... | collective-permute-start | bytes 786440 | tf_op jit(solution)/shard_map/ppermute | solution.py:21
  9.9 8.6 %copy-start = (bf16[1,6,384,768]{3,2,1,0:T(8,128)(2,1)S(1)}, bf16[1,6,384,768]{3,2,1,0:T(8,128)(2,1)}, u32[]{:S(2)}) copy-start(bf16[1,6,384,768]{3,2,1,0:T(8,128)(2,1)} %w_in.1) | copy-start | bytes 10616836
  9.9 14.2 %collective-permute-start = (f32[256,256]{1,0:T(8,128)S(1)}, f32[256,256]{1,0:T(8,128)S(1)}, u32[]{:S(2)}, u32[]{:S(2)}) collective-permute-start(f32[256,256]{1,0:T(8,128)S(1)} %fusion.36), channel_id=1, source_target_pairs={{0,30},{2,0},{4,2},{6,4},{8,6},{10,8},{12,10},{14,12},{16,14},{18,... | collective-permute-start | bytes 786440 | tf_op jit(solution)/shard_map/ppermute | solution.py:21
  11.6 7.0 %collective-permute-start.1 = (f32[256,256]{1,0:T(8,128)S(1)}, f32[256,256]{1,0:T(8,128)S(1)}, u32[]{:S(2)}, u32[]{:S(2)}) collective-permute-start(f32[256,256]{1,0:T(8,128)S(1)} %fusion.37), channel_id=1, source_target_pairs={{0,30},{2,0},{4,2},{6,4},{8,6},{10,8},{12,10},{14,12},{16,14},{18,... | collective-permute-start | bytes 786440 | tf_op jit(solution)/shard_map/ppermute | solution.py:21
  19.4 20.1 %collective-permute-start.4 = (f32[256,256]{1,0:T(8,128)S(1)}, f32[256,256]{1,0:T(8,128)S(1)}, u32[]{:S(2)}, u32[]{:S(2)}) collective-permute-start(f32[256,256]{1,0:T(8,128)S(1)} %fusion.40), channel_id=1, source_target_pairs={{0,30},{2,0},{4,2},{6,4},{8,6},{10,8},{12,10},{14,12},{16,14},{18,... | collective-permute-start | bytes 786440 | tf_op jit(solution)/shard_map/ppermute | solution.py:21
  25.0 15.2 %collective-permute-start.3 = (f32[256,256]{1,0:T(8,128)S(1)}, f32[256,256]{1,0:T(8,128)S(1)}, u32[]{:S(2)}, u32[]{:S(2)}) collective-permute-start(f32[256,256]{1,0:T(8,128)S(1)} %fusion.39), channel_id=1, source_target_pairs={{0,30},{2,0},{4,2},{6,4},{8,6},{10,8},{12,10},{14,12},{16,14},{18,... | collective-permute-start | bytes 786440 | tf_op jit(solution)/shard_map/ppermute | solution.py:21
  26.3 7.3 %collective-permute-start.5 = (f32[256,256]{1,0:T(8,128)S(1)}, f32[256,256]{1,0:T(8,128)S(1)}, u32[]{:S(2)}, u32[]{:S(2)}) collective-permute-start(f32[256,256]{1,0:T(8,128)S(1)} %fusion.41), channel_id=1, source_target_pairs={{0,30},{2,0},{4,2},{6,4},{8,6},{10,8},{12,10},{14,12},{16,14},{18,... | collective-permute-start | bytes 786440 | tf_op jit(solution)/shard_map/ppermute | solution.py:21
  34.9 14.0 %collective-permute-start.9 = (f32[256,256]{1,0:T(8,128)S(1)}, f32[256,256]{1,0:T(8,128)S(1)}, u32[]{:S(2)}, u32[]{:S(2)}) collective-permute-start(f32[256,256]{1,0:T(8,128)S(1)} %fusion.44), channel_id=1, source_target_pairs={{0,30},{2,0},{4,2},{6,4},{8,6},{10,8},{12,10},{14,12},{16,14},{18,... | collective-permute-start | bytes 786440 | tf_op jit(solution)/shard_map/ppermute | solution.py:21
  41.0 7.8 %collective-permute-start.6 = (f32[384,256]{1,0:T(8,128)S(1)}, f32[384,256]{1,0:T(8,128)S(1)}, u32[]{:S(2)}, u32[]{:S(2)}) collective-permute-start(f32[384,256]{1,0:T(8,128)S(1)} %fusion.13), channel_id=1, source_target_pairs={{0,1},{1,0},{2,3},{3,2},{4,5},{5,4},{6,7},{7,6},{8,9},{9,8},{10,11... | collective-permute-start | bytes 1179656 | tf_op jit(solution)/shard_map/ppermute | solution.py:74
  43.1 12.3 %collective-permute-start.8 = (f32[256,256]{1,0:T(8,128)S(1)}, f32[256,256]{1,0:T(8,128)S(1)}, u32[]{:S(2)}, u32[]{:S(2)}) collective-permute-start(f32[256,256]{1,0:T(8,128)S(1)} %fusion.43), channel_id=1, source_target_pairs={{0,30},{2,0},{4,2},{6,4},{8,6},{10,8},{12,10},{14,12},{16,14},{18,... | collective-permute-start | bytes 786440 | tf_op jit(solution)/shard_map/ppermute | solution.py:21
  43.7 6.5 %collective-permute-start.7 = (f32[256,256]{1,0:T(8,128)S(1)}, f32[256,256]{1,0:T(8,128)S(1)}, u32[]{:S(2)}, u32[]{:S(2)}) collective-permute-start(f32[256,256]{1,0:T(8,128)S(1)} %fusion.42), channel_id=1, source_target_pairs={{0,30},{2,0},{4,2},{6,4},{8,6},{10,8},{12,10},{14,12},{16,14},{18,... | collective-permute-start | bytes 786440 | tf_op jit(solution)/shard_map/ppermute | solution.py:21
  50.1 14.7 %collective-permute-start.12 = (f32[256,256]{1,0:T(8,128)S(1)}, f32[256,256]{1,0:T(8,128)S(1)}, u32[]{:S(2)}, u32[]{:S(2)}) collective-permute-start(f32[256,256]{1,0:T(8,128)S(1)} %fusion.47), channel_id=1, source_target_pairs={{0,30},{2,0},{4,2},{6,4},{8,6},{10,8},{12,10},{14,12},{16,14},{18,... | collective-permute-start | bytes 786440 | tf_op jit(solution)/shard_map/ppermute | solution.py:21
  51.1 8.2 %collective-permute-start.10 = (f32[256,256]{1,0:T(8,128)S(1)}, f32[256,256]{1,0:T(8,128)S(1)}, u32[]{:S(2)}, u32[]{:S(2)}) collective-permute-start(f32[256,256]{1,0:T(8,128)S(1)} %fusion.45), channel_id=1, source_target_pairs={{0,30},{2,0},{4,2},{6,4},{8,6},{10,8},{12,10},{14,12},{16,14},{18,... | collective-permute-start | bytes 786440 | tf_op jit(solution)/shard_map/ppermute | solution.py:21
  56.6 9.5 %collective-permute-start.11 = (f32[256,256]{1,0:T(8,128)S(1)}, f32[256,256]{1,0:T(8,128)S(1)}, u32[]{:S(2)}, u32[]{:S(2)}) collective-permute-start(f32[256,256]{1,0:T(8,128)S(1)} %fusion.46), channel_id=1, source_target_pairs={{0,30},{2,0},{4,2},{6,4},{8,6},{10,8},{12,10},{14,12},{16,14},{18,... | collective-permute-start | bytes 786440 | tf_op jit(solution)/shard_map/ppermute | solution.py:21
  60.2 15.5 %collective-permute-start.13 = (f32[256,256]{1,0:T(8,128)S(1)}, f32[256,256]{1,0:T(8,128)S(1)}, u32[]{:S(2)}, u32[]{:S(2)}) collective-permute-start(f32[256,256]{1,0:T(8,128)S(1)} %fusion.48), channel_id=1, source_target_pairs={{0,30},{2,0},{4,2},{6,4},{8,6},{10,8},{12,10},{14,12},{16,14},{18,... | collective-permute-start | bytes 786440 | tf_op jit(solution)/shard_map/ppermute | solution.py:21
  66.1 5.5 %collective-permute-start.15 = (f32[256,256]{1,0:T(8,128)S(1)}, f32[256,256]{1,0:T(8,128)S(1)}, u32[]{:S(2)}, u32[]{:S(2)}) collective-permute-start(f32[256,256]{1,0:T(8,128)S(1)} %fusion.50), channel_id=1, source_target_pairs={{0,30},{2,0},{4,2},{6,4},{8,6},{10,8},{12,10},{14,12},{16,14},{18,... | collective-permute-start | bytes 786440 | tf_op jit(solution)/shard_map/ppermute | solution.py:21
  67.7 6.6 %collective-permute-start.14 = (f32[256,256]{1,0:T(8,128)S(1)}, f32[256,256]{1,0:T(8,128)S(1)}, u32[]{:S(2)}, u32[]{:S(2)}) collective-permute-start(f32[256,256]{1,0:T(8,128)S(1)} %fusion.49), channel_id=1, source_target_pairs={{0,30},{2,0},{4,2},{6,4},{8,6},{10,8},{12,10},{14,12},{16,14},{18,... | collective-permute-start | bytes 786440 | tf_op jit(solution)/shard_map/ppermute | solution.py:21
  75.6 11.0 %collective-permute-start.17 = (f32[256,256]{1,0:T(8,128)S(1)}, f32[256,256]{1,0:T(8,128)S(1)}, u32[]{:S(2)}, u32[]{:S(2)}) collective-permute-start(f32[256,256]{1,0:T(8,128)S(1)} %fusion.51), channel_id=1, source_target_pairs={{0,8},{2,10},{4,12},{6,22},{8,16},{10,18},{12,20},{14,30},{16,24},... | collective-permute-start | bytes 786440 | tf_op jit(solution)/shard_map/ppermute | solution.py:30
  76.4 10.8 %collective-permute-start.16 = (f32[384,256]{1,0:T(8,128)S(1)}, f32[384,256]{1,0:T(8,128)S(1)}, u32[]{:S(2)}, u32[]{:S(2)}) collective-permute-start(f32[384,256]{1,0:T(8,128)S(1)} %fusion.31), channel_id=1, source_target_pairs={{0,1},{1,0},{2,3},{3,2},{4,5},{5,4},{6,7},{7,6},{8,9},{9,8},{10,11... | collective-permute-start | bytes 1179656 | tf_op jit(solution)/shard_map/ppermute | solution.py:74
  77.7 21.8 %collective-permute-start.19 = (f32[256,256]{1,0:T(8,128)S(1)}, f32[256,256]{1,0:T(8,128)S(1)}, u32[]{:S(2)}, u32[]{:S(2)}) collective-permute-start(f32[256,256]{1,0:T(8,128)S(1)} %fusion.52), channel_id=1, source_target_pairs={{0,10},{2,12},{4,14},{6,16},{8,18},{10,20},{12,22},{14,24},{16,26}... | collective-permute-start | bytes 786440 | tf_op jit(solution)/shard_map/ppermute | solution.py:21
  78.3 24.1 %collective-permute-start.20 = (f32[256,256]{1,0:T(8,128)S(1)}, f32[256,256]{1,0:T(8,128)S(1)}, u32[]{:S(2)}, u32[]{:S(2)}) collective-permute-start(f32[256,256]{1,0:T(8,128)S(1)} %fusion.53), channel_id=1, source_target_pairs={{0,10},{2,12},{4,14},{6,16},{8,18},{10,20},{12,22},{14,24},{16,26}... | collective-permute-start | bytes 786440 | tf_op jit(solution)/shard_map/ppermute | solution.py:21
  86.7 15.7 %collective-permute-start.18 = (f32[256,256]{1,0:T(8,128)S(1)}, f32[256,256]{1,0:T(8,128)S(1)}, u32[]{:S(2)}, u32[]{:S(2)}) collective-permute-start(f32[256,256]{1,0:T(8,128)S(1)} %collective-permute-done.17), channel_id=1, source_target_pairs={{0,2},{2,4},{4,6},{6,0},{8,10},{10,12},{12,14},{14,8},{16,18},{18,... | collective-permute-start | bytes 786440 | tf_op jit(solution)/shard_map/ppermute | solution.py:31

commit v6 on v5

--- a/solution.py
+++ b/solution.py
@@ -1,3 +1,5 @@
+import functools
+
 import jax
 import jax.numpy as jnp
 from jax import lax
@@ -10,6 +12,7 @@
 STRATA = 3
 PIECES = 3
 LAYER = 4
+FIRST_LEG = (4, 4, 4, 8)
 SPLIT_ROUTE = (0,)
 
 
@@ -25,8 +28,9 @@
     peers = lax.axis_size("users")
     if not split or peers % LAYER:
         return from_behind(array, "users", by)
-    across = [(i, (i + (i % LAYER + by) // LAYER * LAYER) % peers) for i in range(peers)]
-    within = [(i, i // LAYER * LAYER + (i + by) % LAYER) for i in range(peers)]
+    legs = [FIRST_LEG[i % LAYER] for i in range(peers)]
+    across = [(i, (i + leg) % peers) for i, leg in enumerate(legs)]
+    within = [((i + leg) % peers, (i + by) % peers) for i, leg in enumerate(legs)]
     array = lax.ppermute(array, "users", across)
     return lax.ppermute(array, "users", within)
 
@@ -37,29 +41,68 @@
     )
 
 
-def load_kernel(c_in, v_in, r_in, w_in, c_out, v_out, r_out, w_out, sems):
+def halves(x):
+    high = x.astype(jnp.bfloat16)
+    return high, (x - high.astype(jnp.float32)).astype(jnp.bfloat16)
+
+
+def dot_of_halves(lhs, rhs, dims):
+    part = functools.partial(
+        lax.dot_general, dimension_numbers=(dims, ((), ())), preferred_element_type=jnp.float32
+    )
+    return part(lhs[0], rhs[0]) + (part(lhs[0], rhs[1]) + part(lhs[1], rhs[0]))
+
+
+def first_kernel(c_in, v_in, r_in, w_in, c, v, r, w, residual, moved, sems):
+    rows = moved.shape[0]
+    start, rest = pl.ds(0, rows), pl.ds(rows, v.shape[0] - rows)
     copies = [
-        pltpu.make_async_copy(c_in, c_out, sems.at[0]),
-        pltpu.make_async_copy(v_in.at[0], v_out, sems.at[1]),
-        pltpu.make_async_copy(r_in.at[0, 0], r_out, sems.at[2]),
-        pltpu.make_async_copy(w_in.at[0, 0], w_out, sems.at[3]),
+        pltpu.make_async_copy(source, target, sems.at[i])
+        for i, (source, target) in enumerate(
+            (
+                (c_in, c),
+                (v_in.at[0, start], v.at[start]),
+                (r_in.at[0, 0, :, start], r.at[:, start]),
+                (w_in.at[0, 0, :, start], w.at[:, start]),
+                (v_in.at[0, rest], v.at[rest]),
+                (r_in.at[0, 0, :, rest], r.at[:, rest]),
+                (w_in.at[0, 0, :, rest], w.at[:, rest]),
+            )
+        )
     ]
     for copy in copies:
         copy.start()
-    for copy in copies:
+    for copy in copies[:2]:
+        copy.wait()
+    c_halves = halves(c[...])
+    predicted = dot_of_halves(c_halves, halves(v[start]), ((1,), (1,)))
+    for copy in copies[2:4]:
+        copy.wait()
+    residual[...] = w[:, start].astype(jnp.float32) * (r[:, start] - predicted)
+    change = dot_of_halves(halves(residual[...]), c_halves, ((0,), (0,)))
+    moved[...] = v[start] + step_rate * change
+    for copy in copies[4:]:
         copy.wait()
 
 
-def load_first(user_factors, item_factors, ratings, observed):
+def first_piece(user_factors, item_factors, ratings, observed, rows):
     operands = (user_factors, item_factors, ratings, observed)
-    shapes = (user_factors.shape, item_factors.shape[1:], ratings.shape[2:], observed.shape[2:])
+    users, rank = user_factors.shape
+    outs = [
+        jax.ShapeDtypeStruct(user_factors.shape, user_factors.dtype),
+        jax.ShapeDtypeStruct(item_factors.shape[1:], item_factors.dtype),
+        jax.ShapeDtypeStruct(ratings.shape[2:], ratings.dtype),
+        jax.ShapeDtypeStruct(observed.shape[2:], observed.dtype),
+        jax.ShapeDtypeStruct((users, rows), jnp.float32),
+        jax.ShapeDtypeStruct((rows, rank), jnp.float32),
+    ]
     return pl.pallas_call(
-        load_kernel,
-        out_shape=tuple(jax.ShapeDtypeStruct(s, a.dtype) for s, a in zip(shapes, operands)),
+        first_kernel,
+        out_shape=tuple(outs),
         in_specs=[pl.BlockSpec(memory_space=pltpu.HBM)] * 4,
-        out_specs=(pl.BlockSpec(memory_space=pltpu.VMEM),) * 4,
-        scratch_shapes=[pltpu.SemaphoreType.DMA((4,))],
-        compiler_params=pltpu.CompilerParams(vmem_limit_bytes=8 << 20),
+        out_specs=(pl.BlockSpec(memory_space=pltpu.VMEM),) * len(outs),
+        scratch_shapes=[pltpu.SemaphoreType.DMA((7,))],
+        compiler_params=pltpu.CompilerParams(vmem_limit_bytes=16 << 20),
     )(*[pltpu.with_memory_space_constraint(a, pltpu.HBM) for a in operands])
 
 
@@ -78,11 +121,11 @@
 
 
 def on_device(ratings, observed, user_factors, item_factors):
-    factors_u, first_items, first_ratings, first_weights = load_first(
-        user_factors, item_factors, ratings, observed
-    )
     items = item_factors.shape[1]
     rows = items // PIECES
+    factors_u, first_items, first_ratings, first_weights, *first = first_piece(
+        user_factors, item_factors, ratings, observed, rows
+    )
     pieces = [first_items[i * rows : (i + 1) * rows] for i in range(PIECES)]
     last = OUTER * STRATA - 1
     for outer_step in range(OUTER):
@@ -97,9 +140,12 @@
                 else:
                     tile, weights = ratings[0, stratum, :, cols], observed[0, stratum, :, cols]
                 held = pieces[i]
-                predicted = dot(current, held, ((1,), (1,)))
-                residual = weights.astype(jnp.float32) * (tile - predicted)
-                moved = held + step_rate * dot(residual, current, ((0,), (0,)))
+                if stratum == 0 and i == 0:
+                    residual, moved = first
+                else:
+                    predicted = dot(current, held, ((1,), (1,)))
+                    residual = weights.astype(jnp.float32) * (tile - predicted)
+                    moved = held + step_rate * dot(residual, current, ((0,), (0,)))
                 gained = step_rate * dot(residual, held, ((1,), (0,))) + gained
                 gained = lax.optimization_barrier(gained)
                 if stratum == last:

time: 103 us -> 103 us (level)
    dot_general x54 -> x52, matrix products: 21.9 us -> 21.1 us  [dot(): lax.dot_general(lhs, rhs, (dims, ((), ())), precision=lax.Precision.HIGH,...]
where the time goes in v6:
time: 103 us
  waiting for transfers between devices  48.3 us (47%)
  starting transfers between devices  28.1 us (27%)
  matrix products  21.1 us (20%)
  Pallas kernels  2.34 us (2%)
  other arithmetic  1.78 us (2%)
  between operations  1.17 us (1%)
    ppermute x17, waiting for transfers between devices, from_behind(): lax.ppermute(array, axis, [(i, (i + by) % peers) for i in range(peers)])  34.3 us
    ppermute x17, starting transfers between devices, from_behind(): lax.ppermute(array, axis, [(i, (i + by) % peers) for i in range(peers)])  25.7 us
    dot_general x52, matrix products, dot(): lax.dot_general(lhs, rhs, (dims, ((), ())), precision=lax.Precision.HIGH,...  21.1 us
    ppermute x1, waiting for transfers between devices, home(): array = lax.ppermute(array, 'users', across)  8.31 us
    ppermute x2, waiting for transfers between devices, combine(): partner = lax.ppermute(summed, 'period', partners)  5.64 us
    pallas_call x1, Pallas kernels, first_piece(): pl.pallas_call(first_kernel, out_shape=tuple(outs), in_specs=[pl.BlockSpe...  2.34 us
    ppermute x2, starting transfers between devices, combine(): partner = lax.ppermute(summed, 'period', partners)  2.34 us
  transfers between devices with their start and end apart: 21, of which 10 were waited for; matrix products, arithmetic and copies ran while one was open for 21% of the time, Pallas kernels for 0%

profile of v6, /device:TPU:0, one launch (start us, length us, event | category | flops | bytes accessed | tf_op | source)
XLA Modules:
  0.0 102.8 jit_solution(17062622620802303929)
XLA Ops:
  0.6 2.3 %shard_map.59 = (f32[384,256]{1,0:T(8,128)S(1)}, f32[768,256]{1,0:T(8,128)S(1)}, f32[384,768]{1,0:T(8,128)S(1)}, bf16[384,768]{1,0:T(8,128)(2,1)S(1)}, f32[384,256]{1,0:T(8,128)S(1)}, /*index=5*/f32[256,256]{1,0:T(8,128)S(1)}) custom-call(f32[384,256]{1,0:T(8,128)} %c_in.1, f32[1,768,256]{2,1,0:T(8,128)} %v_in.1, f32[1,6,384,768]{3,2,1,0:T(8,128)} %r_in.1, ...), custom_call_target="tpu_custom_call" | custom-call | tf_op jit(solution)/shard_map/pallas_call | solution.py:99
  3.0 5.5 %collective-permute-start.2 = (f32[256,256]{1,0:T(8,128)S(1)}, f32[256,256]{1,0:T(8,128)S(1)}, u32[]{:S(2)}, u32[]{:S(2)}) collective-permute-start(f32[256,256]{1,0:T(8,128)S(1)} %get-tuple-element.13), channel_id=1, source_target_pairs={{0,30},{2,0},{4,2},{6,4},{8,6},{10,8},{12,10},{14,12},{16,14},{18,... | collective-permute-start | bytes 786440 | tf_op jit(solution)/shard_map/ppermute | solution.py:24
  8.9 0.5 fusion.35
  9.4 0.7 collective-permute-start
  10.5 0.5 fusion.36
  12.1 5.8 %collective-permute-done.1 = f32[256,256]{1,0:T(8,128)S(1)} collective-permute-done((f32[256,256]{1,0:T(8,128)S(1)}, f32[256,256]{1,0:T(8,128)S(1)}, u32[]{:S(2)}, u32[]{:S(2)}) %collective-permute-start.1) | collective-permute-done | bytes 262176 | tf_op jit(solution)/shard_map/ppermute | solution.py:24
  18.9 4.7 %collective-permute-start.4 = (f32[256,256]{1,0:T(8,128)S(1)}, f32[256,256]{1,0:T(8,128)S(1)}, u32[]{:S(2)}, u32[]{:S(2)}) collective-permute-start(f32[256,256]{1,0:T(8,128)S(1)} %fusion.38), channel_id=1, source_target_pairs={{0,30},{2,0},{4,2},{6,4},{8,6},{10,8},{12,10},{14,12},{16,14},{18,... | collective-permute-start | bytes 786440 | tf_op jit(solution)/shard_map/ppermute | solution.py:24
  26.5 6.6 %collective-permute-done.5 = f32[256,256]{1,0:T(8,128)S(1)} collective-permute-done((f32[256,256]{1,0:T(8,128)S(1)}, f32[256,256]{1,0:T(8,128)S(1)}, u32[]{:S(2)}, u32[]{:S(2)}) %collective-permute-start.5) | collective-permute-done | bytes 262176 | tf_op jit(solution)/shard_map/ppermute | solution.py:24
  33.8 0.5 fusion.42
  34.3 4.7 %collective-permute-start.9 = (f32[256,256]{1,0:T(8,128)S(1)}, f32[256,256]{1,0:T(8,128)S(1)}, u32[]{:S(2)}, u32[]{:S(2)}) collective-permute-start(f32[256,256]{1,0:T(8,128)S(1)} %fusion.42), channel_id=1, source_target_pairs={{0,30},{2,0},{4,2},{6,4},{8,6},{10,8},{12,10},{14,12},{16,14},{18,... | collective-permute-start | bytes 786440 | tf_op jit(solution)/shard_map/ppermute | solution.py:24
  40.4 1.6 %collective-permute-start.6 = (f32[384,256]{1,0:T(8,128)S(1)}, f32[384,256]{1,0:T(8,128)S(1)}, u32[]{:S(2)}, u32[]{:S(2)}) collective-permute-start(f32[384,256]{1,0:T(8,128)S(1)} %fusion.12), channel_id=1, source_target_pairs={{0,1},{1,0},{2,3},{3,2},{4,5},{5,4},{6,7},{7,6},{8,9},{9,8},{10,11... | collective-permute-start | bytes 1179656 | tf_op jit(solution)/shard_map/ppermute | solution.py:117
  42.0 0.5 fusion.41
  42.6 0.5 fusion.40
  43.2 5.1 %collective-permute-done.6 = f32[384,256]{1,0:T(8,128)S(1)} collective-permute-done((f32[384,256]{1,0:T(8,128)S(1)}, f32[384,256]{1,0:T(8,128)S(1)}, u32[]{:S(2)}, u32[]{:S(2)}) %collective-permute-start.6) | collective-permute-done | bytes 393248 | tf_op jit(solution)/shard_map/ppermute | solution.py:117
  49.1 0.5 fusion.45
  50.2 0.5 fusion.43
  50.8 4.1 %collective-permute-start.10 = (f32[256,256]{1,0:T(8,128)S(1)}, f32[256,256]{1,0:T(8,128)S(1)}, u32[]{:S(2)}, u32[]{:S(2)}) collective-permute-start(f32[256,256]{1,0:T(8,128)S(1)} %fusion.43), channel_id=1, source_target_pairs={{0,30},{2,0},{4,2},{6,4},{8,6},{10,8},{12,10},{14,12},{16,14},{18,... | collective-permute-start | bytes 786440 | tf_op jit(solution)/shard_map/ppermute | solution.py:24
  55.6 0.5 fusion.44
  56.5 2.2 %collective-permute-done.10 = f32[256,256]{1,0:T(8,128)S(1)} collective-permute-done((f32[256,256]{1,0:T(8,128)S(1)}, f32[256,256]{1,0:T(8,128)S(1)}, u32[]{:S(2)}, u32[]{:S(2)}) %collective-permute-start.10) | collective-permute-done | bytes 262176 | tf_op jit(solution)/shard_map/ppermute | solution.py:24
  59.6 4.7 %collective-permute-start.13 = (f32[256,256]{1,0:T(8,128)S(1)}, f32[256,256]{1,0:T(8,128)S(1)}, u32[]{:S(2)}, u32[]{:S(2)}) collective-permute-start(f32[256,256]{1,0:T(8,128)S(1)} %fusion.46), channel_id=1, source_target_pairs={{0,30},{2,0},{4,2},{6,4},{8,6},{10,8},{12,10},{14,12},{16,14},{18,... | collective-permute-start | bytes 786440 | tf_op jit(solution)/shard_map/ppermute | solution.py:24
  66.7 0.5 fusion.47
  67.2 0.6 collective-permute-start.14
  67.8 3.2 %collective-permute-done.15 = f32[256,256]{1,0:T(8,128)S(1)} collective-permute-done((f32[256,256]{1,0:T(8,128)S(1)}, f32[256,256]{1,0:T(8,128)S(1)}, u32[]{:S(2)}, u32[]{:S(2)}) %collective-permute-start.15) | collective-permute-done | bytes 262176 | tf_op jit(solution)/shard_map/ppermute | solution.py:24
  71.8 2.1 %collective-permute-done.14 = f32[256,256]{1,0:T(8,128)S(1)} collective-permute-done((f32[256,256]{1,0:T(8,128)S(1)}, f32[256,256]{1,0:T(8,128)S(1)}, u32[]{:S(2)}, u32[]{:S(2)}) %collective-permute-start.14) | collective-permute-done | bytes 262176 | tf_op jit(solution)/shard_map/ppermute | solution.py:24
  74.6 0.5 fusion.49
  75.9 0.8 collective-permute-start.16
  77.8 8.3 %collective-permute-done.17 = f32[256,256]{1,0:T(8,128)S(1)} collective-permute-done((f32[256,256]{1,0:T(8,128)S(1)}, f32[256,256]{1,0:T(8,128)S(1)}, u32[]{:S(2)}, u32[]{:S(2)}) %collective-permute-start.17) | collective-permute-done | bytes 262176 | tf_op jit(solution)/shard_map/ppermute | solution.py:34
  86.1 0.6 collective-permute-done.16
  86.7 0.8 add_multiply_fusion
  87.5 11.5 %collective-permute-done.19 = f32[256,256]{1,0:T(8,128)S(1)} collective-permute-done((f32[256,256]{1,0:T(8,128)S(1)}, f32[256,256]{1,0:T(8,128)S(1)}, u32[]{:S(2)}, u32[]{:S(2)}) %collective-permute-start.19) | collective-permute-done | bytes 262176 | tf_op jit(solution)/shard_map/ppermute | solution.py:24
  99.0 2.8 %collective-permute-done.20 = f32[256,256]{1,0:T(8,128)S(1)} collective-permute-done((f32[256,256]{1,0:T(8,128)S(1)}, f32[256,256]{1,0:T(8,128)S(1)}, u32[]{:S(2)}, u32[]{:S(2)}) %collective-permute-start.20) | collective-permute-done | bytes 262176 | tf_op jit(solution)/shard_map/ppermute | solution.py:24
  101.8 0.9 maximum_bitcast_fusion
  (70 shorter events, 16.9 us)
Async XLA Ops:
  0.6 17.4 %copy-start.1 = (bf16[1,6,384,768]{3,2,1,0:T(8,128)(2,1)S(1)}, bf16[1,6,384,768]{3,2,1,0:T(8,128)(2,1)}, u32[]{:S(2)}) copy-start(bf16[1,6,384,768]{3,2,1,0:T(8,128)(2,1)} %w_in.1) | copy-start | bytes 10616836
  3.0 21.5 %collective-permute-start.2 = (f32[256,256]{1,0:T(8,128)S(1)}, f32[256,256]{1,0:T(8,128)S(1)}, u32[]{:S(2)}, u32[]{:S(2)}) collective-permute-start(f32[256,256]{1,0:T(8,128)S(1)} %get-tuple-element.13), channel_id=1, source_target_pairs={{0,30},{2,0},{4,2},{6,4},{8,6},{10,8},{12,10},{14,12},{16,14},{18,... | collective-permute-start | bytes 786440 | tf_op jit(solution)/shard_map/ppermute | solution.py:24
  9.4 8.6 %copy-start = (f32[1,6,384,768]{3,2,1,0:T(8,128)S(1)}, f32[1,6,384,768]{3,2,1,0:T(8,128)}, u32[]{:S(2)}) copy-start(f32[1,6,384,768]{3,2,1,0:T(8,128)} %r_in.1) | copy-start | bytes 21233668
  9.4 14.1 %collective-permute-start = (f32[256,256]{1,0:T(8,128)S(1)}, f32[256,256]{1,0:T(8,128)S(1)}, u32[]{:S(2)}, u32[]{:S(2)}) collective-permute-start(f32[256,256]{1,0:T(8,128)S(1)} %fusion.35), channel_id=1, source_target_pairs={{0,30},{2,0},{4,2},{6,4},{8,6},{10,8},{12,10},{14,12},{16,14},{18,... | collective-permute-start | bytes 786440 | tf_op jit(solution)/shard_map/ppermute | solution.py:24
  11.1 6.9 %collective-permute-start.1 = (f32[256,256]{1,0:T(8,128)S(1)}, f32[256,256]{1,0:T(8,128)S(1)}, u32[]{:S(2)}, u32[]{:S(2)}) collective-permute-start(f32[256,256]{1,0:T(8,128)S(1)} %fusion.36), channel_id=1, source_target_pairs={{0,30},{2,0},{4,2},{6,4},{8,6},{10,8},{12,10},{14,12},{16,14},{18,... | collective-permute-start | bytes 786440 | tf_op jit(solution)/shard_map/ppermute | solution.py:24
  18.9 20.1 %collective-permute-start.4 = (f32[256,256]{1,0:T(8,128)S(1)}, f32[256,256]{1,0:T(8,128)S(1)}, u32[]{:S(2)}, u32[]{:S(2)}) collective-permute-start(f32[256,256]{1,0:T(8,128)S(1)} %fusion.38), channel_id=1, source_target_pairs={{0,30},{2,0},{4,2},{6,4},{8,6},{10,8},{12,10},{14,12},{16,14},{18,... | collective-permute-start | bytes 786440 | tf_op jit(solution)/shard_map/ppermute | solution.py:24
  24.4 15.2 %collective-permute-start.3 = (f32[256,256]{1,0:T(8,128)S(1)}, f32[256,256]{1,0:T(8,128)S(1)}, u32[]{:S(2)}, u32[]{:S(2)}) collective-permute-start(f32[256,256]{1,0:T(8,128)S(1)} %fusion.37), channel_id=1, source_target_pairs={{0,30},{2,0},{4,2},{6,4},{8,6},{10,8},{12,10},{14,12},{16,14},{18,... | collective-permute-start | bytes 786440 | tf_op jit(solution)/shard_map/ppermute | solution.py:24
  25.8 7.3 %collective-permute-start.5 = (f32[256,256]{1,0:T(8,128)S(1)}, f32[256,256]{1,0:T(8,128)S(1)}, u32[]{:S(2)}, u32[]{:S(2)}) collective-permute-start(f32[256,256]{1,0:T(8,128)S(1)} %fusion.39), channel_id=1, source_target_pairs={{0,30},{2,0},{4,2},{6,4},{8,6},{10,8},{12,10},{14,12},{16,14},{18,... | collective-permute-start | bytes 786440 | tf_op jit(solution)/shard_map/ppermute | solution.py:24
  34.3 14.0 %collective-permute-start.9 = (f32[256,256]{1,0:T(8,128)S(1)}, f32[256,256]{1,0:T(8,128)S(1)}, u32[]{:S(2)}, u32[]{:S(2)}) collective-permute-start(f32[256,256]{1,0:T(8,128)S(1)} %fusion.42), channel_id=1, source_target_pairs={{0,30},{2,0},{4,2},{6,4},{8,6},{10,8},{12,10},{14,12},{16,14},{18,... | collective-permute-start | bytes 786440 | tf_op jit(solution)/shard_map/ppermute | solution.py:24
  40.4 7.8 %collective-permute-start.6 = (f32[384,256]{1,0:T(8,128)S(1)}, f32[384,256]{1,0:T(8,128)S(1)}, u32[]{:S(2)}, u32[]{:S(2)}) collective-permute-start(f32[384,256]{1,0:T(8,128)S(1)} %fusion.12), channel_id=1, source_target_pairs={{0,1},{1,0},{2,3},{3,2},{4,5},{5,4},{6,7},{7,6},{8,9},{9,8},{10,11... | collective-permute-start | bytes 1179656 | tf_op jit(solution)/shard_map/ppermute | solution.py:117
  42.5 12.3 %collective-permute-start.8 = (f32[256,256]{1,0:T(8,128)S(1)}, f32[256,256]{1,0:T(8,128)S(1)}, u32[]{:S(2)}, u32[]{:S(2)}) collective-permute-start(f32[256,256]{1,0:T(8,128)S(1)} %fusion.41), channel_id=1, source_target_pairs={{0,30},{2,0},{4,2},{6,4},{8,6},{10,8},{12,10},{14,12},{16,14},{18,... | collective-permute-start | bytes 786440 | tf_op jit(solution)/shard_map/ppermute | solution.py:24
  43.1 6.7 %collective-permute-start.7 = (f32[256,256]{1,0:T(8,128)S(1)}, f32[256,256]{1,0:T(8,128)S(1)}, u32[]{:S(2)}, u32[]{:S(2)}) collective-permute-start(f32[256,256]{1,0:T(8,128)S(1)} %fusion.40), channel_id=1, source_target_pairs={{0,30},{2,0},{4,2},{6,4},{8,6},{10,8},{12,10},{14,12},{16,14},{18,... | collective-permute-start | bytes 786440 | tf_op jit(solution)/shard_map/ppermute | solution.py:24
  49.6 14.7 %collective-permute-start.12 = (f32[256,256]{1,0:T(8,128)S(1)}, f32[256,256]{1,0:T(8,128)S(1)}, u32[]{:S(2)}, u32[]{:S(2)}) collective-permute-start(f32[256,256]{1,0:T(8,128)S(1)} %fusion.45), channel_id=1, source_target_pairs={{0,30},{2,0},{4,2},{6,4},{8,6},{10,8},{12,10},{14,12},{16,14},{18,... | collective-permute-start | bytes 786440 | tf_op jit(solution)/shard_map/ppermute | solution.py:24
  50.8 8.0 %collective-permute-start.10 = (f32[256,256]{1,0:T(8,128)S(1)}, f32[256,256]{1,0:T(8,128)S(1)}, u32[]{:S(2)}, u32[]{:S(2)}) collective-permute-start(f32[256,256]{1,0:T(8,128)S(1)} %fusion.43), channel_id=1, source_target_pairs={{0,30},{2,0},{4,2},{6,4},{8,6},{10,8},{12,10},{14,12},{16,14},{18,... | collective-permute-start | bytes 786440 | tf_op jit(solution)/shard_map/ppermute | solution.py:24
  56.1 9.5 %collective-permute-start.11 = (f32[256,256]{1,0:T(8,128)S(1)}, f32[256,256]{1,0:T(8,128)S(1)}, u32[]{:S(2)}, u32[]{:S(2)}) collective-permute-start(f32[256,256]{1,0:T(8,128)S(1)} %fusion.44), channel_id=1, source_target_pairs={{0,30},{2,0},{4,2},{6,4},{8,6},{10,8},{12,10},{14,12},{16,14},{18,... | collective-permute-start | bytes 786440 | tf_op jit(solution)/shard_map/ppermute | solution.py:24
  59.6 15.5 %collective-permute-start.13 = (f32[256,256]{1,0:T(8,128)S(1)}, f32[256,256]{1,0:T(8,128)S(1)}, u32[]{:S(2)}, u32[]{:S(2)}) collective-permute-start(f32[256,256]{1,0:T(8,128)S(1)} %fusion.46), channel_id=1, source_target_pairs={{0,30},{2,0},{4,2},{6,4},{8,6},{10,8},{12,10},{14,12},{16,14},{18,... | collective-permute-start | bytes 786440 | tf_op jit(solution)/shard_map/ppermute | solution.py:24
  65.5 5.5 %collective-permute-start.15 = (f32[256,256]{1,0:T(8,128)S(1)}, f32[256,256]{1,0:T(8,128)S(1)}, u32[]{:S(2)}, u32[]{:S(2)}) collective-permute-start(f32[256,256]{1,0:T(8,128)S(1)} %fusion.48), channel_id=1, source_target_pairs={{0,30},{2,0},{4,2},{6,4},{8,6},{10,8},{12,10},{14,12},{16,14},{18,... | collective-permute-start | bytes 786440 | tf_op jit(solution)/shard_map/ppermute | solution.py:24
  67.2 6.6 %collective-permute-start.14 = (f32[256,256]{1,0:T(8,128)S(1)}, f32[256,256]{1,0:T(8,128)S(1)}, u32[]{:S(2)}, u32[]{:S(2)}) collective-permute-start(f32[256,256]{1,0:T(8,128)S(1)} %fusion.47), channel_id=1, source_target_pairs={{0,30},{2,0},{4,2},{6,4},{8,6},{10,8},{12,10},{14,12},{16,14},{18,... | collective-permute-start | bytes 786440 | tf_op jit(solution)/shard_map/ppermute | solution.py:24
  75.1 11.0 %collective-permute-start.17 = (f32[256,256]{1,0:T(8,128)S(1)}, f32[256,256]{1,0:T(8,128)S(1)}, u32[]{:S(2)}, u32[]{:S(2)}) collective-permute-start(f32[256,256]{1,0:T(8,128)S(1)} %fusion.49), channel_id=1, source_target_pairs={{0,8},{2,10},{4,12},{6,22},{8,16},{10,18},{12,20},{14,30},{16,24},... | collective-permute-start | bytes 786440 | tf_op jit(solution)/shard_map/ppermute | solution.py:34
  75.9 10.8 %collective-permute-start.16 = (f32[384,256]{1,0:T(8,128)S(1)}, f32[384,256]{1,0:T(8,128)S(1)}, u32[]{:S(2)}, u32[]{:S(2)}) collective-permute-start(f32[384,256]{1,0:T(8,128)S(1)} %fusion.30), channel_id=1, source_target_pairs={{0,1},{1,0},{2,3},{3,2},{4,5},{5,4},{6,7},{7,6},{8,9},{9,8},{10,11... | collective-permute-start | bytes 1179656 | tf_op jit(solution)/shard_map/ppermute | solution.py:117
  77.2 21.9 %collective-permute-start.19 = (f32[256,256]{1,0:T(8,128)S(1)}, f32[256,256]{1,0:T(8,128)S(1)}, u32[]{:S(2)}, u32[]{:S(2)}) collective-permute-start(f32[256,256]{1,0:T(8,128)S(1)} %fusion.50), channel_id=1, source_target_pairs={{0,10},{2,12},{4,14},{6,16},{8,18},{10,20},{12,22},{14,24},{16,26}... | collective-permute-start | bytes 786440 | tf_op jit(solution)/shard_map/ppermute | solution.py:24
  77.7 24.1 %collective-permute-start.20 = (f32[256,256]{1,0:T(8,128)S(1)}, f32[256,256]{1,0:T(8,128)S(1)}, u32[]{:S(2)}, u32[]{:S(2)}) collective-permute-start(f32[256,256]{1,0:T(8,128)S(1)} %fusion.51), channel_id=1, source_target_pairs={{0,10},{2,12},{4,14},{6,16},{8,18},{10,20},{12,22},{14,24},{16,26}... | collective-permute-start | bytes 786440 | tf_op jit(solution)/shard_map/ppermute | solution.py:24
  86.1 15.7 %collective-permute-start.18 = (f32[256,256]{1,0:T(8,128)S(1)}, f32[256,256]{1,0:T(8,128)S(1)}, u32[]{:S(2)}, u32[]{:S(2)}) collective-permute-start(f32[256,256]{1,0:T(8,128)S(1)} %collective-permute-done.17), channel_id=1, source_target_pairs={{8,10},{10,12},{12,14},{22,16},{16,18},{18,20},{20,22},{30,24},{24... | collective-permute-start | bytes 786440 | tf_op jit(solution)/shard_map/ppermute | solution.py:35

commit v7 on v6

--- a/solution.py
+++ b/solution.py
@@ -47,10 +47,12 @@
 
 
 def dot_of_halves(lhs, rhs, dims):
-    part = functools.partial(
-        lax.dot_general, dimension_numbers=(dims, ((), ())), preferred_element_type=jnp.float32
-    )
-    return part(lhs[0], rhs[0]) + (part(lhs[0], rhs[1]) + part(lhs[1], rhs[0]))
+    return lax.dot_general(
+        jnp.concatenate([lhs[0], lhs[0], lhs[1]], axis=dims[0][0]),
+        jnp.concatenate([rhs[0], rhs[1], rhs[0]], axis=dims[1][0]),
+        (dims, ((), ())),
+        preferred_element_type=jnp.float32,
+    )
 
 
 def first_kernel(c_in, v_in, r_in, w_in, c, v, r, w, residual, moved, sems):
@@ -104,6 +106,32 @@
         scratch_shapes=[pltpu.SemaphoreType.DMA((7,))],
         compiler_params=pltpu.CompilerParams(vmem_limit_bytes=16 << 20),
     )(*[pltpu.with_memory_space_constraint(a, pltpu.HBM) for a in operands])
+
+
+def store_kernel(spans, *refs):
+    pieces, whole, sems = refs[: len(spans)], refs[-2], refs[-1]
+    copies = [
+        pltpu.make_async_copy(piece, whole.at[0, span], sems.at[i])
+        for i, (piece, span) in enumerate(zip(pieces, spans))
+    ]
+    for copy in copies:
+        copy.start()
+    for copy in copies:
+        copy.wait()
+
+
+def store(pieces, spans, shape, whole=None):
+    anywhere = pl.BlockSpec(memory_space=pltpu.HBM)
+    inside = pl.BlockSpec(memory_space=pltpu.VMEM)
+    return pl.pallas_call(
+        functools.partial(store_kernel, spans),
+        out_shape=jax.ShapeDtypeStruct(shape, jnp.float32),
+        in_specs=[inside] * len(pieces) + [anywhere] * (whole is not None),
+        out_specs=anywhere,
+        input_output_aliases={} if whole is None else {len(pieces): 0},
+        scratch_shapes=[pltpu.SemaphoreType.DMA((len(pieces),))],
+        compiler_params=pltpu.CompilerParams(vmem_limit_bytes=8 << 20),
+    )(*pieces, *([] if whole is None else [whole]))
 
 
 def combine(current):
@@ -154,7 +182,9 @@
                     pieces[i] = from_behind(moved, "users", -1)
             current = gained
         factors_u = combine(current)
-    return (factors_u, jnp.concatenate(pieces, axis=0)[None])
+    spans = tuple(slice(i * rows, (i + 1) * rows) for i in range(PIECES))
+    whole = store(pieces[:-1], spans[:-1], item_factors.shape)
+    return (factors_u, store(pieces[-1:], spans[-1:], item_factors.shape, whole))
 
 
 def solution(mesh):

time: 103 us -> 103 us (level)
  Pallas kernels: 2.34 us -> 3.81 us
    pallas_call x0 -> x2, Pallas kernels: none -> 1.52 us  [store(): pl.pallas_call(functools.partial(store_kernel, spans), out_shape=jax.Shap...]
  transfers between devices with their start and end apart: 21 -> 21, of which waited for: 10 -> 9; matrix products, arithmetic and copies ran while one was open for 21% -> 21% of each run, Pallas kernels for 0% -> 1%
where the time goes in v7:
time: 103 us
  waiting for transfers between devices  47.5 us (46%)
  starting transfers between devices  28.1 us (27%)
  matrix products  21.1 us (20%)
  Pallas kernels  3.81 us (4%)
  between operations  1.34 us (1%)
    ppermute x17, waiting for transfers between devices, from_behind(): lax.ppermute(array, axis, [(i, (i + by) % peers) for i in range(peers)])  33.5 us
    ppermute x17, starting transfers between devices, from_behind(): lax.ppermute(array, axis, [(i, (i + by) % peers) for i in range(peers)])  25.7 us
    dot_general x52, matrix products, dot(): lax.dot_general(lhs, rhs, (dims, ((), ())), precision=lax.Precision.HIGH,...  21.1 us
    ppermute x1, waiting for transfers between devices, home(): array = lax.ppermute(array, 'users', across)  8.89 us
    ppermute x2, waiting for transfers between devices, combine(): partner = lax.ppermute(summed, 'period', partners)  5.08 us
    ppermute x2, starting transfers between devices, combine(): partner = lax.ppermute(summed, 'period', partners)  2.33 us
    pallas_call x1, Pallas kernels, first_piece(): pl.pallas_call(first_kernel, out_shape=tuple(outs), in_specs=[pl.BlockSpe...  2.29 us
  transfers between devices with their start and end apart: 21, of which 9 were waited for; matrix products, arithmetic and copies ran while one was open for 21% of the time, Pallas kernels for 1%

profile of v7, /device:TPU:0, one launch (start us, length us, event | category | flops | bytes accessed | tf_op | source)
XLA Modules:
  0.0 102.7 jit_solution(16930206704032715958)
XLA Ops:
  0.6 2.3 %shard_map.59 = (f32[384,256]{1,0:T(8,128)S(1)}, f32[768,256]{1,0:T(8,128)S(1)}, f32[384,768]{1,0:T(8,128)S(1)}, bf16[384,768]{1,0:T(8,128)(2,1)S(1)}, f32[384,256]{1,0:T(8,128)S(1)}, /*index=5*/f32[256,256]{1,0:T(8,128)S(1)}) custom-call(f32[384,256]{1,0:T(8,128)} %c_in.1, f32[1,768,256]{2,1,0:T(8,128)} %v_in.1, f32[1,6,384,768]{3,2,1,0:T(8,128)} %r_in.1, ...), custom_call_target="tpu_custom_call" | custom-call | tf_op jit(solution)/shard_map/pallas_call | solution.py:101
  2.9 5.5 %collective-permute-start.2 = (f32[256,256]{1,0:T(8,128)S(1)}, f32[256,256]{1,0:T(8,128)S(1)}, u32[]{:S(2)}, u32[]{:S(2)}) collective-permute-start(f32[256,256]{1,0:T(8,128)S(1)} %get-tuple-element.13), channel_id=1, source_target_pairs={{0,30},{2,0},{4,2},{6,4},{8,6},{10,8},{12,10},{14,12},{16,14},{18,... | collective-permute-start | bytes 786440 | tf_op jit(solution)/shard_map/ppermute | solution.py:24
  8.8 0.5 fusion.35
  9.4 0.7 collective-permute-start
  10.5 0.5 fusion.36
  12.1 5.8 %collective-permute-done.1 = f32[256,256]{1,0:T(8,128)S(1)} collective-permute-done((f32[256,256]{1,0:T(8,128)S(1)}, f32[256,256]{1,0:T(8,128)S(1)}, u32[]{:S(2)}, u32[]{:S(2)}) %collective-permute-start.1) | collective-permute-done | bytes 262176 | tf_op jit(solution)/shard_map/ppermute | solution.py:24
  18.8 4.7 %collective-permute-start.4 = (f32[256,256]{1,0:T(8,128)S(1)}, f32[256,256]{1,0:T(8,128)S(1)}, u32[]{:S(2)}, u32[]{:S(2)}) collective-permute-start(f32[256,256]{1,0:T(8,128)S(1)} %fusion.38), channel_id=1, source_target_pairs={{0,30},{2,0},{4,2},{6,4},{8,6},{10,8},{12,10},{14,12},{16,14},{18,... | collective-permute-start | bytes 786440 | tf_op jit(solution)/shard_map/ppermute | solution.py:24
  26.5 6.6 %collective-permute-done.5 = f32[256,256]{1,0:T(8,128)S(1)} collective-permute-done((f32[256,256]{1,0:T(8,128)S(1)}, f32[256,256]{1,0:T(8,128)S(1)}, u32[]{:S(2)}, u32[]{:S(2)}) %collective-permute-start.5) | collective-permute-done | bytes 262176 | tf_op jit(solution)/shard_map/ppermute | solution.py:24
  33.7 0.5 fusion.42
  34.3 4.7 %collective-permute-start.9 = (f32[256,256]{1,0:T(8,128)S(1)}, f32[256,256]{1,0:T(8,128)S(1)}, u32[]{:S(2)}, u32[]{:S(2)}) collective-permute-start(f32[256,256]{1,0:T(8,128)S(1)} %fusion.42), channel_id=1, source_target_pairs={{0,30},{2,0},{4,2},{6,4},{8,6},{10,8},{12,10},{14,12},{16,14},{18,... | collective-permute-start | bytes 786440 | tf_op jit(solution)/shard_map/ppermute | solution.py:24
  40.4 1.6 %collective-permute-start.6 = (f32[384,256]{1,0:T(8,128)S(1)}, f32[384,256]{1,0:T(8,128)S(1)}, u32[]{:S(2)}, u32[]{:S(2)}) collective-permute-start(f32[384,256]{1,0:T(8,128)S(1)} %fusion.12), channel_id=1, source_target_pairs={{0,1},{1,0},{2,3},{3,2},{4,5},{5,4},{6,7},{7,6},{8,9},{9,8},{10,11... | collective-permute-start | bytes 1179656 | tf_op jit(solution)/shard_map/ppermute | solution.py:145
  42.0 0.5 fusion.41
  42.6 0.5 fusion.40
  43.1 5.1 %collective-permute-done.6 = f32[384,256]{1,0:T(8,128)S(1)} collective-permute-done((f32[384,256]{1,0:T(8,128)S(1)}, f32[384,256]{1,0:T(8,128)S(1)}, u32[]{:S(2)}, u32[]{:S(2)}) %collective-permute-start.6) | collective-permute-done | bytes 393248 | tf_op jit(solution)/shard_map/ppermute | solution.py:145
  49.0 0.5 fusion.45
  50.7 4.1 %collective-permute-start.10 = (f32[256,256]{1,0:T(8,128)S(1)}, f32[256,256]{1,0:T(8,128)S(1)}, u32[]{:S(2)}, u32[]{:S(2)}) collective-permute-start(f32[256,256]{1,0:T(8,128)S(1)} %fusion.43), channel_id=1, source_target_pairs={{0,30},{2,0},{4,2},{6,4},{8,6},{10,8},{12,10},{14,12},{16,14},{18,... | collective-permute-start | bytes 786440 | tf_op jit(solution)/shard_map/ppermute | solution.py:24
  55.5 0.5 fusion.44
  56.5 2.2 %collective-permute-done.10 = f32[256,256]{1,0:T(8,128)S(1)} collective-permute-done((f32[256,256]{1,0:T(8,128)S(1)}, f32[256,256]{1,0:T(8,128)S(1)}, u32[]{:S(2)}, u32[]{:S(2)}) %collective-permute-start.10) | collective-permute-done | bytes 262176 | tf_op jit(solution)/shard_map/ppermute | solution.py:24
  59.6 4.7 %collective-permute-start.13 = (f32[256,256]{1,0:T(8,128)S(1)}, f32[256,256]{1,0:T(8,128)S(1)}, u32[]{:S(2)}, u32[]{:S(2)}) collective-permute-start(f32[256,256]{1,0:T(8,128)S(1)} %fusion.46), channel_id=1, source_target_pairs={{0,30},{2,0},{4,2},{6,4},{8,6},{10,8},{12,10},{14,12},{16,14},{18,... | collective-permute-start | bytes 786440 | tf_op jit(solution)/shard_map/ppermute | solution.py:24
  65.0 0.5 fusion.48
  66.6 0.5 fusion.47
  67.2 0.6 collective-permute-start.14
  67.7 3.2 %collective-permute-done.15 = f32[256,256]{1,0:T(8,128)S(1)} collective-permute-done((f32[256,256]{1,0:T(8,128)S(1)}, f32[256,256]{1,0:T(8,128)S(1)}, u32[]{:S(2)}, u32[]{:S(2)}) %collective-permute-start.15) | collective-permute-done | bytes 262176 | tf_op jit(solution)/shard_map/ppermute | solution.py:24
  71.7 2.1 %collective-permute-done.14 = f32[256,256]{1,0:T(8,128)S(1)} collective-permute-done((f32[256,256]{1,0:T(8,128)S(1)}, f32[256,256]{1,0:T(8,128)S(1)}, u32[]{:S(2)}, u32[]{:S(2)}) %collective-permute-start.14) | collective-permute-done | bytes 262176 | tf_op jit(solution)/shard_map/ppermute | solution.py:24
  74.5 0.5 fusion.50
  75.9 0.8 collective-permute-start.16
  77.2 8.9 %collective-permute-done.18 = f32[256,256]{1,0:T(8,128)S(1)} collective-permute-done((f32[256,256]{1,0:T(8,128)S(1)}, f32[256,256]{1,0:T(8,128)S(1)}, u32[]{:S(2)}, u32[]{:S(2)}) %collective-permute-start.18) | collective-permute-done | bytes 262176 | tf_op jit(solution)/shard_map/ppermute | solution.py:34
  86.7 0.8 add_multiply_fusion
  87.5 11.5 %collective-permute-done.20.refs_1_ = f32[256,256]{1,0:T(8,128)S(1)} collective-permute-done((f32[256,256]{1,0:T(8,128)S(1)}, f32[256,256]{1,0:T(8,128)S(1)}, u32[]{:S(2)}, u32[]{:S(2)}) %collective-permute-start.20) | collective-permute-done | bytes 262176 | tf_op jit(solution)/shard_map/ppermute | solution.py:24
  99.0 0.8 shard_map.60.refs_1_
  99.8 2.0 %collective-permute-done.17.refs_0_ = f32[256,256]{1,0:T(8,128)S(1)} collective-permute-done((f32[256,256]{1,0:T(8,128)S(1)}, f32[256,256]{1,0:T(8,128)S(1)}, u32[]{:S(2)}, u32[]{:S(2)}) %collective-permute-start.17) | collective-permute-done | bytes 262176 | tf_op jit(solution)/shard_map/ppermute | solution.py:24
  101.8 0.7 shard_map.61
  (71 shorter events, 16.9 us)
Async XLA Ops:
  0.6 17.3 %copy-start.1 = (bf16[1,6,384,768]{3,2,1,0:T(8,128)(2,1)S(1)}, bf16[1,6,384,768]{3,2,1,0:T(8,128)(2,1)}, u32[]{:S(2)}) copy-start(bf16[1,6,384,768]{3,2,1,0:T(8,128)(2,1)} %w_in.1) | copy-start | bytes 10616836
  2.9 21.5 %collective-permute-start.2 = (f32[256,256]{1,0:T(8,128)S(1)}, f32[256,256]{1,0:T(8,128)S(1)}, u32[]{:S(2)}, u32[]{:S(2)}) collective-permute-start(f32[256,256]{1,0:T(8,128)S(1)} %get-tuple-element.13), channel_id=1, source_target_pairs={{0,30},{2,0},{4,2},{6,4},{8,6},{10,8},{12,10},{14,12},{16,14},{18,... | collective-permute-start | bytes 786440 | tf_op jit(solution)/shard_map/ppermute | solution.py:24
  9.3 8.6 %copy-start = (f32[1,6,384,768]{3,2,1,0:T(8,128)S(1)}, f32[1,6,384,768]{3,2,1,0:T(8,128)}, u32[]{:S(2)}) copy-start(f32[1,6,384,768]{3,2,1,0:T(8,128)} %r_in.1) | copy-start | bytes 21233668
  9.4 14.1 %collective-permute-start = (f32[256,256]{1,0:T(8,128)S(1)}, f32[256,256]{1,0:T(8,128)S(1)}, u32[]{:S(2)}, u32[]{:S(2)}) collective-permute-start(f32[256,256]{1,0:T(8,128)S(1)} %fusion.35), channel_id=1, source_target_pairs={{0,30},{2,0},{4,2},{6,4},{8,6},{10,8},{12,10},{14,12},{16,14},{18,... | collective-permute-start | bytes 786440 | tf_op jit(solution)/shard_map/ppermute | solution.py:24
  11.0 6.9 %collective-permute-start.1 = (f32[256,256]{1,0:T(8,128)S(1)}, f32[256,256]{1,0:T(8,128)S(1)}, u32[]{:S(2)}, u32[]{:S(2)}) collective-permute-start(f32[256,256]{1,0:T(8,128)S(1)} %fusion.36), channel_id=1, source_target_pairs={{0,30},{2,0},{4,2},{6,4},{8,6},{10,8},{12,10},{14,12},{16,14},{18,... | collective-permute-start | bytes 786440 | tf_op jit(solution)/shard_map/ppermute | solution.py:24
  18.8 20.1 %collective-permute-start.4 = (f32[256,256]{1,0:T(8,128)S(1)}, f32[256,256]{1,0:T(8,128)S(1)}, u32[]{:S(2)}, u32[]{:S(2)}) collective-permute-start(f32[256,256]{1,0:T(8,128)S(1)} %fusion.38), channel_id=1, source_target_pairs={{0,30},{2,0},{4,2},{6,4},{8,6},{10,8},{12,10},{14,12},{16,14},{18,... | collective-permute-start | bytes 786440 | tf_op jit(solution)/shard_map/ppermute | solution.py:24
  24.4 15.2 %collective-permute-start.3 = (f32[256,256]{1,0:T(8,128)S(1)}, f32[256,256]{1,0:T(8,128)S(1)}, u32[]{:S(2)}, u32[]{:S(2)}) collective-permute-start(f32[256,256]{1,0:T(8,128)S(1)} %fusion.37), channel_id=1, source_target_pairs={{0,30},{2,0},{4,2},{6,4},{8,6},{10,8},{12,10},{14,12},{16,14},{18,... | collective-permute-start | bytes 786440 | tf_op jit(solution)/shard_map/ppermute | solution.py:24
  25.7 7.3 %collective-permute-start.5 = (f32[256,256]{1,0:T(8,128)S(1)}, f32[256,256]{1,0:T(8,128)S(1)}, u32[]{:S(2)}, u32[]{:S(2)}) collective-permute-start(f32[256,256]{1,0:T(8,128)S(1)} %fusion.39), channel_id=1, source_target_pairs={{0,30},{2,0},{4,2},{6,4},{8,6},{10,8},{12,10},{14,12},{16,14},{18,... | collective-permute-start | bytes 786440 | tf_op jit(solution)/shard_map/ppermute | solution.py:24
  34.3 14.0 %collective-permute-start.9 = (f32[256,256]{1,0:T(8,128)S(1)}, f32[256,256]{1,0:T(8,128)S(1)}, u32[]{:S(2)}, u32[]{:S(2)}) collective-permute-start(f32[256,256]{1,0:T(8,128)S(1)} %fusion.42), channel_id=1, source_target_pairs={{0,30},{2,0},{4,2},{6,4},{8,6},{10,8},{12,10},{14,12},{16,14},{18,... | collective-permute-start | bytes 786440 | tf_op jit(solution)/shard_map/ppermute | solution.py:24
  40.4 7.8 %collective-permute-start.6 = (f32[384,256]{1,0:T(8,128)S(1)}, f32[384,256]{1,0:T(8,128)S(1)}, u32[]{:S(2)}, u32[]{:S(2)}) collective-permute-start(f32[384,256]{1,0:T(8,128)S(1)} %fusion.12), channel_id=1, source_target_pairs={{0,1},{1,0},{2,3},{3,2},{4,5},{5,4},{6,7},{7,6},{8,9},{9,8},{10,11... | collective-permute-start | bytes 1179656 | tf_op jit(solution)/shard_map/ppermute | solution.py:145
  42.5 12.3 %collective-permute-start.8 = (f32[256,256]{1,0:T(8,128)S(1)}, f32[256,256]{1,0:T(8,128)S(1)}, u32[]{:S(2)}, u32[]{:S(2)}) collective-permute-start(f32[256,256]{1,0:T(8,128)S(1)} %fusion.41), channel_id=1, source_target_pairs={{0,30},{2,0},{4,2},{6,4},{8,6},{10,8},{12,10},{14,12},{16,14},{18,... | collective-permute-start | bytes 786440 | tf_op jit(solution)/shard_map/ppermute | solution.py:24
  43.1 6.7 %collective-permute-start.7 = (f32[256,256]{1,0:T(8,128)S(1)}, f32[256,256]{1,0:T(8,128)S(1)}, u32[]{:S(2)}, u32[]{:S(2)}) collective-permute-start(f32[256,256]{1,0:T(8,128)S(1)} %fusion.40), channel_id=1, source_target_pairs={{0,30},{2,0},{4,2},{6,4},{8,6},{10,8},{12,10},{14,12},{16,14},{18,... | collective-permute-start | bytes 786440 | tf_op jit(solution)/shard_map/ppermute | solution.py:24
  49.5 14.7 %collective-permute-start.12 = (f32[256,256]{1,0:T(8,128)S(1)}, f32[256,256]{1,0:T(8,128)S(1)}, u32[]{:S(2)}, u32[]{:S(2)}) collective-permute-start(f32[256,256]{1,0:T(8,128)S(1)} %fusion.45), channel_id=1, source_target_pairs={{0,30},{2,0},{4,2},{6,4},{8,6},{10,8},{12,10},{14,12},{16,14},{18,... | collective-permute-start | bytes 786440 | tf_op jit(solution)/shard_map/ppermute | solution.py:24
  50.7 8.0 %collective-permute-start.10 = (f32[256,256]{1,0:T(8,128)S(1)}, f32[256,256]{1,0:T(8,128)S(1)}, u32[]{:S(2)}, u32[]{:S(2)}) collective-permute-start(f32[256,256]{1,0:T(8,128)S(1)} %fusion.43), channel_id=1, source_target_pairs={{0,30},{2,0},{4,2},{6,4},{8,6},{10,8},{12,10},{14,12},{16,14},{18,... | collective-permute-start | bytes 786440 | tf_op jit(solution)/shard_map/ppermute | solution.py:24
  56.1 9.5 %collective-permute-start.11 = (f32[256,256]{1,0:T(8,128)S(1)}, f32[256,256]{1,0:T(8,128)S(1)}, u32[]{:S(2)}, u32[]{:S(2)}) collective-permute-start(f32[256,256]{1,0:T(8,128)S(1)} %fusion.44), channel_id=1, source_target_pairs={{0,30},{2,0},{4,2},{6,4},{8,6},{10,8},{12,10},{14,12},{16,14},{18,... | collective-permute-start | bytes 786440 | tf_op jit(solution)/shard_map/ppermute | solution.py:24
  59.6 15.5 %collective-permute-start.13 = (f32[256,256]{1,0:T(8,128)S(1)}, f32[256,256]{1,0:T(8,128)S(1)}, u32[]{:S(2)}, u32[]{:S(2)}) collective-permute-start(f32[256,256]{1,0:T(8,128)S(1)} %fusion.46), channel_id=1, source_target_pairs={{0,30},{2,0},{4,2},{6,4},{8,6},{10,8},{12,10},{14,12},{16,14},{18,... | collective-permute-start | bytes 786440 | tf_op jit(solution)/shard_map/ppermute | solution.py:24
  65.5 5.5 %collective-permute-start.15 = (f32[256,256]{1,0:T(8,128)S(1)}, f32[256,256]{1,0:T(8,128)S(1)}, u32[]{:S(2)}, u32[]{:S(2)}) collective-permute-start(f32[256,256]{1,0:T(8,128)S(1)} %fusion.48), channel_id=1, source_target_pairs={{0,30},{2,0},{4,2},{6,4},{8,6},{10,8},{12,10},{14,12},{16,14},{18,... | collective-permute-start | bytes 786440 | tf_op jit(solution)/shard_map/ppermute | solution.py:24
  67.2 6.6 %collective-permute-start.14 = (f32[256,256]{1,0:T(8,128)S(1)}, f32[256,256]{1,0:T(8,128)S(1)}, u32[]{:S(2)}, u32[]{:S(2)}) collective-permute-start(f32[256,256]{1,0:T(8,128)S(1)} %fusion.47), channel_id=1, source_target_pairs={{0,30},{2,0},{4,2},{6,4},{8,6},{10,8},{12,10},{14,12},{16,14},{18,... | collective-permute-start | bytes 786440 | tf_op jit(solution)/shard_map/ppermute | solution.py:24
  75.0 11.0 %collective-permute-start.18 = (f32[256,256]{1,0:T(8,128)S(1)}, f32[256,256]{1,0:T(8,128)S(1)}, u32[]{:S(2)}, u32[]{:S(2)}) collective-permute-start(f32[256,256]{1,0:T(8,128)S(1)} %fusion.50), channel_id=1, source_target_pairs={{0,8},{2,10},{4,12},{6,22},{8,16},{10,18},{12,20},{14,30},{16,24},... | collective-permute-start | bytes 786440 | tf_op jit(solution)/shard_map/ppermute | solution.py:34
  75.9 10.8 %collective-permute-start.16 = (f32[384,256]{1,0:T(8,128)S(1)}, f32[384,256]{1,0:T(8,128)S(1)}, u32[]{:S(2)}, u32[]{:S(2)}) collective-permute-start(f32[384,256]{1,0:T(8,128)S(1)} %fusion.30), channel_id=1, source_target_pairs={{0,1},{1,0},{2,3},{3,2},{4,5},{5,4},{6,7},{7,6},{8,9},{9,8},{10,11... | collective-permute-start | bytes 1179656 | tf_op jit(solution)/shard_map/ppermute | solution.py:145
  77.1 21.9 %collective-permute-start.20 = (f32[256,256]{1,0:T(8,128)S(1)}, f32[256,256]{1,0:T(8,128)S(1)}, u32[]{:S(2)}, u32[]{:S(2)}) collective-permute-start(f32[256,256]{1,0:T(8,128)S(1)} %fusion.51), channel_id=1, source_target_pairs={{0,10},{2,12},{4,14},{6,16},{8,18},{10,20},{12,22},{14,24},{16,26}... | collective-permute-start | bytes 786440 | tf_op jit(solution)/shard_map/ppermute | solution.py:24
  86.1 12.9 %collective-permute-start.19 = (f32[256,256]{1,0:T(8,128)S(1)}, f32[256,256]{1,0:T(8,128)S(1)}, u32[]{:S(2)}, u32[]{:S(2)}) collective-permute-start(f32[256,256]{1,0:T(8,128)S(1)} %collective-permute-done.18), channel_id=1, source_target_pairs={{8,10},{10,12},{12,14},{22,16},{16,18},{18,20},{20,22},{30,24},{24... | collective-permute-start | bytes 786440 | tf_op jit(solution)/shard_map/ppermute | solution.py:35
  86.6 15.2 %collective-permute-start.17 = (f32[256,256]{1,0:T(8,128)S(1)}, f32[256,256]{1,0:T(8,128)S(1)}, u32[]{:S(2)}, u32[]{:S(2)}) collective-permute-start(f32[256,256]{1,0:T(8,128)S(1)} %fusion.49), channel_id=1, source_target_pairs={{0,10},{2,12},{4,14},{6,16},{8,18},{10,20},{12,22},{14,24},{16,26}... | collective-permute-start | bytes 786440 | tf_op jit(solution)/shard_map/ppermute | solution.py:24

commit v8 on v6

--- a/solution.py
+++ b/solution.py
@@ -1,5 +1,3 @@
-import functools
-
 import jax
 import jax.numpy as jnp
 from jax import lax
@@ -47,10 +45,12 @@
 
 
 def dot_of_halves(lhs, rhs, dims):
-    part = functools.partial(
-        lax.dot_general, dimension_numbers=(dims, ((), ())), preferred_element_type=jnp.float32
+    return lax.dot_general(
+        jnp.concatenate([lhs[0], lhs[0], lhs[1]], axis=dims[0][0]),
+        jnp.concatenate([rhs[0], rhs[1], rhs[0]], axis=dims[1][0]),
+        (dims, ((), ())),
+        preferred_element_type=jnp.float32,
     )
-    return part(lhs[0], rhs[0]) + (part(lhs[0], rhs[1]) + part(lhs[1], rhs[0]))
 
 
 def first_kernel(c_in, v_in, r_in, w_in, c, v, r, w, residual, moved, sems):

time: 103 us -> 103 us (level)
  no operation moved by 1% of the time
where the time goes in v8:
time: 103 us
  waiting for transfers between devices  48.3 us (47%)
  starting transfers between devices  28.1 us (27%)
  matrix products  21.1 us (20%)
  Pallas kernels  2.29 us (2%)
  other arithmetic  1.78 us (2%)
  between operations  1.17 us (1%)
    ppermute x17, waiting for transfers between devices, from_behind(): lax.ppermute(array, axis, [(i, (i + by) % peers) for i in range(peers)])  34.3 us
    ppermute x17, starting transfers between devices, from_behind(): lax.ppermute(array, axis, [(i, (i + by) % peers) for i in range(peers)])  25.7 us
    dot_general x52, matrix products, dot(): lax.dot_general(lhs, rhs, (dims, ((), ())), precision=lax.Precision.HIGH,...  21.1 us
    ppermute x1, waiting for transfers between devices, home(): array = lax.ppermute(array, 'users', across)  8.31 us
    ppermute x2, waiting for transfers between devices, combine(): partner = lax.ppermute(summed, 'period', partners)  5.63 us
    ppermute x2, starting transfers between devices, combine(): partner = lax.ppermute(summed, 'period', partners)  2.33 us
    pallas_call x1, Pallas kernels, first_piece(): pl.pallas_call(first_kernel, out_shape=tuple(outs), in_specs=[pl.BlockSpe...  2.29 us
  transfers between devices with their start and end apart: 21, of which 10 were waited for; matrix products, arithmetic and copies ran while one was open for 21% of the time, Pallas kernels for 0%

profile of v8, /device:TPU:0, one launch (start us, length us, event | category | flops | bytes accessed | tf_op | source)
XLA Modules:
  0.0 102.7 jit_solution(9454830779234161394)
XLA Ops:
  0.6 2.3 %shard_map.59 = (f32[384,256]{1,0:T(8,128)S(1)}, f32[768,256]{1,0:T(8,128)S(1)}, f32[384,768]{1,0:T(8,128)S(1)}, bf16[384,768]{1,0:T(8,128)(2,1)S(1)}, f32[384,256]{1,0:T(8,128)S(1)}, /*index=5*/f32[256,256]{1,0:T(8,128)S(1)}) custom-call(f32[384,256]{1,0:T(8,128)} %c_in.1, f32[1,768,256]{2,1,0:T(8,128)} %v_in.1, f32[1,6,384,768]{3,2,1,0:T(8,128)} %r_in.1, ...), custom_call_target="tpu_custom_call" | custom-call | tf_op jit(solution)/shard_map/pallas_call | solution.py:99
  2.9 5.5 %collective-permute-start.2 = (f32[256,256]{1,0:T(8,128)S(1)}, f32[256,256]{1,0:T(8,128)S(1)}, u32[]{:S(2)}, u32[]{:S(2)}) collective-permute-start(f32[256,256]{1,0:T(8,128)S(1)} %get-tuple-element.13), channel_id=1, source_target_pairs={{0,30},{2,0},{4,2},{6,4},{8,6},{10,8},{12,10},{14,12},{16,14},{18,... | collective-permute-start | bytes 786440 | tf_op jit(solution)/shard_map/ppermute | solution.py:22
  8.8 0.5 fusion.35
  9.4 0.7 collective-permute-start
  10.5 0.5 fusion.36
  12.1 5.8 %collective-permute-done.1 = f32[256,256]{1,0:T(8,128)S(1)} collective-permute-done((f32[256,256]{1,0:T(8,128)S(1)}, f32[256,256]{1,0:T(8,128)S(1)}, u32[]{:S(2)}, u32[]{:S(2)}) %collective-permute-start.1) | collective-permute-done | bytes 262176 | tf_op jit(solution)/shard_map/ppermute | solution.py:22
  18.8 4.7 %collective-permute-start.4 = (f32[256,256]{1,0:T(8,128)S(1)}, f32[256,256]{1,0:T(8,128)S(1)}, u32[]{:S(2)}, u32[]{:S(2)}) collective-permute-start(f32[256,256]{1,0:T(8,128)S(1)} %fusion.38), channel_id=1, source_target_pairs={{0,30},{2,0},{4,2},{6,4},{8,6},{10,8},{12,10},{14,12},{16,14},{18,... | collective-permute-start | bytes 786440 | tf_op jit(solution)/shard_map/ppermute | solution.py:22
  26.5 6.6 %collective-permute-done.5 = f32[256,256]{1,0:T(8,128)S(1)} collective-permute-done((f32[256,256]{1,0:T(8,128)S(1)}, f32[256,256]{1,0:T(8,128)S(1)}, u32[]{:S(2)}, u32[]{:S(2)}) %collective-permute-start.5) | collective-permute-done | bytes 262176 | tf_op jit(solution)/shard_map/ppermute | solution.py:22
  33.7 0.5 fusion.42
  34.3 4.7 %collective-permute-start.9 = (f32[256,256]{1,0:T(8,128)S(1)}, f32[256,256]{1,0:T(8,128)S(1)}, u32[]{:S(2)}, u32[]{:S(2)}) collective-permute-start(f32[256,256]{1,0:T(8,128)S(1)} %fusion.42), channel_id=1, source_target_pairs={{0,30},{2,0},{4,2},{6,4},{8,6},{10,8},{12,10},{14,12},{16,14},{18,... | collective-permute-start | bytes 786440 | tf_op jit(solution)/shard_map/ppermute | solution.py:22
  40.4 1.6 %collective-permute-start.6 = (f32[384,256]{1,0:T(8,128)S(1)}, f32[384,256]{1,0:T(8,128)S(1)}, u32[]{:S(2)}, u32[]{:S(2)}) collective-permute-start(f32[384,256]{1,0:T(8,128)S(1)} %fusion.12), channel_id=1, source_target_pairs={{0,1},{1,0},{2,3},{3,2},{4,5},{5,4},{6,7},{7,6},{8,9},{9,8},{10,11... | collective-permute-start | bytes 1179656 | tf_op jit(solution)/shard_map/ppermute | solution.py:117
  42.0 0.5 fusion.41
  42.6 0.5 fusion.40
  43.1 5.1 %collective-permute-done.6 = f32[384,256]{1,0:T(8,128)S(1)} collective-permute-done((f32[384,256]{1,0:T(8,128)S(1)}, f32[384,256]{1,0:T(8,128)S(1)}, u32[]{:S(2)}, u32[]{:S(2)}) %collective-permute-start.6) | collective-permute-done | bytes 393248 | tf_op jit(solution)/shard_map/ppermute | solution.py:117
  49.0 0.5 fusion.45
  50.7 4.1 %collective-permute-start.10 = (f32[256,256]{1,0:T(8,128)S(1)}, f32[256,256]{1,0:T(8,128)S(1)}, u32[]{:S(2)}, u32[]{:S(2)}) collective-permute-start(f32[256,256]{1,0:T(8,128)S(1)} %fusion.43), channel_id=1, source_target_pairs={{0,30},{2,0},{4,2},{6,4},{8,6},{10,8},{12,10},{14,12},{16,14},{18,... | collective-permute-start | bytes 786440 | tf_op jit(solution)/shard_map/ppermute | solution.py:22
  55.5 0.5 fusion.44
  56.5 2.2 %collective-permute-done.10 = f32[256,256]{1,0:T(8,128)S(1)} collective-permute-done((f32[256,256]{1,0:T(8,128)S(1)}, f32[256,256]{1,0:T(8,128)S(1)}, u32[]{:S(2)}, u32[]{:S(2)}) %collective-permute-start.10) | collective-permute-done | bytes 262176 | tf_op jit(solution)/shard_map/ppermute | solution.py:22
  59.6 4.7 %collective-permute-start.13 = (f32[256,256]{1,0:T(8,128)S(1)}, f32[256,256]{1,0:T(8,128)S(1)}, u32[]{:S(2)}, u32[]{:S(2)}) collective-permute-start(f32[256,256]{1,0:T(8,128)S(1)} %fusion.46), channel_id=1, source_target_pairs={{0,30},{2,0},{4,2},{6,4},{8,6},{10,8},{12,10},{14,12},{16,14},{18,... | collective-permute-start | bytes 786440 | tf_op jit(solution)/shard_map/ppermute | solution.py:22
  65.0 0.5 fusion.48
  66.6 0.5 fusion.47
  67.2 0.6 collective-permute-start.14
  67.7 3.2 %collective-permute-done.15 = f32[256,256]{1,0:T(8,128)S(1)} collective-permute-done((f32[256,256]{1,0:T(8,128)S(1)}, f32[256,256]{1,0:T(8,128)S(1)}, u32[]{:S(2)}, u32[]{:S(2)}) %collective-permute-start.15) | collective-permute-done | bytes 262176 | tf_op jit(solution)/shard_map/ppermute | solution.py:22
  71.7 2.1 %collective-permute-done.14 = f32[256,256]{1,0:T(8,128)S(1)} collective-permute-done((f32[256,256]{1,0:T(8,128)S(1)}, f32[256,256]{1,0:T(8,128)S(1)}, u32[]{:S(2)}, u32[]{:S(2)}) %collective-permute-start.14) | collective-permute-done | bytes 262176 | tf_op jit(solution)/shard_map/ppermute | solution.py:22
  74.5 0.5 fusion.49
  75.9 0.8 collective-permute-start.16
  77.8 8.3 %collective-permute-done.17 = f32[256,256]{1,0:T(8,128)S(1)} collective-permute-done((f32[256,256]{1,0:T(8,128)S(1)}, f32[256,256]{1,0:T(8,128)S(1)}, u32[]{:S(2)}, u32[]{:S(2)}) %collective-permute-start.17) | collective-permute-done | bytes 262176 | tf_op jit(solution)/shard_map/ppermute | solution.py:32
  86.1 0.6 collective-permute-done.16
  86.6 0.8 add_multiply_fusion
  87.4 11.5 %collective-permute-done.19 = f32[256,256]{1,0:T(8,128)S(1)} collective-permute-done((f32[256,256]{1,0:T(8,128)S(1)}, f32[256,256]{1,0:T(8,128)S(1)}, u32[]{:S(2)}, u32[]{:S(2)}) %collective-permute-start.19) | collective-permute-done | bytes 262176 | tf_op jit(solution)/shard_map/ppermute | solution.py:22
  99.0 2.8 %collective-permute-done.20 = f32[256,256]{1,0:T(8,128)S(1)} collective-permute-done((f32[256,256]{1,0:T(8,128)S(1)}, f32[256,256]{1,0:T(8,128)S(1)}, u32[]{:S(2)}, u32[]{:S(2)}) %collective-permute-start.20) | collective-permute-done | bytes 262176 | tf_op jit(solution)/shard_map/ppermute | solution.py:22
  101.8 0.9 maximum_bitcast_fusion
  (70 shorter events, 16.9 us)
Async XLA Ops:
  0.6 17.3 %copy-start.1 = (bf16[1,6,384,768]{3,2,1,0:T(8,128)(2,1)S(1)}, bf16[1,6,384,768]{3,2,1,0:T(8,128)(2,1)}, u32[]{:S(2)}) copy-start(bf16[1,6,384,768]{3,2,1,0:T(8,128)(2,1)} %w_in.1) | copy-start | bytes 10616836
  2.9 21.5 %collective-permute-start.2 = (f32[256,256]{1,0:T(8,128)S(1)}, f32[256,256]{1,0:T(8,128)S(1)}, u32[]{:S(2)}, u32[]{:S(2)}) collective-permute-start(f32[256,256]{1,0:T(8,128)S(1)} %get-tuple-element.13), channel_id=1, source_target_pairs={{0,30},{2,0},{4,2},{6,4},{8,6},{10,8},{12,10},{14,12},{16,14},{18,... | collective-permute-start | bytes 786440 | tf_op jit(solution)/shard_map/ppermute | solution.py:22
  9.3 8.6 %copy-start = (f32[1,6,384,768]{3,2,1,0:T(8,128)S(1)}, f32[1,6,384,768]{3,2,1,0:T(8,128)}, u32[]{:S(2)}) copy-start(f32[1,6,384,768]{3,2,1,0:T(8,128)} %r_in.1) | copy-start | bytes 21233668
  9.4 14.1 %collective-permute-start = (f32[256,256]{1,0:T(8,128)S(1)}, f32[256,256]{1,0:T(8,128)S(1)}, u32[]{:S(2)}, u32[]{:S(2)}) collective-permute-start(f32[256,256]{1,0:T(8,128)S(1)} %fusion.35), channel_id=1, source_target_pairs={{0,30},{2,0},{4,2},{6,4},{8,6},{10,8},{12,10},{14,12},{16,14},{18,... | collective-permute-start | bytes 786440 | tf_op jit(solution)/shard_map/ppermute | solution.py:22
  11.0 6.9 %collective-permute-start.1 = (f32[256,256]{1,0:T(8,128)S(1)}, f32[256,256]{1,0:T(8,128)S(1)}, u32[]{:S(2)}, u32[]{:S(2)}) collective-permute-start(f32[256,256]{1,0:T(8,128)S(1)} %fusion.36), channel_id=1, source_target_pairs={{0,30},{2,0},{4,2},{6,4},{8,6},{10,8},{12,10},{14,12},{16,14},{18,... | collective-permute-start | bytes 786440 | tf_op jit(solution)/shard_map/ppermute | solution.py:22
  18.8 20.1 %collective-permute-start.4 = (f32[256,256]{1,0:T(8,128)S(1)}, f32[256,256]{1,0:T(8,128)S(1)}, u32[]{:S(2)}, u32[]{:S(2)}) collective-permute-start(f32[256,256]{1,0:T(8,128)S(1)} %fusion.38), channel_id=1, source_target_pairs={{0,30},{2,0},{4,2},{6,4},{8,6},{10,8},{12,10},{14,12},{16,14},{18,... | collective-permute-start | bytes 786440 | tf_op jit(solution)/shard_map/ppermute | solution.py:22
  24.4 15.2 %collective-permute-start.3 = (f32[256,256]{1,0:T(8,128)S(1)}, f32[256,256]{1,0:T(8,128)S(1)}, u32[]{:S(2)}, u32[]{:S(2)}) collective-permute-start(f32[256,256]{1,0:T(8,128)S(1)} %fusion.37), channel_id=1, source_target_pairs={{0,30},{2,0},{4,2},{6,4},{8,6},{10,8},{12,10},{14,12},{16,14},{18,... | collective-permute-start | bytes 786440 | tf_op jit(solution)/shard_map/ppermute | solution.py:22
  25.7 7.3 %collective-permute-start.5 = (f32[256,256]{1,0:T(8,128)S(1)}, f32[256,256]{1,0:T(8,128)S(1)}, u32[]{:S(2)}, u32[]{:S(2)}) collective-permute-start(f32[256,256]{1,0:T(8,128)S(1)} %fusion.39), channel_id=1, source_target_pairs={{0,30},{2,0},{4,2},{6,4},{8,6},{10,8},{12,10},{14,12},{16,14},{18,... | collective-permute-start | bytes 786440 | tf_op jit(solution)/shard_map/ppermute | solution.py:22
  34.3 14.0 %collective-permute-start.9 = (f32[256,256]{1,0:T(8,128)S(1)}, f32[256,256]{1,0:T(8,128)S(1)}, u32[]{:S(2)}, u32[]{:S(2)}) collective-permute-start(f32[256,256]{1,0:T(8,128)S(1)} %fusion.42), channel_id=1, source_target_pairs={{0,30},{2,0},{4,2},{6,4},{8,6},{10,8},{12,10},{14,12},{16,14},{18,... | collective-permute-start | bytes 786440 | tf_op jit(solution)/shard_map/ppermute | solution.py:22
  40.4 7.8 %collective-permute-start.6 = (f32[384,256]{1,0:T(8,128)S(1)}, f32[384,256]{1,0:T(8,128)S(1)}, u32[]{:S(2)}, u32[]{:S(2)}) collective-permute-start(f32[384,256]{1,0:T(8,128)S(1)} %fusion.12), channel_id=1, source_target_pairs={{0,1},{1,0},{2,3},{3,2},{4,5},{5,4},{6,7},{7,6},{8,9},{9,8},{10,11... | collective-permute-start | bytes 1179656 | tf_op jit(solution)/shard_map/ppermute | solution.py:117
  42.5 12.3 %collective-permute-start.8 = (f32[256,256]{1,0:T(8,128)S(1)}, f32[256,256]{1,0:T(8,128)S(1)}, u32[]{:S(2)}, u32[]{:S(2)}) collective-permute-start(f32[256,256]{1,0:T(8,128)S(1)} %fusion.41), channel_id=1, source_target_pairs={{0,30},{2,0},{4,2},{6,4},{8,6},{10,8},{12,10},{14,12},{16,14},{18,... | collective-permute-start | bytes 786440 | tf_op jit(solution)/shard_map/ppermute | solution.py:22
  43.1 6.7 %collective-permute-start.7 = (f32[256,256]{1,0:T(8,128)S(1)}, f32[256,256]{1,0:T(8,128)S(1)}, u32[]{:S(2)}, u32[]{:S(2)}) collective-permute-start(f32[256,256]{1,0:T(8,128)S(1)} %fusion.40), channel_id=1, source_target_pairs={{0,30},{2,0},{4,2},{6,4},{8,6},{10,8},{12,10},{14,12},{16,14},{18,... | collective-permute-start | bytes 786440 | tf_op jit(solution)/shard_map/ppermute | solution.py:22
  49.5 14.7 %collective-permute-start.12 = (f32[256,256]{1,0:T(8,128)S(1)}, f32[256,256]{1,0:T(8,128)S(1)}, u32[]{:S(2)}, u32[]{:S(2)}) collective-permute-start(f32[256,256]{1,0:T(8,128)S(1)} %fusion.45), channel_id=1, source_target_pairs={{0,30},{2,0},{4,2},{6,4},{8,6},{10,8},{12,10},{14,12},{16,14},{18,... | collective-permute-start | bytes 786440 | tf_op jit(solution)/shard_map/ppermute | solution.py:22
  50.7 8.0 %collective-permute-start.10 = (f32[256,256]{1,0:T(8,128)S(1)}, f32[256,256]{1,0:T(8,128)S(1)}, u32[]{:S(2)}, u32[]{:S(2)}) collective-permute-start(f32[256,256]{1,0:T(8,128)S(1)} %fusion.43), channel_id=1, source_target_pairs={{0,30},{2,0},{4,2},{6,4},{8,6},{10,8},{12,10},{14,12},{16,14},{18,... | collective-permute-start | bytes 786440 | tf_op jit(solution)/shard_map/ppermute | solution.py:22
  56.1 9.5 %collective-permute-start.11 = (f32[256,256]{1,0:T(8,128)S(1)}, f32[256,256]{1,0:T(8,128)S(1)}, u32[]{:S(2)}, u32[]{:S(2)}) collective-permute-start(f32[256,256]{1,0:T(8,128)S(1)} %fusion.44), channel_id=1, source_target_pairs={{0,30},{2,0},{4,2},{6,4},{8,6},{10,8},{12,10},{14,12},{16,14},{18,... | collective-permute-start | bytes 786440 | tf_op jit(solution)/shard_map/ppermute | solution.py:22
  59.6 15.5 %collective-permute-start.13 = (f32[256,256]{1,0:T(8,128)S(1)}, f32[256,256]{1,0:T(8,128)S(1)}, u32[]{:S(2)}, u32[]{:S(2)}) collective-permute-start(f32[256,256]{1,0:T(8,128)S(1)} %fusion.46), channel_id=1, source_target_pairs={{0,30},{2,0},{4,2},{6,4},{8,6},{10,8},{12,10},{14,12},{16,14},{18,... | collective-permute-start | bytes 786440 | tf_op jit(solution)/shard_map/ppermute | solution.py:22
  65.5 5.5 %collective-permute-start.15 = (f32[256,256]{1,0:T(8,128)S(1)}, f32[256,256]{1,0:T(8,128)S(1)}, u32[]{:S(2)}, u32[]{:S(2)}) collective-permute-start(f32[256,256]{1,0:T(8,128)S(1)} %fusion.48), channel_id=1, source_target_pairs={{0,30},{2,0},{4,2},{6,4},{8,6},{10,8},{12,10},{14,12},{16,14},{18,... | collective-permute-start | bytes 786440 | tf_op jit(solution)/shard_map/ppermute | solution.py:22
  67.2 6.6 %collective-permute-start.14 = (f32[256,256]{1,0:T(8,128)S(1)}, f32[256,256]{1,0:T(8,128)S(1)}, u32[]{:S(2)}, u32[]{:S(2)}) collective-permute-start(f32[256,256]{1,0:T(8,128)S(1)} %fusion.47), channel_id=1, source_target_pairs={{0,30},{2,0},{4,2},{6,4},{8,6},{10,8},{12,10},{14,12},{16,14},{18,... | collective-permute-start | bytes 786440 | tf_op jit(solution)/shard_map/ppermute | solution.py:22
  75.0 11.0 %collective-permute-start.17 = (f32[256,256]{1,0:T(8,128)S(1)}, f32[256,256]{1,0:T(8,128)S(1)}, u32[]{:S(2)}, u32[]{:S(2)}) collective-permute-start(f32[256,256]{1,0:T(8,128)S(1)} %fusion.49), channel_id=1, source_target_pairs={{0,8},{2,10},{4,12},{6,22},{8,16},{10,18},{12,20},{14,30},{16,24},... | collective-permute-start | bytes 786440 | tf_op jit(solution)/shard_map/ppermute | solution.py:32
  75.9 10.8 %collective-permute-start.16 = (f32[384,256]{1,0:T(8,128)S(1)}, f32[384,256]{1,0:T(8,128)S(1)}, u32[]{:S(2)}, u32[]{:S(2)}) collective-permute-start(f32[384,256]{1,0:T(8,128)S(1)} %fusion.30), channel_id=1, source_target_pairs={{0,1},{1,0},{2,3},{3,2},{4,5},{5,4},{6,7},{7,6},{8,9},{9,8},{10,11... | collective-permute-start | bytes 1179656 | tf_op jit(solution)/shard_map/ppermute | solution.py:117
  77.1 21.9 %collective-permute-start.19 = (f32[256,256]{1,0:T(8,128)S(1)}, f32[256,256]{1,0:T(8,128)S(1)}, u32[]{:S(2)}, u32[]{:S(2)}) collective-permute-start(f32[256,256]{1,0:T(8,128)S(1)} %fusion.50), channel_id=1, source_target_pairs={{0,10},{2,12},{4,14},{6,16},{8,18},{10,20},{12,22},{14,24},{16,26}... | collective-permute-start | bytes 786440 | tf_op jit(solution)/shard_map/ppermute | solution.py:22
  77.7 24.1 %collective-permute-start.20 = (f32[256,256]{1,0:T(8,128)S(1)}, f32[256,256]{1,0:T(8,128)S(1)}, u32[]{:S(2)}, u32[]{:S(2)}) collective-permute-start(f32[256,256]{1,0:T(8,128)S(1)} %fusion.51), channel_id=1, source_target_pairs={{0,10},{2,12},{4,14},{6,16},{8,18},{10,20},{12,22},{14,24},{16,26}... | collective-permute-start | bytes 786440 | tf_op jit(solution)/shard_map/ppermute | solution.py:22
  86.1 15.7 %collective-permute-start.18 = (f32[256,256]{1,0:T(8,128)S(1)}, f32[256,256]{1,0:T(8,128)S(1)}, u32[]{:S(2)}, u32[]{:S(2)}) collective-permute-start(f32[256,256]{1,0:T(8,128)S(1)} %collective-permute-done.17), channel_id=1, source_target_pairs={{8,10},{10,12},{12,14},{22,16},{16,18},{18,20},{20,22},{30,24},{24... | collective-permute-start | bytes 786440 | tf_op jit(solution)/shard_map/ppermute | solution.py:33
